TPU v7x, 32 devices: a whole 2x2x4 slice. The times are simulated.
32 devices in a mesh: clip: 2 (over x), seq: 16 (over z, y, core).
Axes of the slice: x: 2, y: 2, z: 4, core: 2. Of those that a mesh axis runs over, the one named last changes fastest.
Arguments:
- tokens: bfloat16 [4, 2048, 1536], P('clip', 'seq'), may hold values from -6 to 6
- condition: float32 [4, 1024], replicated, may hold values from -6 to 6
- caption: bfloat16 [4, 256, 4096], P('clip', 'seq'), may hold values from -6 to 6
- caption_lengths: int32 [4], P('clip'), may hold values from 64 to 256
- positions: int32 [3, 4, 2048], P(None, 'clip', 'seq'), may hold values from 0 to 63
- modulation_weight: bfloat16 [1024, 9216], P(('clip', 'seq')), may hold values from -0.1875 to 0.1875
- modulation_bias: float32 [9216], replicated, may hold values from -3 to 3
- norm_gains: float32 [5, 1536], replicated, may hold values from 0.1 to 1.9
- cross_gate: float32 [24], replicated, may hold values from -0.5 to 0.5
- input_weight: bfloat16 [1536, 4608], P(('clip', 'seq')), may hold values from -0.15625 to 0.15625
- output_weight: bfloat16 [1536, 1536], P(('clip', 'seq')), may hold values from -4 to 4
- caption_key_weight: bfloat16 [4096, 1536], P(('clip', 'seq')), may hold values from -0.09375 to 0.09375
- caption_value_weight: bfloat16 [4096, 1536], P(('clip', 'seq')), may hold values from -0.09375 to 0.09375
- gate_weight: bfloat16 [1536, 4096], P(('clip', 'seq')), may hold values from -0.15625 to 0.15625
- up_weight: bfloat16 [1536, 4096], P(('clip', 'seq')), may hold values from -0.15625 to 0.15625
- down_weight: bfloat16 [4096, 1536], P(('clip', 'seq')), may hold values from -0.09375 to 0.09375
- cotangent: bfloat16 [4, 2048, 1536], P('clip', 'seq'), may hold values from -6 to 6
Outputs:
- output: bfloat16 [4, 2048, 1536], P('clip', 'seq')
- d_tokens: float32 [4, 2048, 1536], P('clip', 'seq')
- d_caption: float32 [4, 256, 4096], P('clip', 'seq')
- d_condition: float32 [4, 1024], replicated
- d_modulation_weight: float32 [1024, 9216], P(('clip', 'seq'))
- d_modulation_bias: float32 [9216], replicated
- d_norm_gains: float32 [5, 1536], replicated
- d_cross_gate: float32 [24], replicated
- d_input_weight: float32 [1536, 4608], P(('clip', 'seq'))
- d_output_weight: float32 [1536, 1536], P(('clip', 'seq'))
- d_caption_key_weight: float32 [4096, 1536], P(('clip', 'seq'))
- d_caption_value_weight: float32 [4096, 1536], P(('clip', 'seq'))
- d_gate_weight: float32 [1536, 4096], P(('clip', 'seq'))
- d_up_weight: float32 [1536, 4096], P(('clip', 'seq'))
- d_down_weight: float32 [4096, 1536], P(('clip', 'seq'))
Inputs may be any that keep to these rules, and one draw needn't show every extreme that they name: `caption_lengths`: caption slots at or after a clip's length are padding.
All inputs are finite; a program needn't handle non-finite values.
Results may differ from a plain program's by a relative error of at most 0.023.
Values may be sent and summed in bfloat16 or wider, within the bound.
No kernel may reach another device: no remote copies, remote signals or barrier semaphores. Data moves between devices by JAX's collectives and lax.ppermute only.
A program may use at most 640 MiB of HBM per device.

v0:
```python
import jax
import jax.numpy as jnp
from jax import lax
from jax.sharding import PartitionSpec as P

EPSILON = 1e-06
NEGATIVE = -1e30


def shifted(block, axis, distance):
    devices = range(lax.axis_size(axis))
    route = [((i - distance) % len(devices), i) for i in devices]
    return lax.ppermute(block, axis, route)


def rms_apply(values, scaling):
    return values * lax.rsqrt(jnp.mean(values * values, axis=-1, keepdims=True) + EPSILON) * scaling


def rope_tables(places, head_dim):
    pair_count = head_dim // 2
    lead_pairs = pair_count // 4
    mid_pairs = (pair_count - lead_pairs) // 2
    pair_index = jnp.arange(pair_count, dtype=jnp.int32)
    axis_pick = (pair_index >= lead_pairs).astype(jnp.int32) + (
        pair_index >= lead_pairs + mid_pairs
    ).astype(jnp.int32)
    anchor = jnp.where(
        axis_pick == 0, 0, jnp.where(axis_pick == 1, lead_pairs, lead_pairs + mid_pairs)
    )
    extent = jnp.where(
        axis_pick == 0,
        lead_pairs,
        jnp.where(axis_pick == 1, mid_pairs, pair_count - lead_pairs - mid_pairs),
    )
    frequency = jnp.power(
        10000.0, -(pair_index - anchor).astype(jnp.float32) / extent.astype(jnp.float32)
    )
    chosen = jnp.where(
        axis_pick == 0,
        places[0][..., None],
        jnp.where(axis_pick == 1, places[1][..., None], places[2][..., None]),
    )
    angles = chosen.astype(jnp.float32) * frequency
    return (jnp.cos(angles), jnp.sin(angles))


def rope_apply(vectors, cosine, sine_part):
    half_width = vectors.shape[-1] // 2
    front_half = vectors[..., :half_width]
    back_half = vectors[..., half_width:]
    cosine = cosine[..., None, :]
    sine_part = sine_part[..., None, :]
    return jnp.concatenate(
        [front_half * cosine - back_half * sine_part, front_half * sine_part + back_half * cosine],
        axis=-1,
    )


def project_heads(query_raw, key_raw, query_gain, key_gain, cosine, sine_part, head_count):
    shape = query_raw.shape[:-1] + (head_count, query_raw.shape[-1] // head_count)
    queries = rope_apply(rms_apply(query_raw, query_gain).reshape(shape), cosine, sine_part)
    keys = rope_apply(rms_apply(key_raw, key_gain).reshape(shape), cosine, sine_part)
    return (queries, keys)


def self_grads(query_blk, grad_blk, log_blk, delta_blk, key_blk, value_blk, score_scale):
    scores = (
        jnp.einsum("cthd,cshd->cths", query_blk, key_blk, preferred_element_type=jnp.float32)
        * score_scale
    )
    probs = jnp.exp(scores - log_blk[..., None])
    d_probs = jnp.einsum("cthd,cshd->cths", grad_blk, value_blk, preferred_element_type=jnp.float32)
    dscore = (probs * (d_probs - delta_blk[..., None])).astype(jnp.bfloat16)
    grad_query = (
        jnp.einsum("cths,cshd->cthd", dscore, key_blk, preferred_element_type=jnp.float32)
        * score_scale
    )
    grad_key = (
        jnp.einsum("cths,cthd->cshd", dscore, query_blk, preferred_element_type=jnp.float32)
        * score_scale
    )
    grad_value = jnp.einsum(
        "cths,cthd->cshd", probs.astype(jnp.bfloat16), grad_blk, preferred_element_type=jnp.float32
    )
    return (grad_query, grad_key, grad_value)


def on_device(
    tokens,
    condition,
    caption,
    caption_lengths,
    positions,
    modulation_weight,
    modulation_bias,
    norm_gains,
    cross_gate,
    input_weight,
    output_weight,
    caption_key_weight,
    caption_value_weight,
    gate_weight,
    up_weight,
    down_weight,
    cotangent,
):
    clips_here, rows_here, width = tokens.shape
    head_count = cross_gate.shape[0]
    head_dim = width // head_count
    score_scale = head_dim ** (-0.5)
    seq_count = lax.axis_size("seq")
    clip_start = lax.axis_index("clip") * clips_here
    head_shape = (clips_here, rows_here, head_count, head_dim)
    full_mod, full_input, full_output, full_ckey, full_cvalue, full_gate, full_up, full_down = (
        lax.all_gather(modulation_weight, ("clip", "seq"), axis=0, tiled=True),
        lax.all_gather(input_weight, ("clip", "seq"), axis=0, tiled=True),
        lax.all_gather(output_weight, ("clip", "seq"), axis=0, tiled=True),
        lax.all_gather(caption_key_weight, ("clip", "seq"), axis=0, tiled=True),
        lax.all_gather(caption_value_weight, ("clip", "seq"), axis=0, tiled=True),
        lax.all_gather(gate_weight, ("clip", "seq"), axis=0, tiled=True),
        lax.all_gather(up_weight, ("clip", "seq"), axis=0, tiled=True),
        lax.all_gather(down_weight, ("clip", "seq"), axis=0, tiled=True),
    )
    silu_all = jax.nn.silu(condition).astype(jnp.bfloat16)
    silu_own = lax.dynamic_slice_in_dim(silu_all, clip_start, clips_here, 0)
    modulation = jnp.dot(silu_own, full_mod, preferred_element_type=jnp.float32) + modulation_bias
    modulation = modulation[:, None, :]
    shift_attn = modulation[..., 0 * width : 1 * width]
    scale_attn = modulation[..., 1 * width : 2 * width]
    gate_attn = modulation[..., 2 * width : 3 * width]
    shift_ffn = modulation[..., 3 * width : 4 * width]
    scale_ffn = modulation[..., 4 * width : 5 * width]
    gate_ffn = modulation[..., 5 * width : 6 * width]
    token_vals = tokens.astype(jnp.float32)
    normed_attn = rms_apply(token_vals, norm_gains[0])
    attn_input = (normed_attn * (1.0 + scale_attn) + shift_attn).astype(jnp.bfloat16)
    projected = jnp.einsum(
        "ctd,de->cte", attn_input, full_input, preferred_element_type=jnp.float32
    )
    raw_query = projected[..., :width]
    raw_key = projected[..., width : 2 * width]
    cosine, sine_part = rope_tables(positions, head_dim)

    def head_project(query_raw, key_raw, query_gain, key_gain):
        return project_heads(
            query_raw, key_raw, query_gain, key_gain, cosine, sine_part, head_count
        )

    query_f, key_f = head_project(raw_query, raw_key, norm_gains[1], norm_gains[2])
    queries = query_f.astype(jnp.bfloat16)
    keys_local = key_f.astype(jnp.bfloat16)
    values_local = projected[..., 2 * width :].reshape(head_shape).astype(jnp.bfloat16)
    caption_raw = jnp.einsum("crx,xd->crd", caption, full_ckey, preferred_element_type=jnp.float32)
    caption_keys = rms_apply(caption_raw, norm_gains[3]).astype(jnp.bfloat16)
    caption_values = jnp.einsum(
        "crx,xd->crd", caption, full_cvalue, preferred_element_type=jnp.float32
    ).astype(jnp.bfloat16)
    all_ckeys, all_cvalues = (
        lax.all_gather(caption_keys, "seq", axis=1, tiled=True),
        lax.all_gather(caption_values, "seq", axis=1, tiled=True),
    )
    cap_total = all_ckeys.shape[1]
    ckey_heads = all_ckeys.reshape(clips_here, cap_total, head_count, head_dim)
    cvalue_heads = all_cvalues.reshape(clips_here, cap_total, head_count, head_dim)
    stat_shape = (clips_here, rows_here, head_count)
    row_peak = jnp.full(stat_shape, NEGATIVE, jnp.float32)
    block_keys = lax.all_gather(keys_local, "seq", axis=1, tiled=True)
    block_values = lax.all_gather(values_local, "seq", axis=1, tiled=True)
    scores = (
        jnp.einsum("cthd,cshd->cths", queries, block_keys, preferred_element_type=jnp.float32)
        * score_scale
    )
    new_peak = jnp.maximum(row_peak, jnp.max(scores, axis=-1))
    weights = jnp.exp(scores - new_peak[..., None])
    row_total = jnp.sum(weights, axis=-1)
    weighted = jnp.einsum(
        "cths,cshd->cthd",
        weights.astype(jnp.bfloat16),
        block_values,
        preferred_element_type=jnp.float32,
    )
    row_peak, row_total, weighted = (new_peak, row_total, weighted)
    o_self = weighted / row_total[..., None]
    log_total = row_peak + jnp.log(row_total)
    key_valid = jnp.arange(cap_total, dtype=jnp.int32)[None, :] < caption_lengths[:, None]
    cross_scores = (
        jnp.einsum("cthd,cshd->cths", queries, ckey_heads, preferred_element_type=jnp.float32)
        * score_scale
    )
    cross_scores = jnp.where(key_valid[:, None, None, :], cross_scores, NEGATIVE)
    cross_log = jax.nn.logsumexp(cross_scores, axis=-1, keepdims=True)
    cross_probs = jnp.exp(cross_scores - cross_log)
    cross_low = cross_probs.astype(jnp.bfloat16)
    o_cross = jnp.einsum(
        "cths,cshd->cthd", cross_low, cvalue_heads, preferred_element_type=jnp.float32
    )
    tanh_gate = jnp.tanh(cross_gate)[:, None]
    combined = (
        (o_self + tanh_gate * o_cross).reshape(clips_here, rows_here, width).astype(jnp.bfloat16)
    )
    branch = jnp.einsum("ctd,de->cte", combined, full_output, preferred_element_type=jnp.float32)
    middle = token_vals + gate_attn * branch
    normed_ffn = rms_apply(middle, norm_gains[4])
    ffn_input = (normed_ffn * (1.0 + scale_ffn) + shift_ffn).astype(jnp.bfloat16)
    gate_vals = jnp.einsum("ctd,df->ctf", ffn_input, full_gate, preferred_element_type=jnp.float32)
    up_vals = jnp.einsum("ctd,df->ctf", ffn_input, full_up, preferred_element_type=jnp.float32)
    hidden = (jax.nn.silu(gate_vals) * up_vals).astype(jnp.bfloat16)
    ffn_out = jnp.einsum("ctf,fd->ctd", hidden, full_down, preferred_element_type=jnp.float32)
    result = (middle + gate_ffn * ffn_out).astype(jnp.bfloat16)
    back_gate, back_up, back_down = (full_gate, full_up, full_down)
    grad_out = cotangent.astype(jnp.float32)
    d_ffn = (gate_ffn * grad_out).astype(jnp.bfloat16)
    d_gate_ffn = jnp.sum(grad_out * ffn_out, axis=1)
    d_hidden = jnp.einsum("ctd,fd->ctf", d_ffn, back_down, preferred_element_type=jnp.float32)
    grad_down = jnp.einsum("ctf,ctd->fd", hidden, d_ffn, preferred_element_type=jnp.float32)
    _, swiglu_back = jax.vjp(
        lambda gate_in, up_in: jax.nn.silu(gate_in) * up_in, gate_vals, up_vals
    )
    d_gate_raw, d_up_raw = swiglu_back(d_hidden)
    d_gate_low = d_gate_raw.astype(jnp.bfloat16)
    d_up_low = d_up_raw.astype(jnp.bfloat16)
    grad_gate = jnp.einsum("ctd,ctf->df", ffn_input, d_gate_low, preferred_element_type=jnp.float32)
    grad_up = jnp.einsum("ctd,ctf->df", ffn_input, d_up_low, preferred_element_type=jnp.float32)
    d_ffn_input = jnp.einsum(
        "ctf,df->ctd", d_gate_low, back_gate, preferred_element_type=jnp.float32
    ) + jnp.einsum("ctf,df->ctd", d_up_low, back_up, preferred_element_type=jnp.float32)
    sum_gate, sum_up, sum_down = (
        lax.psum_scatter(grad_gate, ("clip", "seq"), scatter_dimension=0, tiled=True),
        lax.psum_scatter(grad_up, ("clip", "seq"), scatter_dimension=0, tiled=True),
        lax.psum_scatter(grad_down, ("clip", "seq"), scatter_dimension=0, tiled=True),
    )
    d_scale_ffn = jnp.sum(d_ffn_input * normed_ffn, axis=1)
    d_shift_ffn = jnp.sum(d_ffn_input, axis=1)
    _, ffn_norm_back = jax.vjp(rms_apply, middle, norm_gains[4])
    d_middle_norm, d_gain_ffn = ffn_norm_back(d_ffn_input * (1.0 + scale_ffn))
    d_middle = grad_out + d_middle_norm
    back_mod, back_input, back_output, back_ckey, back_cvalue = (
        full_mod,
        full_input,
        full_output,
        full_ckey,
        full_cvalue,
    )
    d_branch = (gate_attn * d_middle).astype(jnp.bfloat16)
    d_gate_attn = jnp.sum(d_middle * branch, axis=1)
    d_combined = jnp.einsum(
        "cte,de->ctd", d_branch, back_output, preferred_element_type=jnp.float32
    ).reshape(head_shape)
    grad_output = jnp.einsum("ctd,cte->de", combined, d_branch, preferred_element_type=jnp.float32)
    d_self = d_combined.astype(jnp.bfloat16)
    d_cross = (d_combined * tanh_gate).astype(jnp.bfloat16)
    d_cross_gate = jnp.sum(d_combined * o_cross, axis=(0, 1, 3)) * (
        1.0 - tanh_gate[:, 0] * tanh_gate[:, 0]
    )
    cross_dp = jnp.einsum(
        "cthd,cshd->cths", d_cross, cvalue_heads, preferred_element_type=jnp.float32
    )
    cross_delta = jnp.sum(cross_probs * cross_dp, axis=-1, keepdims=True)
    cross_ds = (cross_probs * (cross_dp - cross_delta)).astype(jnp.bfloat16)
    dq_cross = (
        jnp.einsum("cths,cshd->cthd", cross_ds, ckey_heads, preferred_element_type=jnp.float32)
        * score_scale
    )
    d_ckeys = (
        jnp.einsum(
            "cths,cthd->cshd", cross_ds, queries, preferred_element_type=jnp.float32
        ).reshape(clips_here, cap_total, width)
        * score_scale
    )
    d_cvalues = jnp.einsum(
        "cths,cthd->cshd", cross_low, d_cross, preferred_element_type=jnp.float32
    ).reshape(clips_here, cap_total, width)
    own_dkeys, own_dvalues = (
        lax.psum_scatter(d_ckeys, "seq", scatter_dimension=1, tiled=True),
        lax.psum_scatter(d_cvalues, "seq", scatter_dimension=1, tiled=True),
    )
    delta_self = jnp.sum(d_self.astype(jnp.float32) * o_self, axis=-1)
    zero_heads = jnp.zeros(head_shape, jnp.float32)

    def key_turn(step_index, loop_state):
        query_acc, key_blk, value_blk, key_acc, value_acc = loop_state
        grad_query, grad_key, grad_value = self_grads(
            queries, d_self, log_total, delta_self, key_blk, value_blk, score_scale
        )
        key_blk, value_blk, key_acc, value_acc = (
            shifted(key_blk, "seq", 1),
            shifted(value_blk, "seq", 1),
            shifted((key_acc + grad_key).astype(jnp.bfloat16), "seq", 1).astype(jnp.float32),
            shifted((value_acc + grad_value).astype(jnp.bfloat16), "seq", 1).astype(jnp.float32),
        )
        return (query_acc + grad_query, key_blk, value_blk, key_acc, value_acc)

    finished = lax.fori_loop(
        0, seq_count, key_turn, (zero_heads, keys_local, values_local, zero_heads, zero_heads)
    )
    dq_self, dk_self, dv_self = (finished[0], finished[3], finished[4])
    _, heads_back = jax.vjp(head_project, raw_query, raw_key, norm_gains[1], norm_gains[2])
    d_raw_query, d_raw_key, d_gain_query, d_gain_key = heads_back((dq_self + dq_cross, dk_self))
    d_projected = jnp.concatenate(
        [d_raw_query, d_raw_key, dv_self.reshape(clips_here, rows_here, width)], axis=-1
    ).astype(jnp.bfloat16)
    grad_input = jnp.einsum(
        "ctd,cte->de", attn_input, d_projected, preferred_element_type=jnp.float32
    )
    d_attn_input = jnp.einsum(
        "cte,de->ctd", d_projected, back_input, preferred_element_type=jnp.float32
    )
    d_scale_attn = jnp.sum(d_attn_input * normed_attn, axis=1)
    d_shift_attn = jnp.sum(d_attn_input, axis=1)
    _, attn_norm_back = jax.vjp(rms_apply, token_vals, norm_gains[0])
    d_tokens_norm, d_gain_attn = attn_norm_back(d_attn_input * (1.0 + scale_attn))
    d_tokens = d_middle + d_tokens_norm
    _, caption_norm_back = jax.vjp(rms_apply, caption_raw, norm_gains[3])
    d_caption_raw, d_gain_caption = caption_norm_back(own_dkeys)
    d_craw_low = d_caption_raw.astype(jnp.bfloat16)
    d_cval_low = own_dvalues.astype(jnp.bfloat16)
    d_caption = jnp.einsum(
        "crd,xd->crx", d_craw_low, back_ckey, preferred_element_type=jnp.float32
    ) + jnp.einsum("crd,xd->crx", d_cval_low, back_cvalue, preferred_element_type=jnp.float32)
    grad_ckey = jnp.einsum("crx,crd->xd", caption, d_craw_low, preferred_element_type=jnp.float32)
    grad_cvalue = jnp.einsum("crx,crd->xd", caption, d_cval_low, preferred_element_type=jnp.float32)
    sum_input, sum_output, sum_ckey, sum_cvalue = (
        lax.psum_scatter(grad_input, ("clip", "seq"), scatter_dimension=0, tiled=True),
        lax.psum_scatter(grad_output, ("clip", "seq"), scatter_dimension=0, tiled=True),
        lax.psum_scatter(grad_ckey, ("clip", "seq"), scatter_dimension=0, tiled=True),
        lax.psum_scatter(grad_cvalue, ("clip", "seq"), scatter_dimension=0, tiled=True),
    )
    d_mod_own = jnp.concatenate(
        [d_shift_attn, d_scale_attn, d_gate_attn, d_shift_ffn, d_scale_ffn, d_gate_ffn], axis=-1
    )
    d_mod_full = lax.dynamic_update_slice_in_dim(
        jnp.zeros((condition.shape[0], 6 * width), jnp.float32), d_mod_own, clip_start, 0
    )
    gain_terms = jnp.stack([d_gain_attn, d_gain_query, d_gain_key, d_gain_caption, d_gain_ffn])
    d_mod_sum, gain_sum, gate_sum = lax.psum(
        (d_mod_full, gain_terms, d_cross_gate), ("clip", "seq")
    )
    d_mod_low = d_mod_sum.astype(jnp.bfloat16)
    d_bias = jnp.sum(d_mod_low.astype(jnp.float32), axis=0)
    d_silu = jnp.einsum("cm,km->ck", d_mod_low, back_mod, preferred_element_type=jnp.float32)
    _, silu_back = jax.vjp(jax.nn.silu, condition)
    d_condition = silu_back(d_silu)[0]
    shard_rows = modulation_weight.shape[0]
    silu_rows = lax.dynamic_slice_in_dim(
        silu_all, lax.axis_index(("clip", "seq")) * shard_rows, shard_rows, 1
    )
    grad_mod = jnp.einsum("cr,cm->rm", silu_rows, d_mod_low, preferred_element_type=jnp.float32)
    return (
        result,
        d_tokens,
        d_caption,
        d_condition,
        grad_mod,
        d_bias,
        gain_sum,
        gate_sum,
        sum_input,
        sum_output,
        sum_ckey,
        sum_cvalue,
        sum_gate,
        sum_up,
        sum_down,
    )


def solution(mesh):
    return jax.shard_map(
        on_device,
        mesh=mesh,
        in_specs=(
            P("clip", "seq", None),
            P(),
            P("clip", "seq", None),
            P("clip"),
            P(None, "clip", "seq"),
            P(("clip", "seq"), None),
            P(),
            P(),
            P(),
            P(("clip", "seq"), None),
            P(("clip", "seq"), None),
            P(("clip", "seq"), None),
            P(("clip", "seq"), None),
            P(("clip", "seq"), None),
            P(("clip", "seq"), None),
            P(("clip", "seq"), None),
            P("clip", "seq", None),
        ),
        out_specs=(
            P("clip", "seq", None),
            P("clip", "seq", None),
            P("clip", "seq", None),
            P(),
            P(("clip", "seq"), None),
            P(),
            P(),
            P(),
            P(("clip", "seq"), None),
            P(("clip", "seq"), None),
            P(("clip", "seq"), None),
            P(("clip", "seq"), None),
            P(("clip", "seq"), None),
            P(("clip", "seq"), None),
            P(("clip", "seq"), None),
        ),
        check_vma=False,
    )
```

profile of v0, /device:TPU:0, one launch (start us, length us, event | category | flops | bytes accessed | tf_op | source)
XLA Modules:
  0.0 3283.9 jit_solution(18055228339622507775)
XLA Ops:
  10.0 99.6 %all-gather.21.cloned.1.call-done = bf16[4096,1536]{1,0:T(8,128)(2,1)} async-done(((bf16[128,1536]{1,0:T(8,128)(2,1)}), bf16[4096,1536]{1,0:T(8,128)(2,1)}) %all-gather.21.cloned.1.call-update) | async-done | bytes 12582928 | tf_op jit(solution)/shard_map/all_gather | solution.py:120
  117.3 89.5 %all-gather.25.cloned.1.call-done = bf16[4096,1536]{1,0:T(8,128)(2,1)} async-done(((bf16[128,1536]{1,0:T(8,128)(2,1)}), bf16[4096,1536]{1,0:T(8,128)(2,1)}) %all-gather.25.cloned.1.call-update) | async-done | bytes 12582928 | tf_op jit(solution)/shard_map/all_gather | solution.py:119
  216.7 115.9 %all-gather.13.cloned.1.call-done = bf16[1024,9216]{1,0:T(8,128)(2,1)} async-done(((bf16[32,9216]{1,0:T(8,128)(2,1)}), bf16[1024,9216]{1,0:T(8,128)(2,1)}) %all-gather.13.cloned.1.call-update) | async-done | bytes 18874384 | tf_op jit(solution)/shard_map/all_gather | solution.py:116
  341.6 95.2 %all-gather.15.cloned.1.call-done = bf16[1536,4608]{1,0:T(8,128)(2,1)} async-done(((bf16[48,4608]{1,0:T(8,128)(2,1)}), bf16[1536,4608]{1,0:T(8,128)(2,1)}) %all-gather.15.cloned.1.call-update) | async-done | bytes 14155792 | tf_op jit(solution)/shard_map/all_gather | solution.py:117
  479.9 38.8 %all-gather.27.cloned.1.call-done = bf16[2,256,1536]{2,1,0:T(8,128)(2,1)} async-done(((bf16[2,16,1536]{2,1,0:T(8,128)(2,1)}), bf16[2,256,1536]{2,1,0:T(8,128)(2,1)}) %all-gather.27.cloned.1.call-update) | async-done | bytes 1572880 | tf_op jit(solution)/shard_map/all_gather | solution.py:160
  527.7 88.8 %all-gather.35.cloned.1.call-done = bf16[4096,1536]{1,0:T(8,128)(2,1)} async-done(((bf16[128,1536]{1,0:T(8,128)(2,1)}), bf16[4096,1536]{1,0:T(8,128)(2,1)}) %all-gather.35.cloned.1.call-update) | async-done | bytes 12582928 | tf_op jit(solution)/shard_map/all_gather | solution.py:123
  630.6 90.9 %all-gather.19.cloned.1.call-done = bf16[2,2048,24,64]{1,3,2,0:T(8,128)(2,1)} async-done(((bf16[2,128,24,64]{1,3,2,0:T(8,128)(2,1)}), bf16[2,2048,24,64]{1,3,2,0:T(8,128)(2,1)}) %all-gather.19.cloned.1.call-update) | async-done | bytes 12582928 | tf_op jit(solution)/shard_map/all_gather | solution.py:168
  721.5 22.9 bitcast_reduce_fusion
  764.8 61.5 %all-gather.17.cloned.1.call-done = bf16[2,2048,24,64]{1,3,2,0:T(8,128)(2,1)} async-done(((bf16[2,128,24,64]{1,3,2,0:T(8,128)(2,1)}), bf16[2,2048,24,64]{1,3,2,0:T(8,128)(2,1)}) %all-gather.17.cloned.1.call-update) | async-done | bytes 12582928 | tf_op jit(solution)/shard_map/all_gather | solution.py:169
  826.3 24.2 fusion.85
  850.5 40.3 %all-gather.29.cloned.1.call-done = bf16[1536,1536]{1,0:T(8,128)(2,1)} async-done(((bf16[48,1536]{1,0:T(8,128)(2,1)}), bf16[1536,1536]{1,0:T(8,128)(2,1)}) %all-gather.29.cloned.1.call-update) | async-done | bytes 4718608 | tf_op jit(solution)/shard_map/all_gather | solution.py:118
  897.3 91.3 %all-gather.33.cloned.1.call-done = bf16[1536,4096]{1,0:T(8,128)(2,1)} async-done(((bf16[48,4096]{1,0:T(8,128)(2,1)}), bf16[1536,4096]{1,0:T(8,128)(2,1)}) %all-gather.33.cloned.1.call-update) | async-done | bytes 12582928 | tf_op jit(solution)/shard_map/all_gather | solution.py:122
  998.1 87.5 %all-gather.31.cloned.1.call-done = bf16[1536,4096]{1,0:T(8,128)(2,1)} async-done(((bf16[48,4096]{1,0:T(8,128)(2,1)}), bf16[1536,4096]{1,0:T(8,128)(2,1)}) %all-gather.31.cloned.1.call-update) | async-done | bytes 12582928 | tf_op jit(solution)/shard_map/all_gather | solution.py:121
  1153.6 54.7 %reduce-scatter.10.cloned.1.call-done = f32[2,16,1536]{2,1,0:T(8,128)} async-done(((f32[2,256,1536]{2,1,0:T(8,128)}), f32[2,16,1536]{2,1,0:T(8,128)}) %reduce-scatter.10.cloned.1.call-update) | async-done | bytes 196624 | tf_op jit(solution)/shard_map/reduce_scatter | solution.py:275
  1222.4 54.7 %reduce-scatter.12.cloned.1.call-done = f32[2,16,1536]{2,1,0:T(8,128)} async-done(((f32[2,256,1536]{2,1,0:T(8,128)}), f32[2,16,1536]{2,1,0:T(8,128)}) %reduce-scatter.12.cloned.1.call-update) | async-done | bytes 196624 | tf_op jit(solution)/shard_map/reduce_scatter | solution.py:276
  1344.6 1068.4 %while.19 = (s32[]{:T(128)}, f32[2,128,24,64]{1,3,2,0:T(8,128)}, bf16[2,128,24,64]{1,3,2,0:T(8,128)(2,1)S(1)}, bf16[2,128,24,64]{1,3,2,0:T(8,128)(2,1)S(1)}, f32...) while((s32[]{:T(128)}, f32[2,128,24,64]{1,3,2,0:T(8,128)}, ...), condition=%wide.region_12.13_spmd.clone, body=%wide.region_11.12_spmd.clone.sunk | while | flops 514326528 | bytes 76358088 | solution.py:294
  1361.8 22.9 collective-permute-done.2
  1387.2 22.7 collective-permute-done.3
  1411.2 23.9 collective-permute-done
  1523.2 22.1 collective-permute-done.3
  1546.7 23.9 collective-permute-done
  1707.2 25.1 collective-permute-done.2
  1734.7 22.7 collective-permute-done.3
  1758.8 23.9 collective-permute-done
  1875.1 22.7 collective-permute-done.3
  1899.2 20.2 collective-permute-done
  2256.4 23.9 collective-permute-done
  2280.3 25.3 collective-permute-done.1
  2462.6 42.7 %all-reduce.6 = (bf16[4,9216]{1,0:T(4,128)(2,1)S(1)}, f32[5,1536]{1,0:T(8,128)}, f32[24]{0:T(128)}) all-reduce(f32[4,9216]{1,0:T(4,128)S(1)} %constant_dynamic-update-slice_fusion.6, f32[5,1536]{1,0:T(8,128)S(1)} %stack.23, f32[24]{0:T(128)S(1)} %subtract_multiply_fusion.2), channel_id=1, replica_groups=mesh['clip'=2,'seq'=16] {'clip','seq'}, use_global_device_ids=true, to_apply=%region_26.27 | all-reduce | flops 44568 | bytes 282816 | tf_op jit(solution)/shard_map/psum | solution.py:336
  2545.5 207.9 %reduce-scatter.24.cloned.1.call-done = f32[48,4096]{1,0:T(8,128)} async-done(((f32[1536,4096]{1,0:T(8,128)}), f32[48,4096]{1,0:T(8,128)}) %reduce-scatter.24.cloned.1.call-update) | async-done | bytes 786448 | tf_op jit(solution)/shard_map/reduce_scatter | solution.py:230
  2753.3 253.0 %reduce-scatter.26.cloned.1.call-done = f32[128,1536]{1,0:T(8,128)} async-done(((f32[4096,1536]{1,0:T(8,128)}), f32[128,1536]{1,0:T(8,128)}) %reduce-scatter.26.cloned.1.call-update) | async-done | bytes 786448 | tf_op jit(solution)/shard_map/reduce_scatter | solution.py:231
  3006.4 270.5 %reduce-scatter.14.cloned.1.call-done = f32[48,4608]{1,0:T(8,128)} async-done(((f32[1536,4608]{1,0:T(8,128)}), f32[48,4608]{1,0:T(8,128)}) %reduce-scatter.14.cloned.1.call-update) | async-done | bytes 884752 | tf_op jit(solution)/shard_map/reduce_scatter | solution.py:324
  (797 shorter events, 1157.2 us)
Async XLA Ops:
  7.2 102.4 %all-gather.21.cloned.1.call-start = ((), (), s32[]{:S(2)}) async-start(), calls=%async_computation.13 | async-start | bytes 12976128 | tf_op jit(solution)/shard_map/all_gather | solution.py:120
  7.9 198.9 %all-gather.25.cloned.1.call-start = ((), (), s32[]{:S(2)}) async-start(), calls=%async_computation.15 | async-start | bytes 12976128 | tf_op jit(solution)/shard_map/all_gather | solution.py:119
  8.7 323.9 %all-gather.13.cloned.1.call-start = ((), (), s32[]{:S(2)}) async-start(), calls=%async_computation.9 | async-start | bytes 19464192 | tf_op jit(solution)/shard_map/all_gather | solution.py:116
  9.4 427.4 %all-gather.15.cloned.1.call-start = ((), (), s32[]{:S(2)}) async-start(), calls=%async_computation.10 | async-start | bytes 14598144 | tf_op jit(solution)/shard_map/all_gather | solution.py:117
  10.0 467.4 %all-gather.23.cloned.1.call-start = ((), (), s32[]{:S(2)}) async-start(), calls=%async_computation.14 | async-start | bytes 1671168 | tf_op jit(solution)/shard_map/all_gather | solution.py:161
  117.0 401.6 %all-gather.27.cloned.1.call-start = ((), (), s32[]{:S(2)}) async-start(), calls=%async_computation.16 | async-start | bytes 1671168 | tf_op jit(solution)/shard_map/all_gather | solution.py:160
  215.1 401.4 %all-gather.35.cloned.1.call-start = ((), (), s32[]{:S(2)}) async-start(), calls=%async_computation.20 | async-start | bytes 12976128 | tf_op jit(solution)/shard_map/all_gather | solution.py:123
  215.8 505.6 %all-gather.19.cloned.1.call-start = ((), (), s32[]{:S(2)}) async-start(), calls=%async_computation.12 | async-start | bytes 13369344 | tf_op jit(solution)/shard_map/all_gather | solution.py:168
  455.3 371.1 %all-gather.17.cloned.1.call-start = ((), (), s32[]{:S(2)}) async-start(), calls=%async_computation.11 | async-start | bytes 13369344 | tf_op jit(solution)/shard_map/all_gather | solution.py:169
  458.0 432.8 %all-gather.29.cloned.1.call-start = ((), (), s32[]{:S(2)}) async-start(), calls=%async_computation.17 | async-start | bytes 4866048 | tf_op jit(solution)/shard_map/all_gather | solution.py:118
  458.6 529.9 %all-gather.33.cloned.1.call-start = ((), (), s32[]{:S(2)}) async-start(), calls=%async_computation.19 | async-start | bytes 12976128 | tf_op jit(solution)/shard_map/all_gather | solution.py:122
  459.3 626.2 %all-gather.31.cloned.1.call-start = ((), (), s32[]{:S(2)}) async-start(), calls=%async_computation.18 | async-start | bytes 12976128 | tf_op jit(solution)/shard_map/all_gather | solution.py:121
  459.9 748.4 %reduce-scatter.10.cloned.1.call-start = ((), (), s32[]{:S(2)}) async-start(), calls=%async_computation.21 | async-start | bytes 3342336 | tf_op jit(solution)/shard_map/reduce_scatter | solution.py:275
  1143.7 133.5 %reduce-scatter.12.cloned.1.call-start = ((), (), s32[]{:S(2)}) async-start(), calls=%async_computation.22 | async-start | bytes 3342336 | tf_op jit(solution)/shard_map/reduce_scatter | solution.py:276
  1153.6 1387.2 %reduce-scatter.18.cloned.1.call-start = ((), (), s32[]{:S(2)}) async-start(), calls=%async_computation.25 | async-start | bytes 25952256 | tf_op jit(solution)/shard_map/reduce_scatter | solution.py:326
  1222.4 1320.7 %reduce-scatter.20.cloned.1.call-start = ((), (), s32[]{:S(2)}) async-start(), calls=%async_computation.26 | async-start | bytes 25952256 | tf_op jit(solution)/shard_map/reduce_scatter | solution.py:327
  1288.5 1257.0 %reduce-scatter.16.cloned.1.call-start = ((), (), s32[]{:S(2)}) async-start(), calls=%async_computation.24 | async-start | bytes 9732096 | tf_op jit(solution)/shard_map/reduce_scatter | solution.py:325
  1294.7 1250.8 %reduce-scatter.22.cloned.1.call-start = ((), (), s32[]{:S(2)}) async-start(), calls=%async_computation.27 | async-start | bytes 25952256 | tf_op jit(solution)/shard_map/reduce_scatter | solution.py:229
  1310.6 1442.8 %reduce-scatter.24.cloned.1.call-start = ((), (), s32[]{:S(2)}) async-start(), calls=%async_computation.28 | async-start | bytes 25952256 | tf_op jit(solution)/shard_map/reduce_scatter | solution.py:230
  1325.4 1681.0 %reduce-scatter.26.cloned.1.call-start = ((), (), s32[]{:S(2)}) async-start(), calls=%async_computation.29 | async-start | bytes 25952256 | tf_op jit(solution)/shard_map/reduce_scatter | solution.py:231
  1339.0 1937.8 %reduce-scatter.14.cloned.1.call-start = ((), (), s32[]{:S(2)}) async-start(), calls=%async_computation.23 | async-start | bytes 29196288 | tf_op jit(solution)/shard_map/reduce_scatter | solution.py:324
  1355.7 54.2 %collective-permute-start.3 = (bf16[2,128,24,64]{1,3,2,0:T(8,128)(2,1)}, bf16[2,128,24,64]{1,3,2,0:T(8,128)(2,1)S(1)}, u32[]{:S(2)}, u32[]{:S(2)}) collective-permute-start(bf16[2,128,24,64]{1,3,2,0:T(8,128)(2,1)} %fusion.200), channel_id=1, source_target_pairs={{15,0},{0,1},{1,2},{2,3},{3,4},{4,5},{5,6},{6,7},{7,8},{8,9},{9,10... | collective-permute-start | bytes 2359304 | tf_op jit(solution)/shard_map/while/body/eval_jaxpr/ppermute | solution.py:13
  1356.7 78.4 %collective-permute-start = (bf16[2,128,24,64]{1,3,2,0:T(8,128)(2,1)}, bf16[2,128,24,64]{1,3,2,0:T(8,128)(2,1)S(1)}, u32[]{:S(2)}, u32[]{:S(2)}) collective-permute-start(bf16[2,128,24,64]{1,3,2,0:T(8,128)(2,1)} %copy.141), channel_id=1, source_target_pairs={{15,0},{0,1},{1,2},{2,3},{3,4},{4,5},{5,6},{6,7},{7,8},{8,9},{9,10... | collective-permute-start | bytes 2359304 | tf_op jit(solution)/shard_map/while/body/eval_jaxpr/ppermute | solution.py:13
  1356.9 92.7 %collective-permute-start.1 = (bf16[2,128,24,64]{1,3,2,0:T(8,128)(2,1)}, bf16[2,128,24,64]{1,3,2,0:T(8,128)(2,1)S(1)}, u32[]{:S(2)}, u32[]{:S(2)}) collective-permute-start(bf16[2,128,24,64]{1,3,2,0:T(8,128)(2,1)} %copy.142), channel_id=1, source_target_pairs={{15,0},{0,1},{1,2},{2,3},{3,4},{4,5},{5,6},{6,7},{7,8},{8,9},{9,10... | collective-permute-start | bytes 2359304 | tf_op jit(solution)/shard_map/while/body/eval_jaxpr/ppermute | solution.py:13
  1508.3 62.2 %collective-permute-start = (bf16[2,128,24,64]{1,3,2,0:T(8,128)(2,1)}, bf16[2,128,24,64]{1,3,2,0:T(8,128)(2,1)S(1)}, u32[]{:S(2)}, u32[]{:S(2)}) collective-permute-start(bf16[2,128,24,64]{1,3,2,0:T(8,128)(2,1)} %copy.141), channel_id=1, source_target_pairs={{15,0},{0,1},{1,2},{2,3},{3,4},{4,5},{5,6},{6,7},{7,8},{8,9},{9,10... | collective-permute-start | bytes 2359304 | tf_op jit(solution)/shard_map/while/body/eval_jaxpr/ppermute | solution.py:13
  1508.3 71.2 %collective-permute-start.1 = (bf16[2,128,24,64]{1,3,2,0:T(8,128)(2,1)}, bf16[2,128,24,64]{1,3,2,0:T(8,128)(2,1)S(1)}, u32[]{:S(2)}, u32[]{:S(2)}) collective-permute-start(bf16[2,128,24,64]{1,3,2,0:T(8,128)(2,1)} %copy.142), channel_id=1, source_target_pairs={{15,0},{0,1},{1,2},{2,3},{3,4},{4,5},{5,6},{6,7},{7,8},{8,9},{9,10... | collective-permute-start | bytes 2359304 | tf_op jit(solution)/shard_map/while/body/eval_jaxpr/ppermute | solution.py:13
  1703.3 79.3 %collective-permute-start = (bf16[2,128,24,64]{1,3,2,0:T(8,128)(2,1)}, bf16[2,128,24,64]{1,3,2,0:T(8,128)(2,1)S(1)}, u32[]{:S(2)}, u32[]{:S(2)}) collective-permute-start(bf16[2,128,24,64]{1,3,2,0:T(8,128)(2,1)} %copy.141), channel_id=1, source_target_pairs={{15,0},{0,1},{1,2},{2,3},{3,4},{4,5},{5,6},{6,7},{7,8},{8,9},{9,10... | collective-permute-start | bytes 2359304 | tf_op jit(solution)/shard_map/while/body/eval_jaxpr/ppermute | solution.py:13
  1703.3 94.7 %collective-permute-start.1 = (bf16[2,128,24,64]{1,3,2,0:T(8,128)(2,1)}, bf16[2,128,24,64]{1,3,2,0:T(8,128)(2,1)S(1)}, u32[]{:S(2)}, u32[]{:S(2)}) collective-permute-start(bf16[2,128,24,64]{1,3,2,0:T(8,128)(2,1)} %copy.142), channel_id=1, source_target_pairs={{15,0},{0,1},{1,2},{2,3},{3,4},{4,5},{5,6},{6,7},{7,8},{8,9},{9,10... | collective-permute-start | bytes 2359304 | tf_op jit(solution)/shard_map/while/body/eval_jaxpr/ppermute | solution.py:13
  1856.9 62.5 %collective-permute-start = (bf16[2,128,24,64]{1,3,2,0:T(8,128)(2,1)}, bf16[2,128,24,64]{1,3,2,0:T(8,128)(2,1)S(1)}, u32[]{:S(2)}, u32[]{:S(2)}) collective-permute-start(bf16[2,128,24,64]{1,3,2,0:T(8,128)(2,1)} %copy.141), channel_id=1, source_target_pairs={{15,0},{0,1},{1,2},{2,3},{3,4},{4,5},{5,6},{6,7},{7,8},{8,9},{9,10... | collective-permute-start | bytes 2359304 | tf_op jit(solution)/shard_map/while/body/eval_jaxpr/ppermute | solution.py:13
  1856.9 70.9 %collective-permute-start.1 = (bf16[2,128,24,64]{1,3,2,0:T(8,128)(2,1)}, bf16[2,128,24,64]{1,3,2,0:T(8,128)(2,1)S(1)}, u32[]{:S(2)}, u32[]{:S(2)}) collective-permute-start(bf16[2,128,24,64]{1,3,2,0:T(8,128)(2,1)} %copy.142), channel_id=1, source_target_pairs={{15,0},{0,1},{1,2},{2,3},{3,4},{4,5},{5,6},{6,7},{7,8},{8,9},{9,10... | collective-permute-start | bytes 2359304 | tf_op jit(solution)/shard_map/while/body/eval_jaxpr/ppermute | solution.py:13
  2111.2 56.2 %collective-permute-start.1 = (bf16[2,128,24,64]{1,3,2,0:T(8,128)(2,1)}, bf16[2,128,24,64]{1,3,2,0:T(8,128)(2,1)S(1)}, u32[]{:S(2)}, u32[]{:S(2)}) collective-permute-start(bf16[2,128,24,64]{1,3,2,0:T(8,128)(2,1)} %copy.142), channel_id=1, source_target_pairs={{15,0},{0,1},{1,2},{2,3},{3,4},{4,5},{5,6},{6,7},{7,8},{8,9},{9,10... | collective-permute-start | bytes 2359304 | tf_op jit(solution)/shard_map/while/body/eval_jaxpr/ppermute | solution.py:13
  2226.6 79.0 %collective-permute-start.1 = (bf16[2,128,24,64]{1,3,2,0:T(8,128)(2,1)}, bf16[2,128,24,64]{1,3,2,0:T(8,128)(2,1)S(1)}, u32[]{:S(2)}, u32[]{:S(2)}) collective-permute-start(bf16[2,128,24,64]{1,3,2,0:T(8,128)(2,1)} %copy.142), channel_id=1, source_target_pairs={{15,0},{0,1},{1,2},{2,3},{3,4},{4,5},{5,6},{6,7},{7,8},{8,9},{9,10... | collective-permute-start | bytes 2359304 | tf_op jit(solution)/shard_map/while/body/eval_jaxpr/ppermute | solution.py:13
  (244 other events, 6645.4 us)
Sparse Core Ops, SparseCore 0:
  10.9 98.6 all-gather.20
  112.5 94.2 all-gather.24
  209.7 122.8 all-gather.12
  335.4 101.3 all-gather.14
  439.5 37.8 all-gather.22
  480.1 38.5 all-gather.26
  521.6 94.8 all-gather.34
  619.2 102.1 all-gather.18
  724.2 102.1 all-gather.16
  829.1 61.6 all-gather.28
  893.7 94.7 all-gather.32
  991.3 94.2 all-gather.30
  1143.8 64.4 reduce-scatter.9
  1211.9 65.1 reduce-scatter.11
  1283.4 333.6 reduce-scatter.17
  1624.5 340.9 reduce-scatter.19
  1971.8 192.9 reduce-scatter.15
  2172.8 328.4 reduce-scatter.21
  2508.3 245.0 reduce-scatter.23
  2761.3 244.9 reduce-scatter.25
  3013.4 263.4 reduce-scatter.13
where the time goes:
time: 3290 us; the launch traced here: 3280 us
  waiting for transfers between devices  2530 us (77%)
  matrix products  501 us (15%)
  other arithmetic  115 us (3%)
  local copies, waits for them, and re-layouts  74.8 us (2%)
  blocking collectives  42.7 us (1%)
    ppermute x64, waiting for transfers between devices, shifted(): return lax.ppermute(block, axis, route)  767 us
    reduce_scatter x1, waiting for transfers between devices, on_device(): lax.psum_scatter(grad_input, ('clip', 'seq'), scatter_dimension=0, tiled=...  270 us
    reduce_scatter x1, waiting for transfers between devices, on_device(): lax.psum_scatter(grad_down, ('clip', 'seq'), scatter_dimension=0, tiled=T...  253 us
    reduce_scatter x1, waiting for transfers between devices, on_device(): lax.psum_scatter(grad_up, ('clip', 'seq'), scatter_dimension=0, tiled=True)  208 us
    all_gather x1, waiting for transfers between devices, on_device(): lax.all_gather(modulation_weight, ('clip', 'seq'), axis=0, tiled=True)  116 us
    all_gather x1, waiting for transfers between devices, on_device(): lax.all_gather(caption_value_weight, ('clip', 'seq'), axis=0, tiled=True)  99.6 us
    all_gather x1, waiting for transfers between devices, on_device(): lax.all_gather(input_weight, ('clip', 'seq'), axis=0, tiled=True)  95.2 us
    all_gather x1, waiting for transfers between devices, on_device(): lax.all_gather(up_weight, ('clip', 'seq'), axis=0, tiled=True)  91.3 us
  transfers between devices with their start and end apart: 85, of which 81 were waited for; matrix products, arithmetic and copies ran while one was open for 19% of the time, Pallas kernels for 0%

commit v1 on v0

v1 whole, which is shorter than its diff:
```python
import jax
import jax.numpy as jnp
from jax import lax
from jax.sharding import Mesh
from jax.sharding import PartitionSpec as P

EPSILON = 1e-06
NEGATIVE = -1e30
BF = jnp.bfloat16
F32 = jnp.float32
SEQ = ("half", "rep", "tz", "ty", "tc")
GROUPS = ("clip", "half", "rep")
TEAM = ("tz", "ty", "tc")
EVERY = ("clip",) + SEQ


def swap(block, axis):
    return lax.ppermute(block, axis, [(0, 1), (1, 0)])


def dot(left, right, dims, out=F32):
    return lax.dot_general(left, right, (dims, ((), ())), preferred_element_type=out)


def mm(left, right):
    return dot(left, right, ((1,), (0,)))


def mm_t(left, right):
    return dot(left, right, ((1,), (1,)))


def t_mm(left, right):
    return dot(left, right, ((0,), (0,)))


def join(parts, axis=0):
    return jnp.concatenate(parts, axis=axis)


def gather_rows(block):
    half = block.shape[0] // 2
    first, second = block[:half], block[half:]
    first, second = join([first, swap(first, "ty")]), join([second, swap(second, "tz")])
    first, second = join([first, swap(first, "tz")]), join([second, swap(second, "ty")])
    both = join([first, second])
    return join([both, swap(both, "tc")])


def gathered_ids(rank, rows):
    half = rows // 2
    low = jnp.arange(half, dtype=jnp.int32)

    def place(who, part):
        return who * rows + part * half + low

    def chip(who):
        return join(
            [place(who, 0), place(who ^ 2, 0), place(who ^ 4, 0), place(who ^ 6, 0)]
            + [place(who, 1), place(who ^ 4, 1), place(who ^ 2, 1), place(who ^ 6, 1)]
        )

    return join([chip(rank), chip(rank ^ 1)])


def scatter_rows(make, count):
    mid = count // 2
    other = swap(make(mid, count).astype(BF), "tc")
    mine = make(0, mid) + other.astype(F32)
    first, second = mine[: mid // 2], mine[mid // 2 :]
    q = mid // 4
    a, b = swap(first[q:].astype(BF), "tz"), swap(second[q:].astype(BF), "ty")
    first, second = first[:q] + a.astype(F32), second[:q] + b.astype(F32)
    q = q // 2
    a, b = swap(first[q:].astype(BF), "ty"), swap(second[q:].astype(BF), "tz")
    return join([first[:q] + a.astype(F32), second[:q] + b.astype(F32)])


def split_places(rows_last):
    lead = rows_last.shape[:-1]
    half = rows_last.shape[-1] // 16
    tiled = rows_last.reshape(lead + (2, 2, 2, 2, half))
    second = jnp.swapaxes(tiled[..., :, 1, :, :, :], -3, -2)
    return jnp.stack([tiled[..., :, 0, :, :, :], second], axis=-4)


def merge_places(tiled):
    second = jnp.swapaxes(tiled[..., :, 1, :, :, :], -3, -2)
    tiled = jnp.stack([tiled[..., :, 0, :, :, :], second], axis=-4)
    return tiled.reshape(tiled.shape[:-5] + (-1,))


def team_row_sum(values):
    tiled = split_places(values)
    for axis, dim in (("tc", -5), ("ty", -2), ("tz", -3)):
        tiled = tiled + jnp.flip(swap(tiled, axis), dim)
    return merge_places(tiled)


def to_true_blocks(rows, bits):
    width = rows.shape[-1]
    half = rows.shape[0] // 16
    tiled = rows.reshape(2, 2, 2, 2, half, width)
    first = tiled[:, 0]
    second = jnp.swapaxes(tiled[:, 1], 1, 2)
    both = jnp.stack([first, second], axis=3)
    for dim, bit in zip((1, 2, 0), bits):
        both = jnp.where(bit == 1, jnp.flip(both, dim), both)
    return jnp.transpose(both, (1, 2, 0, 3, 4, 5)).reshape(8, 2 * half, width)


def from_true_blocks(blocks, bits):
    width = blocks.shape[-1]
    half = blocks.shape[1] // 2
    both = jnp.transpose(blocks.reshape(2, 2, 2, 2, half, width), (2, 0, 1, 3, 4, 5))
    for dim, bit in zip((1, 2, 0), bits):
        both = jnp.where(bit == 1, jnp.flip(both, dim), both)
    first = both[:, :, :, 0]
    second = jnp.swapaxes(both[:, :, :, 1], 1, 2)
    return jnp.stack([first, second], axis=1).reshape(16 * half, width)


def rms_factor(square_sum, width):
    return lax.rsqrt(square_sum / width + EPSILON)


def rms_apply(values, scaling):
    return values * lax.rsqrt(jnp.mean(values * values, axis=-1, keepdims=True) + EPSILON) * scaling


def rms_back(values, scaling, grad):
    factor = lax.rsqrt(jnp.mean(values * values, axis=-1, keepdims=True) + EPSILON)
    normed = values * factor
    scaled = grad * scaling
    inner = jnp.mean(scaled * normed, axis=-1, keepdims=True)
    return factor * (scaled - normed * inner), jnp.sum(grad * normed, axis=0)


def rope_tables(places, head_dim):
    pair_count = head_dim // 2
    lead_pairs = pair_count // 4
    mid_pairs = (pair_count - lead_pairs) // 2
    last_pairs = pair_count - lead_pairs - mid_pairs
    angles = []
    for which, extent in enumerate((lead_pairs, mid_pairs, last_pairs)):
        offsets = jnp.arange(extent, dtype=F32)
        angles.append(places[which][:, None] * jnp.power(10000.0, -offsets / extent))
    angles = join(angles, axis=1)
    cosine, sine = jnp.cos(angles), jnp.sin(angles)
    return join([cosine, cosine], axis=1), join([-sine, sine], axis=1)


def turn(vectors, cosine, sine):
    rows, width = vectors.shape
    head_dim = cosine.shape[-1]
    heads = vectors.reshape(rows, width // head_dim, head_dim)
    half = head_dim // 2
    crossed = join([heads[..., half:], heads[..., :half]], axis=-1)
    return (heads * cosine[:, None] + crossed * sine[:, None]).reshape(rows, width)


def self_forward(queries, keys, values, scale):
    scores = jnp.einsum("thd,shd->hts", queries, keys, preferred_element_type=F32) * scale
    peak = jnp.max(scores, axis=-1, keepdims=True)
    weights = jnp.exp(scores - peak)
    total = jnp.sum(weights, axis=-1, keepdims=True)
    out = jnp.einsum("hts,shd->htd", weights.astype(BF), values, preferred_element_type=F32)
    return out / total, peak + jnp.log(total)


def self_backward(queries, keys, values, grads, log_total, delta, scale):
    scores = jnp.einsum("thd,shd->hts", queries, keys, preferred_element_type=F32) * scale
    probs = jnp.exp(scores - log_total)
    dp = jnp.einsum("thd,shd->hts", grads, values, preferred_element_type=F32)
    ds = (probs * (dp - delta)).astype(BF)
    dq = jnp.einsum("hts,shd->thd", ds, keys, preferred_element_type=F32) * scale
    dk = jnp.einsum("hts,thd->shd", ds, queries, preferred_element_type=F32) * scale
    dv = jnp.einsum("hts,thd->shd", probs.astype(BF), grads, preferred_element_type=F32)
    return dq, dk, dv


def on_device(
    tokens,
    condition,
    caption,
    caption_lengths,
    positions,
    modulation_weight,
    modulation_bias,
    norm_gains,
    cross_gate,
    input_weight,
    output_weight,
    caption_key_weight,
    caption_value_weight,
    gate_weight,
    up_weight,
    down_weight,
    cotangent,
):
    clips_here, clip_rows, width = tokens.shape
    head_count = cross_gate.shape[0]
    head_dim = width // head_count
    scale = head_dim ** (-0.5)
    team = 8
    heads = head_count // team
    part = heads * head_dim
    groups = lax.axis_size(GROUPS)
    reps = lax.axis_size("rep")
    half = lax.axis_index("half")
    bits = tuple(lax.axis_index(axis) for axis in TEAM)
    rank = bits[0] * 4 + bits[1] * 2 + bits[2]
    clip_pair = lax.axis_index("clip")
    device = lax.axis_index(EVERY)

    def own_clip(block):
        kept = lax.dynamic_index_in_dim(block, half, 0, keepdims=False)
        sent = lax.dynamic_index_in_dim(block, 1 - half, 0, keepdims=False)
        return join([kept, swap(sent, "half")])

    def back_clip(block):
        rows = block.shape[0] // 2
        kept, other = block[:rows], block[rows:]
        other = swap(other.astype(BF), "half").astype(block.dtype)
        return jnp.where(half == 0, jnp.stack([kept, other]), jnp.stack([other, kept]))

    def own_columns(table):
        return lax.dynamic_slice_in_dim(table, rank * part, part, table.ndim - 1)

    shard_rows = modulation_weight.shape[0]
    silu_all = jax.nn.silu(condition).astype(BF)
    silu_rows = lax.dynamic_slice_in_dim(silu_all, device * shard_rows, shard_rows, 1)
    mod_part = mm(silu_rows, modulation_weight)
    mod_part = mod_part.reshape(lax.axis_size("clip"), clips_here, -1)
    mod_pair = lax.dynamic_index_in_dim(mod_part, clip_pair, 0, keepdims=False) + swap(
        lax.dynamic_index_in_dim(mod_part, 1 - clip_pair, 0, keepdims=False), "clip"
    )
    mod_own = lax.dynamic_index_in_dim(mod_pair, half, 0, keepdims=True) + swap(
        lax.dynamic_index_in_dim(mod_pair, 1 - half, 0, keepdims=True), "half"
    )
    if reps > 1:
        mod_own = lax.psum(mod_own, "rep")
    for axis in TEAM:
        mod_own = mod_own + swap(mod_own, axis)
    modulation = mod_own + modulation_bias
    shift_attn, scale_attn, gate_attn, shift_ffn, scale_ffn, gate_ffn = (
        modulation[:, i * width : (i + 1) * width] for i in range(6)
    )

    def team_slice(shard):
        by_rank = jnp.transpose(shard, (1, 0, 2))
        mine = lax.all_to_all(by_rank, TEAM, split_axis=0, concat_axis=0, tiled=True)
        mine = mine.reshape(-1, shard.shape[2])
        return lax.all_gather(mine, GROUPS, axis=0, tiled=True)

    rows_in = input_weight.shape[0]
    w_in = team_slice(
        jnp.transpose(input_weight.reshape(rows_in, 3, team, part), (0, 2, 1, 3)).reshape(
            rows_in, team, 3 * part
        )
    )
    rows_cap = caption_key_weight.shape[0]
    w_cap = team_slice(
        join(
            [
                caption_key_weight.reshape(rows_cap, team, part),
                caption_value_weight.reshape(rows_cap, team, part),
            ],
            axis=2,
        )
    )
    w_out = lax.all_gather(output_weight, EVERY, axis=0, tiled=True)
    ff_block = down_weight.shape[0]

    def ff_columns(weight):
        rows = weight.shape[0]
        tiled = weight.reshape(rows, groups, team, ff_block)
        return jnp.transpose(tiled, (0, 2, 1, 3)).reshape(rows, team, groups * ff_block)

    w_gate_up = team_slice(join([ff_columns(gate_weight), ff_columns(up_weight)], axis=2))
    w_down = lax.all_gather(down_weight, GROUPS, axis=0, tiled=True)
    ff_part = groups * ff_block
    w_gate, w_up = w_gate_up[:, :ff_part], w_gate_up[:, ff_part:]

    token_vals = own_clip(tokens).astype(F32)
    rows_here = token_vals.shape[0]
    team_rows = team * rows_here
    places = own_clip(jnp.transpose(positions, (1, 2, 0)))
    all_places = gather_rows(places)
    cosine, sine = rope_tables(all_places.astype(F32).T, head_dim)
    normed_attn = rms_apply(token_vals, norm_gains[0])
    attn_in = (normed_attn * (1.0 + scale_attn) + shift_attn).astype(BF)
    attn_all = gather_rows(attn_in)
    projected = mm(attn_all, w_in)
    raw_q, raw_k, raw_v = (projected[:, i * part : (i + 1) * part] for i in range(3))
    squares = jnp.stack([jnp.sum(raw_q * raw_q, axis=1), jnp.sum(raw_k * raw_k, axis=1)])
    factors = rms_factor(team_row_sum(squares), width)
    gain_q, gain_k, gain_c = (own_columns(norm_gains[i]) for i in (1, 2, 3))
    factor_q, factor_k = factors[0][:, None], factors[1][:, None]
    queries = turn(raw_q * factor_q * gain_q, cosine, sine).astype(BF)
    keys = turn(raw_k * factor_k * gain_k, cosine, sine).astype(BF)
    values = raw_v.astype(BF)

    cap_rows = own_clip(caption)
    slots_here = caption.shape[1]
    cap_all = gather_rows(cap_rows)
    ids = gathered_ids(rank, cap_rows.shape[0])
    own_rank, own_row = ids // cap_rows.shape[0], ids % cap_rows.shape[0]
    holder = jnp.where(own_row < slots_here, half, 1 - half) * reps + lax.axis_index("rep")
    slot = (holder * team + own_rank) * slots_here + own_row % slots_here
    craw = mm(cap_all, w_cap)
    craw_key, craw_value = craw[:, :part], craw[:, part:]
    factor_c = rms_factor(
        team_row_sum(jnp.sum(craw_key * craw_key, axis=1)[None]), width
    )[0][:, None]
    ckeys = (craw_key * factor_c * gain_c).astype(BF)
    cvalues = craw_value.astype(BF)
    all_keys, all_values, all_ckeys, all_cvalues, all_slots = keys, values, ckeys, cvalues, slot
    if reps > 1:
        all_keys, all_values, all_ckeys, all_cvalues = (
            lax.all_gather(v, "rep", axis=0, tiled=True)
            for v in (keys, values, ckeys, cvalues)
        )
        rep_step = lax.axis_index("rep")
        all_slots = join([slot + (r - rep_step) * team * slots_here for r in range(reps)])
    own_length = lax.dynamic_index_in_dim(caption_lengths, half, 0, keepdims=False)
    live = all_slots < own_length

    def by_head(block):
        return block.reshape(block.shape[0], heads, head_dim)

    q3, k3, v3 = by_head(queries), by_head(all_keys), by_head(all_values)
    ck3, cv3 = by_head(all_ckeys), by_head(all_cvalues)
    o_self, log_total = self_forward(q3, k3, v3, scale)
    cross_scores = jnp.einsum("thd,shd->hts", q3, ck3, preferred_element_type=F32) * scale
    cross_scores = jnp.where(live, cross_scores, NEGATIVE)
    cross_probs = jax.nn.softmax(cross_scores, axis=-1)
    cross_low = cross_probs.astype(BF)
    o_cross = jnp.einsum("hts,shd->htd", cross_low, cv3, preferred_element_type=F32)
    tanh_gate = jnp.tanh(lax.dynamic_slice_in_dim(cross_gate, rank * heads, heads))
    tanh_wide = tanh_gate[:, None, None]
    mixed = jnp.transpose(o_self + tanh_wide * o_cross, (1, 0, 2)).reshape(team_rows, part)
    mixed = to_true_blocks(mixed.astype(BF), bits)
    mixed = lax.all_to_all(mixed, TEAM, split_axis=0, concat_axis=0, tiled=True)
    combined = jnp.transpose(mixed, (1, 0, 2)).reshape(rows_here, width)

    branch = mm(combined, w_out)
    middle = token_vals + gate_attn * branch
    normed_ffn = rms_apply(middle, norm_gains[4])
    ffn_in = (normed_ffn * (1.0 + scale_ffn) + shift_ffn).astype(BF)
    grad_out = own_clip(cotangent).astype(F32)
    d_ffn = (gate_ffn * grad_out).astype(BF)
    d_ffn_all = gather_rows(d_ffn)
    ffn_all = gather_rows(ffn_in)
    gate_vals = mm(ffn_all, w_gate)
    up_vals = mm(ffn_all, w_up)
    hidden = (jax.nn.silu(gate_vals) * up_vals).astype(BF)
    d_hidden = mm_t(d_ffn_all, w_down)
    sig = jax.nn.sigmoid(gate_vals)
    silu_gate = gate_vals * sig
    d_gate = (d_hidden * up_vals * (sig + silu_gate * (1.0 - sig))).astype(BF)
    d_up = (d_hidden * silu_gate).astype(BF)
    d_ffn_in = scatter_rows(
        lambda lo, hi: mm_t(d_gate[lo:hi], w_gate) + mm_t(d_up[lo:hi], w_up), team_rows
    )
    ffn_out = scatter_rows(lambda lo, hi: mm(hidden[lo:hi], w_down), team_rows)
    result = back_clip((middle + gate_ffn * ffn_out).astype(BF))
    d_gate_ffn = jnp.sum(grad_out * ffn_out, axis=0)
    grad_down = t_mm(hidden, d_ffn_all)
    grad_gate = t_mm(ffn_all, d_gate)
    grad_up = t_mm(ffn_all, d_up)

    def own_rows(slice_grad):
        summed = lax.psum_scatter(slice_grad.astype(BF), GROUPS, scatter_dimension=0, tiled=True)
        by_rank = summed.reshape(team, -1, summed.shape[-1])
        by_rank = lax.all_to_all(by_rank, TEAM, split_axis=0, concat_axis=0, tiled=True)
        return jnp.transpose(by_rank, (1, 0, 2)).astype(F32)

    sum_down = lax.psum_scatter(
        grad_down.astype(BF), GROUPS, scatter_dimension=0, tiled=True
    ).astype(F32)
    sum_gate_up = own_rows(join([grad_gate, grad_up], axis=1))

    def ff_rows(block):
        rows = block.shape[0]
        tiled = block.reshape(rows, team, groups, ff_block)
        return jnp.transpose(tiled, (0, 2, 1, 3)).reshape(rows, -1)

    sum_gate, sum_up = ff_rows(sum_gate_up[..., :ff_part]), ff_rows(sum_gate_up[..., ff_part:])

    d_scale_ffn = jnp.sum(d_ffn_in * normed_ffn, axis=0)
    d_shift_ffn = jnp.sum(d_ffn_in, axis=0)
    d_middle_norm, d_gain_ffn = rms_back(middle, norm_gains[4], d_ffn_in * (1.0 + scale_ffn))
    d_middle = grad_out + d_middle_norm
    d_branch = (gate_attn * d_middle).astype(BF)
    d_gate_attn = jnp.sum(d_middle * branch, axis=0)
    d_combined = mm_t(d_branch, w_out).astype(BF)
    grad_output = t_mm(combined, d_branch)
    sum_output = lax.psum_scatter(
        grad_output.astype(BF), EVERY, scatter_dimension=0, tiled=True
    ).astype(F32)
    d_mixed = jnp.transpose(d_combined.reshape(rows_here, team, part), (1, 0, 2))
    d_mixed = lax.all_to_all(d_mixed, TEAM, split_axis=0, concat_axis=0, tiled=True)
    d_self = by_head(from_true_blocks(d_mixed, bits))
    d_self_f = jnp.transpose(d_self.astype(F32), (1, 0, 2))
    d_cross = jnp.transpose((tanh_wide * d_self_f).astype(BF), (1, 0, 2))

    d_cross_gate = jnp.sum(d_self_f * o_cross, axis=(1, 2)) * (1.0 - tanh_gate * tanh_gate)
    cross_dp = jnp.einsum("thd,shd->hts", d_cross, cv3, preferred_element_type=F32)
    cross_delta = jnp.sum(cross_probs * cross_dp, axis=-1, keepdims=True)
    cross_ds = (cross_probs * (cross_dp - cross_delta)).astype(BF)
    dq_cross = jnp.einsum("hts,shd->thd", cross_ds, ck3, preferred_element_type=F32) * scale
    d_ckeys = jnp.einsum("hts,thd->shd", cross_ds, q3, preferred_element_type=F32) * scale
    d_cvalues = jnp.einsum("hts,thd->shd", cross_low, d_cross, preferred_element_type=F32)
    delta = jnp.sum(d_self_f * o_self, axis=-1, keepdims=True)
    dq_self, dk, dv = self_backward(q3, k3, v3, d_self, log_total, delta, scale)
    dq = (dq_self + dq_cross).reshape(team_rows, part)
    dk, dv = dk.reshape(-1, part), dv.reshape(-1, part)
    d_ckeys, d_cvalues = d_ckeys.reshape(-1, part), d_cvalues.reshape(-1, part)
    if reps > 1:
        dk, dv, d_ckeys, d_cvalues = (
            lax.psum_scatter(v, "rep", scatter_dimension=0, tiled=True)
            for v in (dk, dv, d_ckeys, d_cvalues)
        )

    turned_q, turned_k = turn(dq, cosine, -sine), turn(dk, cosine, -sine)
    inner = jnp.stack(
        [
            jnp.sum(turned_q * gain_q * raw_q, axis=1),
            jnp.sum(turned_k * gain_k * raw_k, axis=1),
        ]
    )
    inner = team_row_sum(inner)

    def norm_back(grad, gain, raw, factor, row_sum):
        normed = raw * factor
        return (
            factor * (grad * gain - normed * (factor * row_sum[:, None] / width)),
            jnp.sum(grad * normed, axis=0),
        )

    d_raw_q, d_gain_q = norm_back(turned_q, gain_q, raw_q, factor_q, inner[0])
    d_raw_k, d_gain_k = norm_back(turned_k, gain_k, raw_k, factor_k, inner[1])
    d_projected = join([d_raw_q, d_raw_k, dv], axis=1).astype(BF)
    d_attn_in = scatter_rows(lambda lo, hi: mm_t(d_projected[lo:hi], w_in), team_rows)
    inner_c = team_row_sum(jnp.sum(d_ckeys * gain_c * craw_key, axis=1)[None])[0]
    d_craw, d_gain_c = norm_back(d_ckeys, gain_c, craw_key, factor_c, inner_c)
    d_cap_low = join([d_craw, d_cvalues], axis=1).astype(BF)
    d_caption = scatter_rows(lambda lo, hi: mm_t(d_cap_low[lo:hi], w_cap), cap_all.shape[0])
    d_caption = back_clip(d_caption)
    sum_input = own_rows(t_mm(attn_all, d_projected))
    sum_input = jnp.transpose(sum_input.reshape(rows_in, team, 3, part), (0, 2, 1, 3)).reshape(
        rows_in, -1
    )
    sum_cap = own_rows(t_mm(cap_all, d_cap_low))
    sum_ckey = sum_cap[..., :part].reshape(rows_cap, -1)
    sum_cvalue = sum_cap[..., part:].reshape(rows_cap, -1)

    d_scale_attn = jnp.sum(d_attn_in * normed_attn, axis=0)
    d_shift_attn = jnp.sum(d_attn_in, axis=0)
    d_tokens_norm, d_gain_attn = rms_back(token_vals, norm_gains[0], d_attn_in * (1.0 + scale_attn))
    d_tokens = back_clip(d_middle + d_tokens_norm)

    d_mod = join([d_shift_attn, d_scale_attn, d_gate_attn, d_shift_ffn, d_scale_ffn, d_gate_ffn])

    def placed(values, total, start):
        return lax.dynamic_update_slice_in_dim(jnp.zeros((total,), F32), values, start, 0)

    small = join(
        [d_gain_attn]
        + [placed(v, width, rank * part) for v in (d_gain_q, d_gain_k, d_gain_c)]
        + [d_gain_ffn, placed(d_cross_gate, 128, rank * heads)]
    )
    sums = join([d_mod, small])
    for axis in TEAM:
        sums = sums + swap(sums, axis)
    if reps > 1:
        sums = lax.psum(sums, "rep")
    mod_size = d_mod.shape[0]
    mod_low, small = sums[:mod_size].astype(BF)[None], sums[mod_size:]
    for axis, bit in (("half", half), ("clip", clip_pair)):
        other = swap(mod_low, axis)
        mod_low = jnp.where(bit == 0, join([mod_low, other]), join([other, mod_low]))
        small = small + swap(small, axis)
    gain_sum = small[: 5 * width].reshape(5, width)
    gate_sum = small[5 * width : 5 * width + head_count]
    d_bias = jnp.sum(mod_low.astype(F32), axis=0)
    grad_mod = t_mm(silu_rows, mod_low)
    d_silu = mm_t(mod_low, modulation_weight)
    d_silu = lax.dynamic_update_slice_in_dim(
        jnp.zeros(condition.shape, F32), d_silu, device * shard_rows, 1
    )
    if reps > 1:
        d_silu = lax.psum(d_silu, "rep")
    for axis in ("tc", "ty", "tz", "half", "clip"):
        d_silu = d_silu + swap(d_silu, axis)
    _, silu_back = jax.vjp(jax.nn.silu, condition)
    d_condition = silu_back(d_silu)[0]
    return (
        result,
        d_tokens,
        d_caption,
        d_condition,
        grad_mod,
        d_bias,
        gain_sum,
        gate_sum,
        sum_input,
        sum_output,
        sum_ckey,
        sum_cvalue,
        sum_gate,
        sum_up,
        sum_down,
    )


def solution(mesh):
    clip_count, seq_count = mesh.shape["clip"], mesh.shape["seq"]

    def program(*arrays):
        halves = arrays[0].shape[0] // clip_count
        shape = (clip_count, halves, seq_count // (halves * 8), 2, 2, 2)
        fine = Mesh(mesh.devices.reshape(shape), EVERY)
        rows = P("clip", SEQ, None)
        shard = P(EVERY, None)
        mapped = jax.shard_map(
            on_device,
            mesh=fine,
            in_specs=(
                rows,
                P(),
                rows,
                P("clip"),
                P(None, "clip", SEQ),
                shard,
                P(),
                P(),
                P(),
                shard,
                shard,
                shard,
                shard,
                shard,
                shard,
                shard,
                rows,
            ),
            out_specs=(rows, rows, rows, P(), shard, P(), P(), P()) + (shard,) * 7,
            check_vma=False,
        )
        return mapped(*arrays)

    return program
```

time: 3290 us -> 1030 us (0.31)
  waiting for transfers between devices: 2530 us -> 411 us
  matrix products: 501 us -> 252 us
  starting transfers between devices: 3.95 us -> 105 us
  local copies, waits for them, and re-layouts: 74.8 us -> 125 us
    all_gather x12 -> x5, waiting for transfers between devices: 916 us -> 16.1 us  [the longest x1 16.1 us: on_device(): w_down = lax.all_gather(down_weight, GROUPS, axis=0, tiled=True)]
    reduce_scatter x9 -> x5, waiting for transfers between devices: 841 us -> 52.7 us  [the longest x1 52.7 us: on_device(): lax.psum_scatter(grad_output.astype(BF), EVERY, scatter_dimension=0, tile...]
    ppermute x64 -> x81, waiting for transfers between devices: 767 us -> 330 us  [swap(): return lax.ppermute(block, axis, [(0, 1), (1, 0)])]
    dot_general x112 -> x37, matrix products: 501 us -> 247 us  [the longest x26 118 us: dot(): lax.dot_general(left, right, (dims, ((), ())), preferred_element_type=out)]
    ppermute x64 -> x81, starting transfers between devices: 2.93 us -> 79.8 us  [swap(): return lax.ppermute(block, axis, [(0, 1), (1, 0)])]
    convert_element_type x37 -> x11, other arithmetic: 65.9 us -> 13.1 us  [the longest x1 6.31 us: on_device(): cross_ds = (cross_probs * (cross_dp - cross_delta)).astype(BF)]
    psum x1 -> x0, blocking collectives: 42.7 us -> none  [on_device(): lax.psum((d_mod_full, gain_terms, d_cross_gate), ('clip', 'seq'))]
    unnamed x197 -> x307, local copies, waits for them, and re-layouts: 17 us -> 58 us
  transfers between devices with their start and end apart: 85 -> 97, of which waited for: 81 -> 45; matrix products, arithmetic and copies ran while one was open for 19% -> 42% of each run, Pallas kernels for 0% -> 0%
where the time goes in v1:
time: 1030 us
  waiting for transfers between devices  411 us (40%)
  matrix products  252 us (24%)
  local copies, waits for them, and re-layouts  125 us (12%)
  starting transfers between devices  105 us (10%)
  other arithmetic  85.9 us (8%)
  blocking collectives  32.2 us (3%)
  between operations  17.6 us (2%)
    ppermute x81, waiting for transfers between devices, swap(): return lax.ppermute(block, axis, [(0, 1), (1, 0)])  330 us
    dot_general x26, matrix products, dot(): lax.dot_general(left, right, (dims, ((), ())), preferred_element_type=out)  118 us
    ppermute x81, starting transfers between devices, swap(): return lax.ppermute(block, axis, [(0, 1), (1, 0)])  79.8 us
    unnamed x307, local copies, waits for them, and re-layouts  58 us
    reduce_scatter x1, waiting for transfers between devices, on_device(): lax.psum_scatter(grad_output.astype(BF), EVERY, scatter_dimension=0, tile...  52.7 us
    all_to_all x2, blocking collectives, team_slice(): lax.all_to_all(by_rank, TEAM, split_axis=0, concat_axis=0, tiled=True)  32.2 us
    dot_general x1, matrix products, self_backward(): dp = jnp.einsum('thd,shd->hts', grads, values, preferred_element_type=F32)  28.1 us
    reduce_sum x1, other arithmetic, self_forward(): total = jnp.sum(weights, axis=-1, keepdims=True)  20.7 us
  transfers between devices with their start and end apart: 97, of which 45 were waited for; matrix products, arithmetic and copies ran while one was open for 42% of the time, Pallas kernels for 0%

profile of v1, /device:TPU:0, one launch (start us, length us, event | category | flops | bytes accessed | tf_op | source)
XLA Modules:
  0.0 1028.4 jit_solution(14651454297770577170)
XLA Ops:
  9.9 13.8 %all_to_all.40 = bf16[8,48,576]{2,1,0:T(8,128)(2,1)} all-to-all(bf16[8,48,576]{2,1,0:T(8,128)(2,1)S(1)} %copy.327), channel_id=1, replica_groups=mesh['clip'=2,'half'=2,'rep'=1,'tz'=2,'ty'=2,'tc'=2] {'tz','ty','tc'}, dimensions={0} | all-to-all | bytes 884736 | tf_op jit(solution)/shard_map/all_to_all | solution.py:252
  24.3 18.3 %all_to_all.41 = bf16[8,128,384]{1,2,0:T(8,128)(2,1)S(1)} all-to-all(bf16[8,128,384]{1,2,0:T(8,128)(2,1)S(1)} %maximum_bitcast_fusion), channel_id=1, replica_groups=mesh['clip'=2,'half'=2,'rep'=1,'tz'=2,'ty'=2,'tc'=2] {'tz','ty','tc'}, dimensions={0} | all-to-all | bytes 1572864 | tf_op jit(solution)/shard_map/all_to_all | solution.py:252
  69.0 17.1 %collective-permute-done.16 = s32[128,3]{0,1:T(4,128)S(1)} collective-permute-done((s32[128,3]{0,1:T(4,128)S(1)}, s32[128,3]{0,1:T(4,128)S(1)}, u32[]{:S(2)}, u32[]{:S(2)}) %collective-permute-start.16) | collective-permute-done | bytes 1568 | tf_op jit(solution)/shard_map/ppermute | solution.py:18
  107.6 23.5 %collective-permute-done.2 = f32[1,9216]{1,0:T(1,128)S(1)} collective-permute-done((f32[1,9216]{1,0:T(1,128)S(1)}, f32[1,9216]{1,0:T(1,128)S(1)}, u32[]{:S(2)}, u32[]{:S(2)}) %collective-permute-start.2) | collective-permute-done | bytes 36896 | tf_op jit(solution)/shard_map/ppermute | solution.py:18
  145.9 9.6 collective-permute-done.6
  158.5 31.0 %collective-permute-done.7 = bf16[256,1536]{1,0:T(8,128)(2,1)S(1)} collective-permute-done((bf16[256,1536]{1,0:T(8,128)(2,1)S(1)}, bf16[256,1536]{1,0:T(8,128)(2,1)S(1)}, u32[]{:S(2)}, u32[]{:S(2)}) %collective-permute-start.7) | collective-permute-done | bytes 786464 | tf_op jit(solution)/shard_map/ppermute | solution.py:18
  193.4 10.8 %collective-permute-done.8 = bf16[128,1536]{1,0:T(8,128)(2,1)S(1)} collective-permute-done((bf16[128,1536]{1,0:T(8,128)(2,1)S(1)}, bf16[128,1536]{1,0:T(8,128)(2,1)S(1)}, u32[]{:S(2)}, u32[]{:S(2)}) %collective-permute-start.8) | collective-permute-done | bytes 393248 | tf_op jit(solution)/shard_map/ppermute | solution.py:18
  208.4 12.5 %collective-permute-done.9 = bf16[256,1536]{1,0:T(8,128)(2,1)S(1)} collective-permute-done((bf16[256,1536]{1,0:T(8,128)(2,1)S(1)}, bf16[256,1536]{1,0:T(8,128)(2,1)S(1)}, u32[]{:S(2)}, u32[]{:S(2)}) %collective-permute-start.9) | collective-permute-done | bytes 786464 | tf_op jit(solution)/shard_map/ppermute | solution.py:18
  227.8 8.4 collective-permute-done.24
  254.9 15.5 %collective-permute-done.13 = f32[2,2,2,2,2,128]{5,3,4,1,0,2:T(2,128)S(1)} collective-permute-done((f32[2,2,2,2,2,128]{5,3,4,1,0,2:T(2,128)S(1)}, f32[2,2,2,2,2,128]{5,3,4,1,0,2:T(2,128)S(1)}, u32[]{:S(2)}, u32[]{:S(2)}) %collective-permute-start.13) | collective-permute-done | bytes 16416 | tf_op jit(solution)/shard_map/ppermute | solution.py:18
  290.7 20.1 %multiply_reduce_fusion = (f32[3,2048]{1,0:T(4,128)}, f32[3,2048,2048]{1,2,0:T(8,128)}) fusion(bf16[2048,3,64]{0,2,1:T(8,128)(2,1)S(1)} %bitcast.328, bf16[2048,3,64]{0,2,1:T(8,128)(2,1)S(1)} %bitcast.326), kind=kOutput, calls=%fused_computation.7 | convolution fusion | flops 1635772416 | bytes 51929088 | tf_op jit(solution)/shard_map/thd,shd->hts/dot_general | solution.py:163
  313.7 20.7 %fusion.1 = f32[3,2048]{1,0:T(4,128)} fusion(f32[3,2048,2048]{1,2,0:T(8,128)} %get-tuple-element.287, f32[3,2048]{1,0:T(4,128)} %get-tuple-element.286), kind=kLoop, calls=%fused_computation.4 | loop fusion | flops 37742592 | bytes 50380800 | tf_op jit(solution)/shard_map/reduce_sum | solution.py:166
  344.5 20.0 %fusion.45 = (bf16[2048,3,64]{0,2,1:T(8,128)(2,1)S(1)}, f32[3,2048,64]{1,2,0:T(8,128)}) fusion(f32[3,2048,64]{1,2,0:T(8,128)S(1)} %fusion.48, f32[3]{0:T(128)S(1)} %copy-done.107, f32[2048,3]{0,1:T(4,128)S(1)} %bitcast.362, bf16[2048,3,64]{0,2,1:T(8,128)(2,1)S(1)} %bitcast.324, f32[3,2048,2048]{1,2,0:T(8,128)} %get-tuple-element.287, ...), kind=kOutput, calls=%fused_computation.99 | convolution fusion | flops 1649934336 | bytes 55099404 | tf_op jit(solution)/shard_map/hts,shd->htd/dot_general | solution.py:167
  409.2 21.0 %collective-permute-done.30 = bf16[256,1536]{1,0:T(8,128)(2,1)S(1)} collective-permute-done((bf16[256,1536]{1,0:T(8,128)(2,1)S(1)}, bf16[256,1536]{1,0:T(8,128)(2,1)S(1)}, u32[]{:S(2)}, u32[]{:S(2)}) %collective-permute-start.30) | collective-permute-done | bytes 786464 | tf_op jit(solution)/shard_map/ppermute | solution.py:18
  436.6 11.6 %collective-permute-done.31 = bf16[128,1536]{1,0:T(8,128)(2,1)S(1)} collective-permute-done((bf16[128,1536]{1,0:T(8,128)(2,1)S(1)}, bf16[128,1536]{1,0:T(8,128)(2,1)S(1)}, u32[]{:S(2)}, u32[]{:S(2)}) %collective-permute-start.31) | collective-permute-done | bytes 393248 | tf_op jit(solution)/shard_map/ppermute | solution.py:18
  452.5 13.5 %collective-permute-done.32 = bf16[256,1536]{1,0:T(8,128)(2,1)S(1)} collective-permute-done((bf16[256,1536]{1,0:T(8,128)(2,1)S(1)}, bf16[256,1536]{1,0:T(8,128)(2,1)S(1)}, u32[]{:S(2)}, u32[]{:S(2)}) %collective-permute-start.32) | collective-permute-done | bytes 786464 | tf_op jit(solution)/shard_map/ppermute | solution.py:18
  477.2 8.8 fusion.54
  486.0 8.2 fusion.60
  494.1 16.1 %all-gather.14.cloned.1.call-done = bf16[512,1536]{1,0:T(8,128)(2,1)} async-done(((bf16[128,1536]{1,0:T(8,128)(2,1)}), bf16[512,1536]{1,0:T(8,128)(2,1)}) %all-gather.14.cloned.1.call-update) | async-done | bytes 1572880 | tf_op jit(solution)/shard_map/all_gather | solution.py:281
  510.3 10.8 %multiply_convert_fusion.2 = (bf16[2048,512]{1,0:T(8,128)(2,1)S(1)}, bf16[2048,512]{1,0:T(8,128)(2,1)S(1)}, bf16[2048,512]{1,0:T(8,128)(2,1)S(1)}) fusion(f32[2048,512]{1,0:T(8,128)} %fusion.60, f32[2048,512]{1,0:T(8,128)} %fusion.54, bf16[2048,1536]{1,0:T(8,128)(2,1)} %constant_dynamic-update-slice_fusion.58, ...), kind=kOutput, calls=%fused_computation.22 | convolution fusion | flops 3235905536 | bytes 22544384 | tf_op jit(solution)/shard_map/dot_general | solution.py:22
  551.1 30.6 %collective-permute-done.35 = bf16[256,1536]{1,0:T(8,128)(2,1)} collective-permute-done((bf16[256,1536]{1,0:T(8,128)(2,1)}, bf16[256,1536]{1,0:T(8,128)(2,1)}, u32[]{:S(2)}, u32[]{:S(2)}) %collective-permute-start.35) | collective-permute-done | bytes 786464 | tf_op jit(solution)/shard_map/ppermute | solution.py:18
  650.5 28.1 %multiply_convert_fusion = bf16[3,2048,2048]{1,2,0:T(8,128)(2,1)} fusion(f32[3,2048,2048]{1,2,0:T(8,128)} %get-tuple-element.287, f32[3,2048]{1,0:T(4,128)S(1)} %get-tuple-element.118, f32[3,2048]{1,0:T(4,128)S(1)} %log_add_fusion, bf16[2048,3,64]{0,2,1:T(8,128)(2,1)S(1)} %reshape_reshape.3, bf16[2048,3,64]{0,2,1:T(8,128)(2,1)S(1)} %bitcast.325), kind=kOutput, calls=%fused_computation.1 | convolution fusion | flops 1673527296 | bytes 77119488 | tf_op jit(solution)/shard_map/thd,shd->hts/dot_general | solution.py:174
  678.5 14.5 %broadcast_multiply_fusion = (f32[2048,3,64]{0,2,1:T(8,128)}, f32[2048,3,64]{0,2,1:T(8,128)}) fusion(bf16[2048,3,64]{0,2,1:T(8,128)(2,1)S(1)} %bitcast.330, bf16[3,2048,2048]{1,2,0:T(8,128)(2,1)} %multiply_convert_fusion), kind=kOutput, calls=%fused_computation.188 | convolution fusion | flops 1611005952 | bytes 29097984 | tf_op jit(solution)/shard_map/hts,thd->shd/dot_general | solution.py:177
  693.0 10.8 %fusion.163 = f32[3,64,2048]{2,1,0:T(8,128)S(1)} fusion(bf16[2048,3,64]{0,2,1:T(8,128)(2,1)S(1)} %bitcast.327, bf16[3,2048,2048]{1,2,0:T(8,128)(2,1)} %multiply_convert_fusion), kind=kOutput, calls=%fused_computation.485 | convolution fusion | flops 1610612736 | bytes 27525120 | tf_op jit(solution)/shard_map/hts,shd->thd/dot_general | solution.py:176
  723.5 18.0 %fusion.14 = bf16[3,64,2048]{2,1,0:T(8,128)(2,1)S(1)} fusion(bf16[2048,3,64]{0,2,1:T(8,128)(2,1)S(1)} %reshape_reshape.3, f32[3,2048,2048]{1,2,0:T(8,128)} %get-tuple-element.287, f32[3,2048]{1,0:T(4,128)S(1)} %log_add_fusion), kind=kOutput, calls=%fused_computation.42 | convolution fusion | flops 1648754688 | bytes 51929088 | tf_op jit(solution)/shard_map/hts,thd->shd/dot_general | solution.py:178
  746.5 9.3 convolution_convert_fusion.5
  823.5 7.2 collective-permute-done.67
  830.9 27.4 %collective-permute-done.55 = bf16[256,1536]{1,0:T(8,128)(2,1)S(1)} collective-permute-done((bf16[256,1536]{1,0:T(8,128)(2,1)S(1)}, bf16[256,1536]{1,0:T(8,128)(2,1)S(1)}, u32[]{:S(2)}, u32[]{:S(2)}) %collective-permute-start.55) | collective-permute-done | bytes 786464 | tf_op jit(solution)/shard_map/ppermute | solution.py:18
  860.6 9.3 collective-permute-done.56
  870.0 9.4 collective-permute-done.58
  948.4 9.0 collective-permute-done.77
  964.2 52.7 %reduce-scatter.10.cloned.1.call-done = bf16[48,1536]{1,0:T(8,128)(2,1)} async-done(((bf16[1536,1536]{1,0:T(8,128)(2,1)}), bf16[48,1536]{1,0:T(8,128)(2,1)}) %reduce-scatter.10.cloned.1.call-update) | async-done | bytes 147472 | tf_op jit(solution)/shard_map/reduce_scatter | solution.py:399
  (774 shorter events, 473.1 us)
Async XLA Ops:
  7.2 231.9 %all-gather.6.cloned.1.call-start = ((), (), s32[]{:S(2)}) async-start(), calls=%async_computation.13 | async-start | bytes 2457600 | tf_op jit(solution)/shard_map/all_gather | solution.py:254
  23.7 251.9 %all-gather.8.cloned.1.call-start = ((), (), s32[]{:S(2)}) async-start(), calls=%async_computation.14 | async-start | bytes 3932160 | tf_op jit(solution)/shard_map/all_gather | solution.py:254
  45.0 57.8 %collective-permute-start.1 = (f32[2,9216]{1,0:T(2,128)}, f32[2,9216]{1,0:T(2,128)S(1)}, u32[]{:S(2)}, u32[]{:S(2)}) collective-permute-start(f32[2,9216]{1,0:T(2,128)} %dynamic-slice_bitcast_fusion.6), channel_id=1, source_target_pairs={{0,16},{16,0},{1,17},{17,1},{2,18},{18,2},{3,19},{19,3},{4,20},{20... | collective-permute-start | bytes 221192 | tf_op jit(solution)/shard_map/ppermute | solution.py:18
  47.3 96.1 %collective-permute-start = (bf16[128,1536]{1,0:T(8,128)(2,1)}, bf16[128,1536]{1,0:T(8,128)(2,1)S(1)}, u32[]{:S(2)}, u32[]{:S(2)}) collective-permute-start(bf16[128,1536]{1,0:T(8,128)(2,1)} %get-tuple-element.216), channel_id=1, source_target_pairs={{0,8},{8,0},{1,9},{9,1},{2,10},{10,2},{3,11},{11,3},{4,12},{12,4},... | collective-permute-start | bytes 1179656 | tf_op jit(solution)/shard_map/ppermute | solution.py:18
  50.3 35.8 %collective-permute-start.16 = (s32[128,3]{0,1:T(4,128)S(1)}, s32[128,3]{0,1:T(4,128)S(1)}, u32[]{:S(2)}, u32[]{:S(2)}) collective-permute-start(s32[128,3]{0,1:T(4,128)S(1)} %bitcast.410), channel_id=1, source_target_pairs={{0,8},{8,0},{1,9},{9,1},{2,10},{10,2},{3,11},{11,3},{4,12},{12,4},... | collective-permute-start | bytes 4616 | tf_op jit(solution)/shard_map/ppermute | solution.py:18
  50.4 36.4 %collective-permute-start.14 = (s32[128,3]{0,1:T(4,128)S(1)}, s32[128,3]{0,1:T(4,128)S(1)}, u32[]{:S(2)}, u32[]{:S(2)}) collective-permute-start(s32[128,3]{0,1:T(4,128)S(1)} %bitcast.408), channel_id=1, source_target_pairs={{0,2},{2,0},{1,3},{3,1},{4,6},{6,4},{5,7},{7,5},{8,10},{10,8},{9,1... | collective-permute-start | bytes 4616 | tf_op jit(solution)/shard_map/ppermute | solution.py:18
  53.5 136.9 %collective-permute-start.20 = (bf16[16,4096]{1,0:T(8,128)(2,1)S(1)}, bf16[16,4096]{1,0:T(8,128)(2,1)S(1)}, u32[]{:S(2)}, u32[]{:S(2)}) collective-permute-start(bf16[16,4096]{1,0:T(8,128)(2,1)S(1)} %get-tuple-element.142), channel_id=1, source_target_pairs={{0,2},{2,0},{1,3},{3,1},{4,6},{6,4},{5,7},{7,5},{8,10},{10,8},{9,1... | collective-permute-start | bytes 393224 | tf_op jit(solution)/shard_map/ppermute | solution.py:18
  55.9 312.8 %all-to-all-start.3 = ((bf16[8,48,1024]{2,1,0:T(8,128)(2,1)}), bf16[8,48,1024]{2,1,0:T(8,128)(2,1)}, u32[]{:S(2)}, u32[]{:S(2)}) async-start(bf16[8,48,1024]{2,1,0:T(8,128)(2,1)} %maximum_bitcast_fusion.1), calls=%async_computation.3 | async-start | bytes 1572864 | tf_op jit(solution)/shard_map/all_to_all | solution.py:252
  60.2 324.1 %all-gather.10.cloned.1.call-start = ((), (), s32[]{:S(2)}) async-start(), calls=%async_computation.15 | async-start | bytes 4866048 | tf_op jit(solution)/shard_map/all_gather | solution.py:272
  86.8 56.9 %collective-permute-start.40 = (bf16[128,1536]{1,0:T(8,128)(2,1)S(1)}, bf16[128,1536]{1,0:T(8,128)(2,1)S(1)}, u32[]{:S(2)}, u32[]{:S(2)}) collective-permute-start(bf16[128,1536]{1,0:T(8,128)(2,1)S(1)} %get-tuple-element.196), channel_id=1, source_target_pairs={{0,8},{8,0},{1,9},{9,1},{2,10},{10,2},{3,11},{11,3},{4,12},{12,4},... | collective-permute-start | bytes 1179656 | tf_op jit(solution)/shard_map/ppermute | solution.py:18
  95.7 96.9 %collective-permute-start.22 = (bf16[16,4096]{1,0:T(8,128)(2,1)}, bf16[16,4096]{1,0:T(8,128)(2,1)S(1)}, u32[]{:S(2)}, u32[]{:S(2)}) collective-permute-start(bf16[16,4096]{1,0:T(8,128)(2,1)} %dynamic-slice_bitcast_fusion.4), channel_id=1, source_target_pairs={{0,8},{8,0},{1,9},{9,1},{2,10},{10,2},{3,11},{11,3},{4,12},{12,4},... | collective-permute-start | bytes 393224 | tf_op jit(solution)/shard_map/ppermute | solution.py:18
  155.6 33.9 %collective-permute-start.7 = (bf16[256,1536]{1,0:T(8,128)(2,1)S(1)}, bf16[256,1536]{1,0:T(8,128)(2,1)S(1)}, u32[]{:S(2)}, u32[]{:S(2)}) collective-permute-start(bf16[256,1536]{1,0:T(8,128)(2,1)S(1)} %pad_maximum_fusion.6), channel_id=1, source_target_pairs={{0,4},{4,0},{1,5},{5,1},{2,6},{6,2},{3,7},{7,3},{8,12},{12,8},{9,1... | collective-permute-start | bytes 2359304 | tf_op jit(solution)/shard_map/ppermute | solution.py:18
  190.4 33.9 %collective-permute-start.21 = (bf16[32,4096]{1,0:T(8,128)(2,1)S(1)}, bf16[32,4096]{1,0:T(8,128)(2,1)S(1)}, u32[]{:S(2)}, u32[]{:S(2)}) collective-permute-start(bf16[32,4096]{1,0:T(8,128)(2,1)S(1)} %pad_maximum_fusion.18), channel_id=1, source_target_pairs={{0,4},{4,0},{1,5},{5,1},{2,6},{6,2},{3,7},{7,3},{8,12},{12,8},{9,1... | collective-permute-start | bytes 786440 | tf_op jit(solution)/shard_map/ppermute | solution.py:18
  249.8 124.4 %collective-permute-start.42 = (bf16[256,1536]{1,0:T(8,128)(2,1)}, bf16[256,1536]{1,0:T(8,128)(2,1)}, u32[]{:S(2)}, u32[]{:S(2)}) collective-permute-start(bf16[256,1536]{1,0:T(8,128)(2,1)} %pad_maximum_fusion.12), channel_id=1, source_target_pairs={{0,4},{4,0},{1,5},{5,1},{2,6},{6,2},{3,7},{7,3},{8,12},{12,8},{9,1... | collective-permute-start | bytes 2359304 | tf_op jit(solution)/shard_map/ppermute | solution.py:18
  372.3 104.8 %all-gather.12.cloned.1.call-start = ((), (), s32[]{:S(2)}) async-start(), calls=%async_computation.16 | async-start | bytes 3932160 | tf_op jit(solution)/shard_map/all_gather | solution.py:254
  374.2 136.1 %all-gather.14.cloned.1.call-start = ((), (), s32[]{:S(2)}) async-start(), calls=%async_computation.17 | async-start | bytes 1966080 | tf_op jit(solution)/shard_map/all_gather | solution.py:281
  435.8 31.6 %collective-permute-start.45 = (bf16[1024,1536]{1,0:T(8,128)(2,1)}, bf16[1024,1536]{1,0:T(8,128)(2,1)}, u32[]{:S(2)}, u32[]{:S(2)}) collective-permute-start(bf16[1024,1536]{1,0:T(8,128)(2,1)} %get-tuple-element.188), channel_id=1, source_target_pairs={{0,1},{1,0},{2,3},{3,2},{4,5},{5,4},{6,7},{7,6},{8,9},{9,8},{10,11... | collective-permute-start | bytes 9437192 | tf_op jit(solution)/shard_map/ppermute | solution.py:18
  467.3 310.1 %reduce-scatter.14.cloned.1.call-start = ((), (), s32[]{:S(2)}) async-start(), calls=%async_computation.20 | async-start | bytes 1966080 | tf_op jit(solution)/shard_map/reduce_scatter | solution.py:379
  536.7 49.7 %collective-permute-start.47 = (bf16[256,1536]{1,0:T(8,128)(2,1)}, bf16[256,1536]{1,0:T(8,128)(2,1)}, u32[]{:S(2)}, u32[]{:S(2)}) collective-permute-start(bf16[256,1536]{1,0:T(8,128)(2,1)} %get-tuple-element.160), channel_id=1, source_target_pairs={{0,4},{4,0},{1,5},{5,1},{2,6},{6,2},{3,7},{7,3},{8,12},{12,8},{9,1... | collective-permute-start | bytes 2359304 | tf_op jit(solution)/shard_map/ppermute | solution.py:18
  536.7 49.7 %collective-permute-start.49 = (bf16[256,1536]{1,0:T(8,128)(2,1)}, bf16[256,1536]{1,0:T(8,128)(2,1)}, u32[]{:S(2)}, u32[]{:S(2)}) collective-permute-start(bf16[256,1536]{1,0:T(8,128)(2,1)} %get-tuple-element.161), channel_id=1, source_target_pairs={{0,2},{2,0},{1,3},{3,1},{4,6},{6,4},{5,7},{7,5},{8,10},{10,8},{9,1... | collective-permute-start | bytes 2359304 | tf_op jit(solution)/shard_map/ppermute | solution.py:18
  543.8 38.0 %collective-permute-start.35 = (bf16[256,1536]{1,0:T(8,128)(2,1)}, bf16[256,1536]{1,0:T(8,128)(2,1)}, u32[]{:S(2)}, u32[]{:S(2)}) collective-permute-start(bf16[256,1536]{1,0:T(8,128)(2,1)} %get-tuple-element.162), channel_id=1, source_target_pairs={{0,4},{4,0},{1,5},{5,1},{2,6},{6,2},{3,7},{7,3},{8,12},{12,8},{9,1... | collective-permute-start | bytes 2359304 | tf_op jit(solution)/shard_map/ppermute | solution.py:18
  545.8 35.9 %collective-permute-start.37 = (bf16[256,1536]{1,0:T(8,128)(2,1)}, bf16[256,1536]{1,0:T(8,128)(2,1)}, u32[]{:S(2)}, u32[]{:S(2)}) collective-permute-start(bf16[256,1536]{1,0:T(8,128)(2,1)} %get-tuple-element.163), channel_id=1, source_target_pairs={{0,2},{2,0},{1,3},{3,1},{4,6},{6,4},{5,7},{7,5},{8,10},{10,8},{9,1... | collective-permute-start | bytes 2359304 | tf_op jit(solution)/shard_map/ppermute | solution.py:18
  620.4 187.2 %reduce-scatter.18.cloned.1.call-start = ((), (), s32[]{:S(2)}) async-start(), calls=%async_computation.22 | async-start | bytes 3932160 | tf_op jit(solution)/shard_map/reduce_scatter | solution.py:374
  640.6 264.3 %reduce-scatter.16.cloned.1.call-start = ((), (), s32[]{:S(2)}) async-start(), calls=%async_computation.21 | async-start | bytes 2457600 | tf_op jit(solution)/shard_map/reduce_scatter | solution.py:374
  759.7 181.2 %reduce-scatter.12.cloned.1.call-start = ((), (), s32[]{:S(2)}) async-start(), calls=%async_computation.19 | async-start | bytes 3932160 | tf_op jit(solution)/shard_map/reduce_scatter | solution.py:374
  777.4 239.5 %reduce-scatter.10.cloned.1.call-start = ((), (), s32[]{:S(2)}) async-start(), calls=%async_computation.18 | async-start | bytes 4866048 | tf_op jit(solution)/shard_map/reduce_scatter | solution.py:399
  807.6 82.9 %all-to-all-start.7 = ((bf16[8,48,1024]{2,1,0:T(8,128)(2,1)}), bf16[8,48,1024]{2,1,0:T(8,128)(2,1)}, u32[]{:S(2)}, u32[]{:S(2)}) async-start(bf16[8,48,1024]{2,1,0:T(8,128)(2,1)} %bitcast.366), calls=%async_computation.9 | async-start | bytes 1572864 | tf_op jit(solution)/shard_map/all_to_all | solution.py:376
  813.9 46.5 %collective-permute-start.65 = (bf16[16,4096]{1,0:T(8,128)(2,1)S(1)}, bf16[16,4096]{1,0:T(8,128)(2,1)S(1)}, u32[]{:S(2)}, u32[]{:S(2)}) collective-permute-start(bf16[16,4096]{1,0:T(8,128)(2,1)S(1)} %slice.774), channel_id=1, source_target_pairs={{0,2},{2,0},{1,3},{3,1},{4,6},{6,4},{5,7},{7,5},{8,10},{10,8},{9,1... | collective-permute-start | bytes 393224 | tf_op jit(solution)/shard_map/ppermute | solution.py:18
  822.6 35.7 %collective-permute-start.55 = (bf16[256,1536]{1,0:T(8,128)(2,1)S(1)}, bf16[256,1536]{1,0:T(8,128)(2,1)S(1)}, u32[]{:S(2)}, u32[]{:S(2)}) collective-permute-start(bf16[256,1536]{1,0:T(8,128)(2,1)S(1)} %get-tuple-element.158), channel_id=1, source_target_pairs={{0,4},{4,0},{1,5},{5,1},{2,6},{6,2},{3,7},{7,3},{8,12},{12,8},{9,1... | collective-permute-start | bytes 2359304 | tf_op jit(solution)/shard_map/ppermute | solution.py:18
  823.2 35.1 %collective-permute-start.57 = (bf16[256,1536]{1,0:T(8,128)(2,1)S(1)}, bf16[256,1536]{1,0:T(8,128)(2,1)S(1)}, u32[]{:S(2)}, u32[]{:S(2)}) collective-permute-start(bf16[256,1536]{1,0:T(8,128)(2,1)S(1)} %get-tuple-element.159), channel_id=1, source_target_pairs={{0,2},{2,0},{1,3},{3,1},{4,6},{6,4},{5,7},{7,5},{8,10},{10,8},{9,1... | collective-permute-start | bytes 2359304 | tf_op jit(solution)/shard_map/ppermute | solution.py:18
  830.8 50.0 %collective-permute-start.68 = (bf16[16,4096]{1,0:T(8,128)(2,1)S(1)}, bf16[16,4096]{1,0:T(8,128)(2,1)S(1)}, u32[]{:S(2)}, u32[]{:S(2)}) collective-permute-start(bf16[16,4096]{1,0:T(8,128)(2,1)S(1)} %fusion.85), channel_id=1, source_target_pairs={{0,8},{8,0},{1,9},{9,1},{2,10},{10,2},{3,11},{11,3},{4,12},{12,4},... | collective-permute-start | bytes 393224 | tf_op jit(solution)/shard_map/ppermute | solution.py:18
  943.3 75.3 %all-to-all-start.6 = ((bf16[8,128,384]{1,2,0:T(8,128)(2,1)}), bf16[8,128,384]{1,2,0:T(8,128)(2,1)S(1)}, u32[]{:S(2)}, u32[]{:S(2)}) async-start(bf16[8,128,384]{1,2,0:T(8,128)(2,1)} %copy.371), calls=%async_computation.8 | async-start | bytes 1572864 | tf_op jit(solution)/shard_map/all_to_all | solution.py:376
  (187 other events, 2400.7 us)
Sparse Core Ops, SparseCore 0:
  23.9 64.5 all-gather.5
  90.9 80.6 all-gather.7
  174.6 69.9 all-gather.9
  374.7 71.5 all-gather.11
  467.5 42.7 all-gather.13
  551.2 43.5 reduce-scatter.13
  640.7 69.5 reduce-scatter.17
  759.8 62.3 reduce-scatter.15
  825.1 75.9 reduce-scatter.11
  906.4 110.4 reduce-scatter.9

commit v2 on v1

v2 whole, which is shorter than its diff:
```python
import jax
import jax.numpy as jnp
from jax import lax
from jax.experimental import pallas as pl
from jax.experimental.pallas import tpu as pltpu
from jax.sharding import Mesh
from jax.sharding import PartitionSpec as P

EPSILON = 1e-06
NEGATIVE = -1e30
BF = jnp.bfloat16
F32 = jnp.float32
SEQ = ("half", "rep", "tz", "ty", "tc")
GROUPS = ("clip", "half", "rep")
TEAM = ("tz", "ty", "tc")
EVERY = ("clip",) + SEQ
KERNEL = pltpu.CompilerParams(
    vmem_limit_bytes=56 * 1024 * 1024, dimension_semantics=("arbitrary", "arbitrary")
)


def swap(block, axis):
    return lax.ppermute(block, axis, [(0, 1), (1, 0)])


def after(value, *others):
    return lax.optimization_barrier((value,) + others)[0]


def dot(left, right, left_dim, right_dim):
    dims = (((left_dim,), (right_dim,)), ((), ()))
    return lax.dot_general(left, right, dims, preferred_element_type=F32)


def join(parts, axis=0):
    return jnp.concatenate(parts, axis=axis)


def upright(block):
    return jnp.transpose(block.astype(F32)).astype(BF)


def self_forward_kernel(q_ref, k_ref, v_ref, o_ref, log_ref, k_rows):
    @pl.when(pl.program_id(1) == 0)
    def _():
        k_rows[...] = upright(k_ref[0])

    scores = dot(k_rows[...], q_ref[0], 1, 0)
    peak = jnp.max(scores, axis=0, keepdims=True)
    weights = jnp.exp(scores - peak)
    total = jnp.sum(weights, axis=0, keepdims=True)
    o_ref[0] = dot(v_ref[0], weights.astype(BF), 1, 0) / total
    log_ref[0] = peak + jnp.log(total)


def self_backward_kernel(
    q_ref, g_ref, log_ref, delta_ref, k_ref, v_ref, dq_ref, dk_ref, dv_ref, k_rows, v_rows, dk, dv
):
    step = pl.program_id(1)

    @pl.when(step == 0)
    def _():
        k_rows[...] = upright(k_ref[0])
        v_rows[...] = upright(v_ref[0])
        dk[...] = jnp.zeros_like(dk)
        dv[...] = jnp.zeros_like(dv)

    q, g = q_ref[0], g_ref[0]
    probs = jnp.exp(dot(k_rows[...], q, 1, 0) - log_ref[0])
    ds = (probs * (dot(v_rows[...], g, 1, 0) - delta_ref[0])).astype(BF)
    dv[...] += dot(probs.astype(BF), g, 1, 1)
    dk[...] += dot(ds, q, 1, 1)
    dq_ref[0] = dot(k_ref[0], ds, 1, 0)

    @pl.when(step == pl.num_programs(1) - 1)
    def _():
        dk_ref[0] = jnp.transpose(dk[...])
        dv_ref[0] = jnp.transpose(dv[...])


def cross_forward_kernel(q_ref, k_ref, v_ref, mask_ref, o_ref):
    scores = dot(upright(k_ref[0]), q_ref[0], 1, 0) + mask_ref[...]
    weights = jnp.exp(scores - jnp.max(scores, axis=0, keepdims=True))
    total = jnp.sum(weights, axis=0, keepdims=True)
    o_ref[0] = dot(v_ref[0], weights.astype(BF), 1, 0) / total


def cross_backward_kernel(
    q_ref, g_ref, k_ref, v_ref, mask_ref, gate_ref, dq_ref, dk_ref, dv_ref, dg_ref
):
    q, g, gate = q_ref[0], g_ref[0], gate_ref[0, 0:1, 0:1]
    scores = dot(upright(k_ref[0]), q, 1, 0) + mask_ref[...]
    weights = jnp.exp(scores - jnp.max(scores, axis=0, keepdims=True))
    probs = weights / jnp.sum(weights, axis=0, keepdims=True)
    dp = dot(upright(v_ref[0]), g, 1, 0)
    inner = jnp.sum(probs * dp, axis=0, keepdims=True)
    ds = (probs * (gate * (dp - inner))).astype(BF)
    dg_ref[0] = inner
    dq_ref[0] = dot(k_ref[0], ds, 1, 0)
    dk = dot(q, ds, 1, 1)
    dv = dot(g, probs.astype(BF), 1, 1) * gate

    @pl.when(pl.program_id(1) == 0)
    def _():
        dk_ref[0] = dk
        dv_ref[0] = dv

    @pl.when(pl.program_id(1) > 0)
    def _():
        dk_ref[0] += dk
        dv_ref[0] += dv


def by_query(rows, block):
    return pl.BlockSpec((1, rows, block), lambda h, i: (h, 0, i))


def whole_head(rows, columns):
    return pl.BlockSpec((1, rows, columns), lambda h, i: (h, 0, 0))


def mask_spec(rows):
    return pl.BlockSpec((rows, 1), lambda h, i: (0, 0))


def f32(*shape):
    return jax.ShapeDtypeStruct(shape, F32)


def query_block(rows, keys, most):
    block = rows
    while block > 128 and block * keys > most:
        block //= 2
    return block


def self_forward(q, k, v):
    heads, dim, rows = q.shape
    keys = k.shape[2]
    block = query_block(rows, keys, 1 << 21)
    return pl.pallas_call(
        self_forward_kernel,
        grid=(heads, rows // block),
        in_specs=[by_query(dim, block), whole_head(dim, keys), whole_head(dim, keys)],
        out_specs=[by_query(dim, block), by_query(1, block)],
        out_shape=[f32(heads, dim, rows), f32(heads, 1, rows)],
        scratch_shapes=[pltpu.VMEM((keys, dim), BF)],
        compiler_params=KERNEL,
    )(q, k, v)


def self_backward(q, g, log_total, delta, k, v):
    heads, dim, rows = q.shape
    keys = k.shape[2]
    block = query_block(rows, keys, 1 << 20)
    held = [pltpu.VMEM((keys, dim), t) for t in (BF, BF, F32, F32)]
    return pl.pallas_call(
        self_backward_kernel,
        grid=(heads, rows // block),
        in_specs=[by_query(dim, block)] * 2
        + [by_query(1, block)] * 2
        + [whole_head(dim, keys)] * 2,
        out_specs=[by_query(dim, block), whole_head(dim, keys), whole_head(dim, keys)],
        out_shape=[f32(heads, dim, rows), f32(heads, dim, keys), f32(heads, dim, keys)],
        scratch_shapes=held,
        compiler_params=KERNEL,
    )(q, g, log_total, delta, k, v)


def cross_forward(q, k, v, mask):
    heads, dim, rows = q.shape
    keys = k.shape[2]
    block = query_block(rows, keys, 1 << 19)
    return pl.pallas_call(
        cross_forward_kernel,
        grid=(heads, rows // block),
        in_specs=[
            by_query(dim, block),
            whole_head(dim, keys),
            whole_head(dim, keys),
            mask_spec(keys),
        ],
        out_specs=by_query(dim, block),
        out_shape=f32(heads, dim, rows),
        compiler_params=KERNEL,
    )(q, k, v, mask)


def cross_backward(q, g, k, v, mask, gate):
    heads, dim, rows = q.shape
    keys = k.shape[2]
    block = query_block(rows, keys, 1 << 19)
    return pl.pallas_call(
        cross_backward_kernel,
        grid=(heads, rows // block),
        in_specs=[
            by_query(dim, block),
            by_query(dim, block),
            whole_head(dim, keys),
            whole_head(dim, keys),
            mask_spec(keys),
            whole_head(8, 128),
        ],
        out_specs=[
            by_query(dim, block),
            whole_head(dim, keys),
            whole_head(dim, keys),
            by_query(1, block),
        ],
        out_shape=[
            f32(heads, dim, rows),
            f32(heads, dim, keys),
            f32(heads, dim, keys),
            f32(heads, 1, rows),
        ],
        compiler_params=KERNEL,
    )(q, g, k, v, mask, gate)


def gather_parts(first, second):
    first = jnp.stack([first, swap(first, "ty")])
    second = jnp.stack([second, swap(second, "tz")])
    first = jnp.stack([first, swap(first, "tz")])
    second = jnp.stack([second, swap(second, "ty")], axis=1)
    return jnp.stack([first, second])


def gather_rows(block):
    half = block.shape[0] // 2
    both = gather_parts(block[:half], block[half:])
    return jnp.stack([both, swap(both, "tc")]).reshape(-1, block.shape[1])


def scatter_rows(make, count):
    other = swap(make(1).astype(BF), "tc")
    mine = make(0) + other.astype(F32)
    first, second = mine[: count // 4], mine[count // 4 :]
    rows = count // 16
    second = second.reshape(2, 2, rows, -1)
    a, b = swap(first[2 * rows :].astype(BF), "tz"), swap(second[:, 1].astype(BF), "ty")
    first, second = first[: 2 * rows] + a.astype(F32), second[:, 0] + b.astype(F32)
    a, b = swap(first[rows:].astype(BF), "ty"), swap(second[1].astype(BF), "tz")
    return join([first[:rows] + a.astype(F32), second[0] + b.astype(F32)])


def team_row_sum(values):
    tiled = values.reshape(values.shape[0], 2, 2, 2, 2, -1)
    for axis, dim in (("tc", 1), ("ty", 4), ("tz", 3)):
        tiled = tiled + jnp.flip(swap(tiled, axis), dim)
    return tiled.reshape(values.shape)


def flip_by(tiled, bits):
    for dim, bit in enumerate(bits):
        tiled = jnp.where(bit == 1, jnp.flip(tiled, dim), tiled)
    return tiled


def to_ranks(columns, bits):
    width = columns.shape[0]
    tiled = columns.reshape(width, 2, 2, 2, 2, -1)
    tiled = flip_by(jnp.transpose(tiled, (3, 4, 1, 0, 2, 5)), bits)
    return tiled.reshape(8, width, -1)


def from_ranks(blocks, bits):
    width = blocks.shape[1]
    tiled = flip_by(blocks.reshape(2, 2, 2, width, 2, -1), bits)
    return jnp.transpose(tiled, (3, 2, 4, 0, 1, 5)).reshape(width, -1)


def row_factor(values):
    return lax.rsqrt(jnp.mean(values * values, axis=-1, keepdims=True) + EPSILON)


def rms_back(grad, gain, normed, factor, row_mean):
    return factor * (grad * gain - normed * row_mean)


def rope_tables(places, head_dim):
    pair_count = head_dim // 2
    lead_pairs = pair_count // 4
    mid_pairs = (pair_count - lead_pairs) // 2
    last_pairs = pair_count - lead_pairs - mid_pairs
    angles = []
    for which, extent in enumerate((lead_pairs, mid_pairs, last_pairs)):
        offsets = jnp.arange(extent, dtype=F32)
        angles.append(jnp.power(10000.0, -offsets / extent)[:, None] * places[which][None])
    angles = join(angles)
    cosine, sine = jnp.cos(angles), jnp.sin(angles)
    return join([cosine, cosine]), join([-sine, sine])


def turn(vectors, cosine, sine):
    half = vectors.shape[1] // 2
    crossed = join([vectors[:, half:], vectors[:, :half]], axis=1)
    return vectors * cosine + crossed * sine


def on_device(
    tokens,
    condition,
    caption,
    caption_lengths,
    positions,
    modulation_weight,
    modulation_bias,
    norm_gains,
    cross_gate,
    input_weight,
    output_weight,
    caption_key_weight,
    caption_value_weight,
    gate_weight,
    up_weight,
    down_weight,
    cotangent,
):
    clips_here, clip_rows, width = tokens.shape
    head_count = cross_gate.shape[0]
    head_dim = width // head_count
    scale = head_dim ** (-0.5)
    team = 8
    heads = head_count // team
    part = heads * head_dim
    groups = lax.axis_size(GROUPS)
    reps = lax.axis_size("rep")
    half = lax.axis_index("half")
    bits = tuple(lax.axis_index(axis) for axis in TEAM)
    rank = bits[0] * 4 + bits[1] * 2 + bits[2]
    clip_pair = lax.axis_index("clip")
    device = lax.axis_index(EVERY)

    def pick(block, index, dim=0, keep=False):
        return lax.dynamic_index_in_dim(block, index, dim, keepdims=keep)

    def own_clip(block):
        return pick(block, half), swap(pick(block, 1 - half), "half")

    def back_clip(block):
        rows = block.shape[0] // 2
        kept, other = block[:rows], block[rows:]
        other = swap(other.astype(BF), "half").astype(block.dtype)
        return jnp.where(half == 0, jnp.stack([kept, other]), jnp.stack([other, kept]))

    def own_columns(table):
        return lax.dynamic_slice_in_dim(table, rank * part, part, table.ndim - 1)

    places = jnp.pad(
        jnp.transpose(positions, (1, 0, 2)).astype(BF),
        ((0, 0), (0, 5), (0, width - clip_rows)),
    )
    kept, received = own_clip(join([tokens, places], axis=1))

    def chip_square(block):
        block = jnp.stack([block, swap(block, "tz")])
        return jnp.stack([block, swap(block, "ty")], axis=1)

    pieces = [chip_square(kept), chip_square(received)]
    pieces = pieces + [swap(piece, "tc") for piece in pieces]
    tokens_all = join([piece[:, :, :clip_rows].reshape(-1, width) for piece in pieces])
    all_places = join(
        [
            jnp.transpose(piece[:, :, clip_rows : clip_rows + 3, :clip_rows], (2, 0, 1, 3)).reshape(
                3, -1
            )
            for piece in pieces
        ],
        axis=1,
    ).astype(F32)
    token_vals = join([kept[:clip_rows], received[:clip_rows]]).astype(F32)
    rows_here = token_vals.shape[0]
    team_rows = team * rows_here

    shard_rows = modulation_weight.shape[0]
    silu_all = jax.nn.silu(condition).astype(BF)
    silu_rows = lax.dynamic_slice_in_dim(silu_all, device * shard_rows, shard_rows, 1)
    mod_part = dot(silu_rows, modulation_weight, 1, 0)
    mod_part = mod_part.reshape(lax.axis_size("clip"), clips_here, -1)
    mod_pair = pick(mod_part, clip_pair) + swap(pick(mod_part, 1 - clip_pair), "clip")
    mod_own = pick(mod_pair, half, keep=True) + swap(pick(mod_pair, 1 - half, keep=True), "half")
    if reps > 1:
        mod_own = lax.psum(mod_own, "rep")
    for axis in TEAM:
        mod_own = mod_own + swap(mod_own, axis)
    modulation = mod_own + modulation_bias
    shift_attn, scale_attn, gate_attn, shift_ffn, scale_ffn, gate_ffn = (
        modulation[:, i * width : (i + 1) * width] for i in range(6)
    )

    def team_slice(shard):
        by_rank = jnp.transpose(shard, (1, 0, 2))
        mine = lax.all_to_all(by_rank, TEAM, split_axis=0, concat_axis=0, tiled=True)
        mine = mine.reshape(-1, shard.shape[2])
        return lax.all_gather(mine, GROUPS, axis=0, tiled=True)

    rows_in = input_weight.shape[0]
    w_in = team_slice(
        jnp.transpose(input_weight.reshape(rows_in, 3, team, part), (0, 2, 1, 3)).reshape(
            rows_in, team, 3 * part
        )
    )
    later = after(
        (caption_key_weight, caption_value_weight, output_weight, gate_weight, up_weight), mod_own
    )
    caption_key_weight, caption_value_weight, output_weight, gate_weight, up_weight = later
    rows_cap = caption_key_weight.shape[0]
    w_cap = team_slice(
        join(
            [
                caption_key_weight.reshape(rows_cap, team, part),
                caption_value_weight.reshape(rows_cap, team, part),
            ],
            axis=2,
        )
    )

    def both_sides(block, axis, bit, dim):
        other = swap(block, axis)
        return jnp.where(
            bit == 0, jnp.stack([block, other], dim), jnp.stack([other, block], dim)
        )

    out_rows = output_weight.shape[0]
    w_out = both_sides(both_sides(output_weight, "half", half, 0), "clip", clip_pair, 0)
    if reps > 1:
        w_out = lax.all_gather(w_out, "rep", axis=2)
    else:
        w_out = w_out[:, :, None]
    for place, axis in enumerate(TEAM):
        w_out = both_sides(w_out, axis, bits[place], 3 + place)
    w_out = w_out.reshape(-1, width)
    ff_block = down_weight.shape[0]

    def ff_columns(weight):
        rows = weight.shape[0]
        tiled = weight.reshape(rows, groups, team, ff_block)
        return jnp.transpose(tiled, (0, 2, 1, 3)).reshape(rows, team, groups * ff_block)

    w_gate_up = team_slice(join([ff_columns(gate_weight), ff_columns(up_weight)], axis=2))
    w_down = lax.all_gather(after(down_weight, w_cap), GROUPS, axis=0, tiled=True)
    ff_part = groups * ff_block

    def by_head(block):
        return block.reshape(heads, head_dim, block.shape[-1])

    tokens_f = tokens_all.astype(F32)
    factor_all = row_factor(tokens_f)
    attn_all = (
        tokens_f * factor_all * (norm_gains[0] * (1.0 + scale_attn)) + shift_attn
    ).astype(BF)
    cosine, sine = rope_tables(all_places, head_dim)
    raw_qk = dot(w_in[:, : 2 * part], attn_all, 0, 1).reshape(2, heads, head_dim, team_rows)
    squares = jnp.sum(raw_qk * raw_qk, axis=(1, 2))
    factors = lax.rsqrt(team_row_sum(squares) / width + EPSILON)[:, None, None]
    values = by_head(dot(w_in[:, 2 * part :], attn_all, 0, 1).astype(BF))
    gains = jnp.stack([own_columns(norm_gains[i]) for i in (1, 2, 3)])
    gains = gains.reshape(3, heads, head_dim, 1)
    normed_qk = raw_qk * factors
    turned = normed_qk * gains[:2]
    queries = (turn(turned[0], cosine, sine) * scale).astype(BF)
    keys = turn(turned[1], cosine, sine).astype(BF)

    slots_here = caption.shape[1]
    cap_all = gather_rows(join(own_clip(after(caption, tokens_all))))
    source = jnp.arange(2, dtype=jnp.int32)

    def along(dim):
        return source.reshape([2 if i == dim else 1 for i in range(5)])

    from_rank = rank ^ (along(2) * 4 + along(3) * 2 + along(0))
    holder = (half ^ along(1)) * reps + lax.axis_index("rep")
    slots = (holder * team + from_rank) * slots_here + jnp.arange(slots_here, dtype=jnp.int32)
    slots = slots.reshape(-1)
    craw = dot(w_cap, cap_all, 0, 1)
    craw_key = by_head(craw[:part])
    factor_c = lax.rsqrt(
        team_row_sum(jnp.sum(craw_key * craw_key, axis=(0, 1))[None]) / width + EPSILON
    )[None]
    normed_c = craw_key * factor_c
    ckeys = (normed_c * gains[2]).astype(BF)
    cvalues = by_head(craw[part:]).astype(BF)
    all_keys, all_values, all_ckeys, all_cvalues = keys, values, ckeys, cvalues
    if reps > 1:
        all_keys, all_values, all_ckeys, all_cvalues = (
            lax.all_gather(v, "rep", axis=2, tiled=True) for v in (keys, values, ckeys, cvalues)
        )
        step = lax.axis_index("rep")
        slots = join([slots + (r - step) * team * slots_here for r in range(reps)])
    mask = jnp.where(slots < pick(caption_lengths, half), 0.0, NEGATIVE).astype(F32)[:, None]

    o_self, log_total = self_forward(queries, all_keys, all_values)
    o_cross = cross_forward(queries, all_ckeys, all_cvalues, mask)
    tanh_gate = jnp.tanh(lax.dynamic_slice_in_dim(cross_gate, rank * heads, heads))
    tanh_wide = tanh_gate[:, None, None]
    mixed = (o_self + tanh_wide * o_cross).astype(BF).reshape(part, team_rows)
    mixed = lax.all_to_all(
        to_ranks(mixed, bits), TEAM, split_axis=0, concat_axis=0, tiled=True
    )
    combined = mixed.reshape(width, rows_here)

    branch = dot(combined, w_out, 0, 0)
    middle = token_vals + gate_attn * branch
    factor_f = row_factor(middle)
    core_f = middle * factor_f
    ffn_in = (core_f * norm_gains[4] * (1.0 + scale_ffn) + shift_ffn).astype(BF)
    ffn_all = gather_rows(ffn_in)
    grad_out = join(own_clip(after(cotangent, tokens_all))).astype(F32)
    d_ffn_all = gather_rows((gate_ffn * grad_out).astype(BF))
    w_gate, w_up = w_gate_up[:, :ff_part], w_gate_up[:, ff_part:]
    gate_vals = dot(ffn_all, w_gate, 1, 0)
    up_vals = dot(ffn_all, w_up, 1, 0)
    d_hidden = dot(d_ffn_all, w_down, 1, 1)
    sig = jax.nn.sigmoid(gate_vals)
    silu_gate = gate_vals * sig
    hidden = (silu_gate * up_vals).astype(BF)
    d_gate = (d_hidden * up_vals * (sig + silu_gate * (1.0 - sig))).astype(BF)
    d_up = (d_hidden * silu_gate).astype(BF)

    def side(block, which, dim=0):
        count = block.shape[dim] // 2
        return lax.slice_in_dim(block, which * count, (which + 1) * count, axis=dim)

    d_ffn_in = scatter_rows(
        lambda s: dot(side(d_gate, s), w_gate, 1, 1) + dot(side(d_up, s), w_up, 1, 1), team_rows
    )
    ffn_out = scatter_rows(
        lambda s: dot(side(after(hidden, d_ffn_in), s), w_down, 1, 0), team_rows
    )
    result = back_clip((middle + gate_ffn * ffn_out).astype(BF))
    d_gate_ffn = jnp.sum(grad_out * ffn_out, axis=0)
    grad_down = dot(hidden, d_ffn_all, 0, 0)
    grad_gate = dot(ffn_all, d_gate, 0, 0)
    grad_up = dot(ffn_all, d_up, 0, 0)

    def own_rows(slice_grad):
        summed = lax.psum_scatter(slice_grad.astype(BF), GROUPS, scatter_dimension=0, tiled=True)
        by_rank = summed.reshape(team, -1, summed.shape[-1])
        by_rank = lax.all_to_all(by_rank, TEAM, split_axis=0, concat_axis=0, tiled=True)
        return jnp.transpose(by_rank, (1, 0, 2)).astype(F32)

    sum_down = lax.psum_scatter(
        grad_down.astype(BF), GROUPS, scatter_dimension=0, tiled=True
    ).astype(F32)
    sum_gate_up = own_rows(join([grad_gate, grad_up], axis=1))

    def ff_rows(block):
        rows = block.shape[0]
        tiled = block.reshape(rows, team, groups, ff_block)
        return jnp.transpose(tiled, (0, 2, 1, 3)).reshape(rows, -1)

    sum_gate, sum_up = ff_rows(sum_gate_up[..., :ff_part]), ff_rows(sum_gate_up[..., ff_part:])

    d_shift_ffn = jnp.sum(d_ffn_in, axis=0)
    moment_f = jnp.sum(d_ffn_in * core_f, axis=0)
    d_scale_ffn = moment_f * norm_gains[4]
    d_gain_ffn = moment_f * (1.0 + scale_ffn[0])
    d_core = d_ffn_in * (norm_gains[4] * (1.0 + scale_ffn))
    d_middle = grad_out + factor_f * (
        d_core - core_f * jnp.mean(d_core * core_f, axis=-1, keepdims=True)
    )
    d_branch = (gate_attn * d_middle).astype(BF)
    d_gate_attn = jnp.sum(d_middle * branch, axis=0)
    d_combined = dot(w_out, d_branch, 1, 1).astype(BF)
    d_mixed = lax.all_to_all(
        d_combined.reshape(team, part, rows_here), TEAM, split_axis=0, concat_axis=0, tiled=True
    )
    d_self = by_head(from_ranks(d_mixed, bits))

    def kept_sum(block, axis, bit, dim):
        other = swap(pick(block, 1 - bit, dim).astype(BF), axis)
        return pick(block, bit, dim) + other.astype(F32)

    sum_output = dot(combined, d_branch, 1, 0).reshape(
        lax.axis_size("clip"), clips_here, reps, 2, 2, 2, out_rows, width
    )
    for place in (2, 1, 0):
        sum_output = kept_sum(sum_output, TEAM[place], bits[place], 3 + place)
    if reps > 1:
        sum_output = lax.psum_scatter(sum_output, "rep", scatter_dimension=2, tiled=True)
    sum_output = sum_output[:, :, 0]
    sum_output = kept_sum(sum_output, "clip", clip_pair, 0)
    sum_output = kept_sum(sum_output, "half", half, 0)

    gate_tile = jnp.broadcast_to(tanh_wide, (heads, 8, 128))
    dq_cross, d_ckeys, d_cvalues, gate_rows = cross_backward(
        queries, d_self, all_ckeys, all_cvalues, mask, gate_tile
    )
    d_cross_gate = jnp.sum(gate_rows, axis=(1, 2)) * (1.0 - tanh_gate * tanh_gate)
    if reps > 1:
        d_ckeys, d_cvalues = (
            lax.psum_scatter(v, "rep", scatter_dimension=2, tiled=True)
            for v in (d_ckeys, d_cvalues)
        )

    def team_mean(block):
        return jnp.sum(block, axis=(-3, -2))

    scaled_c = d_ckeys * gains[2]
    mean_c = team_row_sum(team_mean(scaled_c * normed_c)[None])[None] / width
    d_craw = factor_c * (scaled_c - normed_c * mean_c)
    d_gain_c = jnp.sum(d_ckeys * normed_c, axis=2).reshape(part)
    d_cap_low = join([d_craw, d_cvalues]).reshape(2 * part, -1).astype(BF)
    sum_cap = own_rows(dot(cap_all, d_cap_low, 0, 1))
    sum_ckey = sum_cap[..., :part].reshape(rows_cap, -1)
    sum_cvalue = sum_cap[..., part:].reshape(rows_cap, -1)
    d_caption = back_clip(
        scatter_rows(lambda s: dot(side(d_cap_low, s, 1), w_cap, 0, 1), cap_all.shape[0])
    )

    delta = jnp.sum(d_self.astype(F32) * o_self, axis=1, keepdims=True)
    dq_self, dk, dv = self_backward(queries, d_self, log_total, delta, all_keys, all_values)
    if reps > 1:
        dk, dv = (lax.psum_scatter(v, "rep", scatter_dimension=2, tiled=True) for v in (dk, dv))

    turned_grad = jnp.stack(
        [turn((dq_self + dq_cross) * scale, cosine, -sine), turn(dk, cosine, -sine)]
    )
    scaled_qk = turned_grad * gains[:2]
    mean_qk = team_row_sum(team_mean(scaled_qk * normed_qk))[:, None, None] / width
    d_gain_qk = jnp.sum(turned_grad * normed_qk, axis=3).reshape(2, part)
    d_qk = (factors * (scaled_qk - normed_qk * mean_qk)).reshape(2 * part, team_rows)
    d_projected = join([d_qk, dv.reshape(part, team_rows)]).astype(BF)
    sum_input = own_rows(dot(attn_all, d_projected, 0, 1))
    sum_input = jnp.transpose(sum_input.reshape(rows_in, team, 3, part), (0, 2, 1, 3)).reshape(
        rows_in, -1
    )
    sides = [dot(side(d_projected, s, 1), w_in, 0, 1) for s in (0, 1)]
    d_attn_in = scatter_rows(lambda s: sides[s], team_rows)

    d_shift_attn = sum(jnp.sum(block, axis=0) for block in sides)
    moment_a = sum(
        jnp.sum(sides[s] * (side(tokens_f, s) * side(factor_all, s)), axis=0) for s in (0, 1)
    )
    d_scale_attn = moment_a * norm_gains[0]
    d_gain_attn = moment_a * (1.0 + scale_attn[0])
    factor_a = row_factor(token_vals)
    core_a = token_vals * factor_a
    d_core = d_attn_in * (norm_gains[0] * (1.0 + scale_attn))
    d_tokens = back_clip(
        d_middle
        + factor_a * (d_core - core_a * jnp.mean(d_core * core_a, axis=-1, keepdims=True))
    )

    d_mod = join([d_shift_attn, d_scale_attn, d_gate_attn, d_shift_ffn, d_scale_ffn, d_gate_ffn])

    def placed(values, total, start):
        return lax.dynamic_update_slice_in_dim(jnp.zeros((total,), F32), values, start, 0)

    small = join(
        [d_gain_attn]
        + [placed(v, width, rank * part) for v in (d_gain_qk[0], d_gain_qk[1], d_gain_c)]
        + [d_gain_ffn, placed(d_cross_gate, 128, rank * heads)]
    )
    sums = join([d_mod, small])
    for axis in TEAM:
        sums = sums + swap(sums, axis)
    if reps > 1:
        sums = lax.psum(sums, "rep")
    mod_size = d_mod.shape[0]
    mod_low, small = sums[:mod_size].astype(BF)[None], sums[mod_size:]
    for axis, bit in (("half", half), ("clip", clip_pair)):
        other = swap(mod_low, axis)
        mod_low = jnp.where(bit == 0, join([mod_low, other]), join([other, mod_low]))
        small = small + swap(small, axis)
    gain_sum = small[: 5 * width].reshape(5, width)
    gate_sum = small[5 * width : 5 * width + head_count]
    d_bias = jnp.sum(mod_low.astype(F32), axis=0)
    grad_mod = dot(silu_rows, mod_low, 0, 0)
    d_silu = dot(mod_low, modulation_weight, 1, 1)
    d_silu = lax.dynamic_update_slice_in_dim(
        jnp.zeros(condition.shape, F32), d_silu, device * shard_rows, 1
    )
    if reps > 1:
        d_silu = lax.psum(d_silu, "rep")
    for axis in ("tc", "ty", "tz", "half", "clip"):
        d_silu = d_silu + swap(d_silu, axis)
    _, silu_back = jax.vjp(jax.nn.silu, condition)
    d_condition = silu_back(d_silu)[0]
    return (
        result,
        d_tokens,
        d_caption,
        d_condition,
        grad_mod,
        d_bias,
        gain_sum,
        gate_sum,
        sum_input,
        sum_output,
        sum_ckey,
        sum_cvalue,
        sum_gate,
        sum_up,
        sum_down,
    )


def solution(mesh):
    clip_count, seq_count = mesh.shape["clip"], mesh.shape["seq"]

    def program(*arrays):
        halves = arrays[0].shape[0] // clip_count
        shape = (clip_count, halves, seq_count // (halves * 8), 2, 2, 2)
        fine = Mesh(mesh.devices.reshape(shape), EVERY)
        rows = P("clip", SEQ, None)
        shard = P(EVERY, None)
        mapped = jax.shard_map(
            on_device,
            mesh=fine,
            in_specs=(
                rows,
                P(),
                rows,
                P("clip"),
                P(None, "clip", SEQ),
                shard,
                P(),
                P(),
                P(),
                shard,
                shard,
                shard,
                shard,
                shard,
                shard,
                shard,
                rows,
            ),
            out_specs=(rows, rows, rows, P(), shard, P(), P(), P()) + (shard,) * 7,
            check_vma=False,
        )
        return mapped(*arrays)

    return program
```

time: 1030 us -> 959 us (0.931)
  matrix products: 252 us -> 131 us
  waiting for transfers between devices: 411 us -> 332 us
  Pallas kernels: 0 us -> 71.8 us
  other arithmetic: 85.9 us -> 146 us
  blocking collectives: 32.2 us -> 0 us
  starting transfers between devices: 105 us -> 122 us
    dot_general x37 -> x27, matrix products: 247 us -> 131 us  [dot(): return lax.dot_general(left, right, dims, preferred_element_type=F32)]
    pallas_call x0 -> x4, Pallas kernels: none -> 71.8 us  [the longest x1 38.2 us: self_backward(): pl.pallas_call(self_backward_kernel, grid=(heads, rows // block), in_spec...]
    reduce_scatter x1 -> x0, waiting for transfers between devices: 52.7 us -> none  [on_device(): lax.psum_scatter(grad_output.astype(BF), EVERY, scatter_dimension=0, tile...]
    all_to_all x2 -> x0, blocking collectives: 32.2 us -> none  [team_slice(): lax.all_to_all(by_rank, TEAM, split_axis=0, concat_axis=0, tiled=True)]
    another operation x10 -> x30, other arithmetic: 0.23 us -> 31.2 us  [the longest x6 12.3 us: gather_rows(): return jnp.stack([both, swap(both, 'tc')]).reshape(-1, block.shape[1])]
    ppermute x81 -> x86, waiting for transfers between devices: 330 us -> 301 us  [swap(): return lax.ppermute(block, axis, [(0, 1), (1, 0)])]
    unnamed x307 -> x278, local copies, waits for them, and re-layouts: 58 us -> 39.8 us
    convert_element_type x6 -> x8, other arithmetic: 9.58 us -> 24.3 us  [the longest x1 7.3 us: on_device(): attn_all = (tokens_f * factor_all * (norm_gains[0] * (1.0 + scale_attn))...]
  transfers between devices with their start and end apart: 97 -> 102, of which waited for: 45 -> 40; matrix products, arithmetic and copies ran while one was open for 42% -> 38% of each run, Pallas kernels for 0% -> 8%
where the time goes in v2:
time: 959 us; the launch traced here: 950 us
  waiting for transfers between devices  332 us (35%)
  other arithmetic  146 us (15%)
  local copies, waits for them, and re-layouts  131 us (14%)
  matrix products  131 us (14%)
  starting transfers between devices  122 us (13%)
  Pallas kernels  71.8 us (7%)
  between operations  17 us (2%)
    ppermute x86, waiting for transfers between devices, swap(): return lax.ppermute(block, axis, [(0, 1), (1, 0)])  301 us
    dot_general x27, matrix products, dot(): return lax.dot_general(left, right, dims, preferred_element_type=F32)  131 us
    ppermute x86, starting transfers between devices, swap(): return lax.ppermute(block, axis, [(0, 1), (1, 0)])  89.1 us
    unnamed x278, local copies, waits for them, and re-layouts  39.8 us
    pallas_call x1, Pallas kernels, self_backward(): pl.pallas_call(self_backward_kernel, grid=(heads, rows // block), in_spec...  38.2 us
    all_gather x1, waiting for transfers between devices, on_device(): lax.all_gather(after(down_weight, w_cap), GROUPS, axis=0, tiled=True)  20.1 us
    pallas_call x1, Pallas kernels, self_forward(): pl.pallas_call(self_forward_kernel, grid=(heads, rows // block), in_specs...  19.3 us
  transfers between devices with their start and end apart: 102, of which 40 were waited for; matrix products, arithmetic and copies ran while one was open for 38% of the time, Pallas kernels for 8%

profile of v2, /device:TPU:0, one launch (start us, length us, event | category | flops | bytes accessed | tf_op | source)
XLA Modules:
  0.0 950.5 jit_solution(13453206208066893121)
XLA Ops:
  29.2 11.6 %collective-permute-done.2 = f32[1,9216]{1,0:T(1,128)S(1)} collective-permute-done((f32[1,9216]{1,0:T(1,128)S(1)}, f32[1,9216]{1,0:T(1,128)S(1)}, u32[]{:S(2)}, u32[]{:S(2)}) %collective-permute-start.2) | collective-permute-done | bytes 36896 | tf_op jit(solution)/shard_map/ppermute | solution.py:23
  74.8 17.9 %collective-permute-done.8 = bf16[136,1536]{1,0:T(8,128)(2,1)S(1)} collective-permute-done((bf16[136,1536]{1,0:T(8,128)(2,1)}, bf16[136,1536]{1,0:T(8,128)(2,1)S(1)}, u32[]{:S(2)}, u32[]{:S(2)}) %collective-permute-start.8) | collective-permute-done | bytes 417824 | tf_op jit(solution)/shard_map/ppermute | solution.py:23
  97.5 13.3 %collective-permute-done.26 = bf16[2,2,1,48,1536]{4,3,1,0,2:T(8,128)(2,1)S(1)} collective-permute-done((bf16[2,2,1,48,1536]{4,3,1,0,2:T(8,128)(2,1)S(1)}, bf16[2,2,1,48,1536]{4,3,1,0,2:T(8,128)(2,1)S(1)}, u32[]{:S(2)}, u32[]{:S(2)}) %collective-permute-start.26) | collective-permute-done | bytes 589856 | tf_op jit(solution)/shard_map/ppermute | solution.py:23
  123.5 17.0 %collective-permute-done.27 = bf16[2,2,1,2,48,1536]{5,4,3,1,0,2:T(8,128)(2,1)S(1)} collective-permute-done((bf16[2,2,1,2,48,1536]{5,4,3,1,0,2:T(8,128)(2,1)}, bf16[2,2,1,2,48,1536]{5,4,3,1,0,2:T(8,128)(2,1)S(1)}, u32[]{:S(2)}, u32[]{:S(2)}) %collective-permute-start.27) | collective-permute-done | bytes 1179680 | tf_op jit(solution)/shard_map/ppermute | solution.py:23
  165.8 7.3 add_convert_fusion
  182.6 6.0 convolution_convert_fusion.8
  192.1 5.8 collective-permute-done.14
  197.9 8.3 collective-permute-done.18
  207.9 6.7 collective-permute-done.19
  235.7 19.3 %shard_map.280 = (f32[3,64,2048]{2,1,0:T(8,128)}, f32[3,1,2048]{2,1,0:T(1,128)}) custom-call(bf16[3,64,2048]{2,1,0:T(8,128)(2,1)} %get-tuple-element.180.q_ref, bf16[3,64,2048]{2,1,0:T(8,128)(2,1)} %get-tuple-element.179.k_ref, bf16[3,64,2048]{2,1,0:T(8,128)(2,1)} %bitcast.435), custom_call_target="tpu_custom_call" | custom-call | tf_op jit(solution)/shard_map/pallas_call | solution.py:141
  284.5 10.5 %all-to-all-done.2 = bf16[8,192,256]{2,1,0:T(8,128)(2,1)S(1)} async-done(((bf16[8,192,256]{2,1,0:T(8,128)(2,1)}), bf16[8,192,256]{2,1,0:T(8,128)(2,1)S(1)}, u32[]{:S(2)}, u32[]{:S(2)}) %all-to-all-start.2) | async-done | bytes 786464 | tf_op jit(solution)/shard_map/all_to_all | solution.py:497
  311.7 7.9 collective-permute-done.35
  330.9 27.6 %collective-permute-done.31 = bf16[128,1536]{1,0:T(8,128)(2,1)} collective-permute-done((bf16[128,1536]{1,0:T(8,128)(2,1)}, bf16[128,1536]{1,0:T(8,128)(2,1)}, u32[]{:S(2)}, u32[]{:S(2)}) %collective-permute-start.31) | collective-permute-done | bytes 393248 | tf_op jit(solution)/shard_map/ppermute | solution.py:23
  366.2 22.9 %collective-permute-done.30 = bf16[2,128,1536]{2,1,0:T(8,128)(2,1)S(1)} collective-permute-done((bf16[2,128,1536]{2,1,0:T(8,128)(2,1)S(1)}, bf16[2,128,1536]{2,1,0:T(8,128)(2,1)S(1)}, u32[]{:S(2)}, u32[]{:S(2)}) %collective-permute-start.30) | collective-permute-done | bytes 786464 | tf_op jit(solution)/shard_map/ppermute | solution.py:23
  405.1 8.9 fusion.37
  419.6 20.1 %all-gather.11.cloned.1.call-done = bf16[512,1536]{1,0:T(8,128)(2,1)} async-done(((bf16[128,1536]{1,0:T(8,128)(2,1)}), bf16[512,1536]{1,0:T(8,128)(2,1)}) %all-gather.11.cloned.1.call-update) | async-done | bytes 1572880 | tf_op jit(solution)/shard_map/all_gather | solution.py:441
  439.7 10.8 %multiply_convert_fusion = (bf16[2048,512]{1,0:T(8,128)(2,1)S(1)}, bf16[2048,512]{1,0:T(8,128)(2,1)S(1)}, bf16[2048,512]{1,0:T(8,128)(2,1)S(1)}) fusion(f32[2048,512]{1,0:T(8,128)} %fusion.43, f32[2048,512]{1,0:T(8,128)} %fusion.37, bf16[2048,1536]{1,0:T(8,128)(2,1)} %bitcast.403, bf16[512,1536]{1,0:T(8,128)(2,1)} %all-gather.11.cloned.1.call-done), kind=kOutput, calls=%fused_computation.27 | convolution fusion | flops 3235905536 | bytes 22544384 | tf_op jit(solution)/shard_map/dot_general | solution.py:32
  468.7 7.8 convolution_convert_fusion.5
  489.2 19.6 %collective-permute-done.41 = bf16[256,1536]{1,0:T(8,128)(2,1)S(1)} collective-permute-done((bf16[256,1536]{1,0:T(8,128)(2,1)S(1)}, bf16[256,1536]{1,0:T(8,128)(2,1)S(1)}, u32[]{:S(2)}, u32[]{:S(2)}) %collective-permute-start.41) | collective-permute-done | bytes 786464 | tf_op jit(solution)/shard_map/ppermute | solution.py:23
  510.7 14.8 %collective-permute-done.46 = bf16[256,1536]{1,0:T(8,128)(2,1)S(1)} collective-permute-done((bf16[256,1536]{1,0:T(8,128)(2,1)S(1)}, bf16[256,1536]{1,0:T(8,128)(2,1)S(1)}, u32[]{:S(2)}, u32[]{:S(2)}) %collective-permute-start.46) | collective-permute-done | bytes 786464 | tf_op jit(solution)/shard_map/ppermute | solution.py:23
  552.3 7.0 convolution_convert_fusion.6
  578.6 9.3 shard_map.283
  590.2 38.2 %shard_map.282 = (f32[3,64,2048]{2,1,0:T(8,128)}, f32[3,64,2048]{2,1,0:T(8,128)}, f32[3,64,2048]{2,1,0:T(8,128)}) custom-call(bf16[3,64,2048]{2,1,0:T(8,128)(2,1)} %get-tuple-element.180.q_ref, bf16[3,64,2048]{2,1,0:T(8,128)(2,1)} %reshape_reshape.7.g_ref, f32[3,1,2048]{2,1,0:T(1,128)} %get-tuple-element.43.log_ref, ...), custom_call_target="tpu_custom_call" | custom-call | tf_op jit(solution)/shard_map/pallas_call | solution.py:157
  652.9 8.2 convolution_convert_fusion.3
  681.6 23.8 %collective-permute-done.50 = bf16[128,1536]{1,0:T(8,128)(2,1)} collective-permute-done((bf16[128,1536]{1,0:T(8,128)(2,1)}, bf16[128,1536]{1,0:T(8,128)(2,1)}, u32[]{:S(2)}, u32[]{:S(2)}) %collective-permute-start.50) | collective-permute-done | bytes 393248 | tf_op jit(solution)/shard_map/ppermute | solution.py:23
  722.7 8.2 fusion.142
  747.0 7.1 collective-permute-done.66
  755.5 12.3 %collective-permute-done.64 = bf16[32,4096]{1,0:T(8,128)(2,1)S(1)} collective-permute-done((bf16[32,4096]{1,0:T(8,128)(2,1)S(1)}, bf16[32,4096]{1,0:T(8,128)(2,1)S(1)}, u32[]{:S(2)}, u32[]{:S(2)}) %collective-permute-start.64) | collective-permute-done | bytes 262176 | tf_op jit(solution)/shard_map/ppermute | solution.py:23
  773.1 8.8 collective-permute-done.65
  786.1 9.5 fusion.1
  860.7 13.5 %collective-permute-done.76 = f32[4,1024]{1,0:T(4,128)S(1)} collective-permute-done((f32[4,1024]{1,0:T(4,128)S(1)}, f32[4,1024]{1,0:T(4,128)S(1)}, u32[]{:S(2)}, u32[]{:S(2)}) %collective-permute-start.76) | collective-permute-done | bytes 16416 | tf_op jit(solution)/shard_map/ppermute | solution.py:23
  919.6 18.5 %collective-permute-done.59 = bf16[128,1536]{1,0:T(8,128)(2,1)S(1)} collective-permute-done((bf16[128,1536]{1,0:T(8,128)(2,1)S(1)}, bf16[128,1536]{1,0:T(8,128)(2,1)S(1)}, u32[]{:S(2)}, u32[]{:S(2)}) %collective-permute-start.59) | collective-permute-done | bytes 393248 | tf_op jit(solution)/shard_map/ppermute | solution.py:23
  (787 shorter events, 504.8 us)
Async XLA Ops:
  14.4 56.2 %collective-permute-start = (bf16[136,1536]{1,0:T(8,128)(2,1)}, bf16[136,1536]{1,0:T(8,128)(2,1)}, u32[]{:S(2)}, u32[]{:S(2)}) collective-permute-start(bf16[136,1536]{1,0:T(8,128)(2,1)} %get-tuple-element.215), channel_id=1, source_target_pairs={{0,8},{8,0},{1,9},{9,1},{2,10},{10,2},{3,11},{11,3},{4,12},{12,4},... | collective-permute-start | bytes 1253384 | tf_op jit(solution)/shard_map/ppermute | solution.py:23
  17.0 50.5 %collective-permute-start.6 = (bf16[136,1536]{1,0:T(8,128)(2,1)S(1)}, bf16[136,1536]{1,0:T(8,128)(2,1)}, u32[]{:S(2)}, u32[]{:S(2)}) collective-permute-start(bf16[136,1536]{1,0:T(8,128)(2,1)S(1)} %bitcast.444), channel_id=1, source_target_pairs={{0,4},{4,0},{1,5},{5,1},{2,6},{6,2},{3,7},{7,3},{8,12},{12,8},{9,1... | collective-permute-start | bytes 1253384 | tf_op jit(solution)/shard_map/ppermute | solution.py:23
  21.9 40.4 %all-to-all-start = ((bf16[8,48,576]{2,1,0:T(8,128)(2,1)}), bf16[8,48,576]{2,1,0:T(8,128)(2,1)S(1)}, u32[]{:S(2)}, u32[]{:S(2)}) async-start(bf16[8,48,576]{2,1,0:T(8,128)(2,1)} %copy.277), calls=%async_computation | async-start | bytes 983040 | tf_op jit(solution)/shard_map/all_to_all | solution.py:393
  62.3 57.4 %all-to-all-start.1 = ((bf16[8,128,384]{1,2,0:T(8,128)(2,1)}), bf16[8,128,384]{1,2,0:T(8,128)(2,1)}, u32[]{:S(2)}, u32[]{:S(2)}) async-start(bf16[8,128,384]{1,2,0:T(8,128)(2,1)} %maximum_bitcast_fusion.4), calls=%async_computation.1 | async-start | bytes 1572864 | tf_op jit(solution)/shard_map/all_to_all | solution.py:393
  66.5 106.6 %all-gather.5.cloned.1.call-start = ((), (), s32[]{:S(2)}) async-start(), calls=%async_computation.12 | async-start | bytes 2457600 | tf_op jit(solution)/shard_map/all_gather | solution.py:395
  67.2 152.4 %all-gather.7.cloned.1.call-start = ((), (), s32[]{:S(2)}) async-start(), calls=%async_computation.13 | async-start | bytes 3932160 | tf_op jit(solution)/shard_map/all_gather | solution.py:395
  74.1 36.7 %collective-permute-start.26 = (bf16[2,2,1,48,1536]{4,3,1,0,2:T(8,128)(2,1)S(1)}, bf16[2,2,1,48,1536]{4,3,1,0,2:T(8,128)(2,1)S(1)}, u32[]{:S(2)}, u32[]{:S(2)}) collective-permute-start(bf16[2,2,1,48,1536]{4,3,1,0,2:T(8,128)(2,1)S(1)} %maximum_select_fusion.7), channel_id=1, source_target_pairs={{0,4},{4,0},{1,5},{5,1},{2,6},{6,2},{3,7},{7,3},{8,12},{12,8},{9,1... | collective-permute-start | bytes 1769480 | tf_op jit(solution)/shard_map/ppermute | solution.py:23
  114.3 33.0 %collective-permute-start.10 = (bf16[2,2,136,1536]{3,2,0,1:T(8,128)(2,1)}, bf16[2,2,136,1536]{3,2,0,1:T(8,128)(2,1)}, u32[]{:S(2)}, u32[]{:S(2)}) collective-permute-start(bf16[2,2,136,1536]{3,2,0,1:T(8,128)(2,1)} %pad_maximum_fusion.13), channel_id=1, source_target_pairs={{0,1},{1,0},{2,3},{3,2},{4,5},{5,4},{6,7},{7,6},{8,9},{9,8},{10,11... | collective-permute-start | bytes 5013512 | tf_op jit(solution)/shard_map/ppermute | solution.py:23
  117.2 32.6 %collective-permute-start.11 = (bf16[2,2,136,1536]{3,2,0,1:T(8,128)(2,1)}, bf16[2,2,136,1536]{3,2,0,1:T(8,128)(2,1)}, u32[]{:S(2)}, u32[]{:S(2)}) collective-permute-start(bf16[2,2,136,1536]{3,2,0,1:T(8,128)(2,1)} %pad_maximum_fusion.14), channel_id=1, source_target_pairs={{0,1},{1,0},{2,3},{3,2},{4,5},{5,4},{6,7},{7,6},{8,9},{9,8},{10,11... | collective-permute-start | bytes 5013512 | tf_op jit(solution)/shard_map/ppermute | solution.py:23
  144.1 134.3 %collective-permute-start.28 = (bf16[2,2,1,2,2,48,1536]{6,5,3,1,0,4,2:T(8,128)(2,1)}, bf16[2,2,1,2,2,48,1536]{6,5,3,1,0,4,2:T(8,128)(2,1)}, u32[]{:S(2)}, u32[]{:S(2)}) collective-permute-start(bf16[2,2,1,2,2,48,1536]{6,5,3,1,0,4,2:T(8,128)(2,1)} %maximum_select_fusion.1), channel_id=1, source_target_pairs={{0,1},{1,0},{2,3},{3,2},{4,5},{5,4},{6,7},{7,6},{8,9},{9,8},{10,11... | collective-permute-start | bytes 7077896 | tf_op jit(solution)/shard_map/ppermute | solution.py:23
  295.0 30.0 %all-to-all-start.3 = ((bf16[8,48,1024]{2,1,0:T(8,128)(2,1)}), bf16[8,48,1024]{2,1,0:T(8,128)(2,1)}, u32[]{:S(2)}, u32[]{:S(2)}) async-start(bf16[8,48,1024]{2,1,0:T(8,128)(2,1)} %maximum_bitcast_fusion.5), calls=%async_computation.3 | async-start | bytes 1572864 | tf_op jit(solution)/shard_map/all_to_all | solution.py:393
  299.2 105.9 %all-gather.9.cloned.1.call-start = ((), (), s32[]{:S(2)}) async-start(), calls=%async_computation.14 | async-start | bytes 3932160 | tf_op jit(solution)/shard_map/all_gather | solution.py:395
  320.8 39.8 %collective-permute-start.36 = (bf16[2,128,1536]{2,1,0:T(8,128)(2,1)}, bf16[2,128,1536]{2,1,0:T(8,128)(2,1)}, u32[]{:S(2)}, u32[]{:S(2)}) collective-permute-start(bf16[2,128,1536]{2,1,0:T(8,128)(2,1)} %get-tuple-element.220), channel_id=1, source_target_pairs={{0,4},{4,0},{1,5},{5,1},{2,6},{6,2},{3,7},{7,3},{8,12},{12,8},{9,1... | collective-permute-start | bytes 2359304 | tf_op jit(solution)/shard_map/ppermute | solution.py:23
  322.3 36.2 %collective-permute-start.31 = (bf16[128,1536]{1,0:T(8,128)(2,1)}, bf16[128,1536]{1,0:T(8,128)(2,1)}, u32[]{:S(2)}, u32[]{:S(2)}) collective-permute-start(bf16[128,1536]{1,0:T(8,128)(2,1)} %get-tuple-element.235), channel_id=1, source_target_pairs={{0,4},{4,0},{1,5},{5,1},{2,6},{6,2},{3,7},{7,3},{8,12},{12,8},{9,1... | collective-permute-start | bytes 1179656 | tf_op jit(solution)/shard_map/ppermute | solution.py:23
  324.1 37.8 %collective-permute-start.38 = (bf16[2,128,1536]{2,1,0:T(8,128)(2,1)}, bf16[2,128,1536]{2,1,0:T(8,128)(2,1)}, u32[]{:S(2)}, u32[]{:S(2)}) collective-permute-start(bf16[2,128,1536]{2,1,0:T(8,128)(2,1)} %get-tuple-element.226), channel_id=1, source_target_pairs={{0,2},{2,0},{1,3},{3,1},{4,6},{6,4},{5,7},{7,5},{8,10},{10,8},{9,1... | collective-permute-start | bytes 2359304 | tf_op jit(solution)/shard_map/ppermute | solution.py:23
  325.0 114.7 %all-gather.11.cloned.1.call-start = ((), (), s32[]{:S(2)}) async-start(), calls=%async_computation.15 | async-start | bytes 1966080 | tf_op jit(solution)/shard_map/all_gather | solution.py:441
  329.4 59.8 %collective-permute-start.30 = (bf16[2,128,1536]{2,1,0:T(8,128)(2,1)S(1)}, bf16[2,128,1536]{2,1,0:T(8,128)(2,1)S(1)}, u32[]{:S(2)}, u32[]{:S(2)}) collective-permute-start(bf16[2,128,1536]{2,1,0:T(8,128)(2,1)S(1)} %get-tuple-element.232), channel_id=1, source_target_pairs={{0,4},{4,0},{1,5},{5,1},{2,6},{6,2},{3,7},{7,3},{8,12},{12,8},{9,1... | collective-permute-start | bytes 2359304 | tf_op jit(solution)/shard_map/ppermute | solution.py:23
  359.6 29.7 %collective-permute-start.32 = (bf16[2,128,1536]{2,1,0:T(8,128)(2,1)S(1)}, bf16[2,128,1536]{2,1,0:T(8,128)(2,1)S(1)}, u32[]{:S(2)}, u32[]{:S(2)}) collective-permute-start(bf16[2,128,1536]{2,1,0:T(8,128)(2,1)S(1)} %get-tuple-element.238), channel_id=1, source_target_pairs={{0,2},{2,0},{1,3},{3,1},{4,6},{6,4},{5,7},{7,5},{8,10},{10,8},{9,1... | collective-permute-start | bytes 2359304 | tf_op jit(solution)/shard_map/ppermute | solution.py:23
  392.6 251.4 %reduce-scatter.11.cloned.1.call-start = ((), (), s32[]{:S(2)}) async-start(), calls=%async_computation.17 | async-start | bytes 1966080 | tf_op jit(solution)/shard_map/reduce_scatter | solution.py:542
  488.4 37.2 %collective-permute-start.46 = (bf16[256,1536]{1,0:T(8,128)(2,1)S(1)}, bf16[256,1536]{1,0:T(8,128)(2,1)S(1)}, u32[]{:S(2)}, u32[]{:S(2)}) collective-permute-start(bf16[256,1536]{1,0:T(8,128)(2,1)S(1)} %slice.761), channel_id=1, source_target_pairs={{0,4},{4,0},{1,5},{5,1},{2,6},{6,2},{3,7},{7,3},{8,12},{12,8},{9,1... | collective-permute-start | bytes 2359304 | tf_op jit(solution)/shard_map/ppermute | solution.py:23
  488.5 38.7 %collective-permute-start.48 = (bf16[2,128,1536]{2,1,0:T(8,128)(2,1)S(1)}, bf16[2,128,1536]{2,1,0:T(8,128)(2,1)S(1)}, u32[]{:S(2)}, u32[]{:S(2)}) collective-permute-start(bf16[2,128,1536]{2,1,0:T(8,128)(2,1)S(1)} %fusion.66), channel_id=1, source_target_pairs={{0,2},{2,0},{1,3},{3,1},{4,6},{6,4},{5,7},{7,5},{8,10},{10,8},{9,1... | collective-permute-start | bytes 2359304 | tf_op jit(solution)/shard_map/ppermute | solution.py:23
  552.2 179.5 %reduce-scatter.15.cloned.1.call-start = ((), (), s32[]{:S(2)}) async-start(), calls=%async_computation.19 | async-start | bytes 3932160 | tf_op jit(solution)/shard_map/reduce_scatter | solution.py:537
  565.8 318.4 %reduce-scatter.13.cloned.1.call-start = ((), (), s32[]{:S(2)}) async-start(), calls=%async_computation.18 | async-start | bytes 2457600 | tf_op jit(solution)/shard_map/reduce_scatter | solution.py:537
  665.1 244.0 %reduce-scatter.9.cloned.1.call-start = ((), (), s32[]{:S(2)}) async-start(), calls=%async_computation.16 | async-start | bytes 3932160 | tf_op jit(solution)/shard_map/reduce_scatter | solution.py:537
  667.1 38.3 %collective-permute-start.50 = (bf16[128,1536]{1,0:T(8,128)(2,1)}, bf16[128,1536]{1,0:T(8,128)(2,1)}, u32[]{:S(2)}, u32[]{:S(2)}) collective-permute-start(bf16[128,1536]{1,0:T(8,128)(2,1)} %get-tuple-element.230), channel_id=1, source_target_pairs={{0,8},{8,0},{1,9},{9,1},{2,10},{10,2},{3,11},{11,3},{4,12},{12,4},... | collective-permute-start | bytes 1179656 | tf_op jit(solution)/shard_map/ppermute | solution.py:23
  679.0 57.1 %collective-permute-start.81 = (bf16[2,2,1,2,2,48,1536]{6,5,4,3,1,0,2:T(8,128)(2,1)}, bf16[2,2,1,2,2,48,1536]{6,5,4,3,1,0,2:T(8,128)(2,1)}, u32[]{:S(2)}, u32[]{:S(2)}) collective-permute-start(bf16[2,2,1,2,2,48,1536]{6,5,4,3,1,0,2:T(8,128)(2,1)} %fusion.10), channel_id=1, source_target_pairs={{0,1},{1,0},{2,3},{3,2},{4,5},{5,4},{6,7},{7,6},{8,9},{9,8},{10,11... | collective-permute-start | bytes 7077896 | tf_op jit(solution)/shard_map/ppermute | solution.py:23
  730.9 55.1 %collective-permute-start.54 = (bf16[1024,1536]{1,0:T(8,128)(2,1)}, bf16[1024,1536]{1,0:T(8,128)(2,1)}, u32[]{:S(2)}, u32[]{:S(2)}) collective-permute-start(bf16[1024,1536]{1,0:T(8,128)(2,1)} %get-tuple-element.275), channel_id=1, source_target_pairs={{0,1},{1,0},{2,3},{3,2},{4,5},{5,4},{6,7},{7,6},{8,9},{9,8},{10,11... | collective-permute-start | bytes 9437192 | tf_op jit(solution)/shard_map/ppermute | solution.py:23
  731.7 80.7 %all-to-all-start.7 = ((bf16[8,48,1024]{2,1,0:T(8,128)(2,1)}), bf16[8,48,1024]{2,1,0:T(8,128)(2,1)}, u32[]{:S(2)}, u32[]{:S(2)}) async-start(bf16[8,48,1024]{2,1,0:T(8,128)(2,1)} %bitcast.456), calls=%async_computation.8 | async-start | bytes 1572864 | tf_op jit(solution)/shard_map/all_to_all | solution.py:539
  744.8 38.1 %collective-permute-start.82 = (bf16[2,2,1,2,48,1536]{5,4,3,1,0,2:T(8,128)(2,1)S(1)}, bf16[2,2,1,2,48,1536]{5,4,3,1,0,2:T(8,128)(2,1)S(1)}, u32[]{:S(2)}, u32[]{:S(2)}) collective-permute-start(bf16[2,2,1,2,48,1536]{5,4,3,1,0,2:T(8,128)(2,1)S(1)} %fusion.45), channel_id=1, source_target_pairs={{0,2},{2,0},{1,3},{3,1},{4,6},{6,4},{5,7},{7,5},{8,10},{10,8},{9,1... | collective-permute-start | bytes 3538952 | tf_op jit(solution)/shard_map/ppermute | solution.py:23
  784.7 42.3 %collective-permute-start.83 = (bf16[2,2,1,48,1536]{4,3,1,0,2:T(8,128)(2,1)S(1)}, bf16[2,2,1,48,1536]{4,3,1,0,2:T(8,128)(2,1)}, u32[]{:S(2)}, u32[]{:S(2)}) collective-permute-start(bf16[2,2,1,48,1536]{4,3,1,0,2:T(8,128)(2,1)S(1)} %fusion.74), channel_id=1, source_target_pairs={{0,4},{4,0},{1,5},{5,1},{2,6},{6,2},{3,7},{7,3},{8,12},{12,8},{9,1... | collective-permute-start | bytes 1769480 | tf_op jit(solution)/shard_map/ppermute | solution.py:23
  853.9 34.1 %collective-permute-start.55 = (bf16[256,1536]{1,0:T(8,128)(2,1)S(1)}, bf16[256,1536]{1,0:T(8,128)(2,1)}, u32[]{:S(2)}, u32[]{:S(2)}) collective-permute-start(bf16[256,1536]{1,0:T(8,128)(2,1)S(1)} %slice.760), channel_id=1, source_target_pairs={{0,4},{4,0},{1,5},{5,1},{2,6},{6,2},{3,7},{7,3},{8,12},{12,8},{9,1... | collective-permute-start | bytes 2359304 | tf_op jit(solution)/shard_map/ppermute | solution.py:23
  859.5 33.3 %collective-permute-start.57 = (bf16[2,128,1536]{2,1,0:T(8,128)(2,1)}, bf16[2,128,1536]{2,1,0:T(8,128)(2,1)}, u32[]{:S(2)}, u32[]{:S(2)}) collective-permute-start(bf16[2,128,1536]{2,1,0:T(8,128)(2,1)} %fusion.67), channel_id=1, source_target_pairs={{0,2},{2,0},{1,3},{3,1},{4,6},{6,4},{5,7},{7,5},{8,10},{10,8},{9,1... | collective-permute-start | bytes 2359304 | tf_op jit(solution)/shard_map/ppermute | solution.py:23
  (202 other events, 2956.1 us)
Sparse Core Ops, SparseCore 0:
  69.8 50.8 all-gather.4
  123.0 74.8 all-gather.6
  325.1 69.3 all-gather.8
  396.2 43.4 all-gather.10
  465.1 42.0 reduce-scatter.10
  565.9 69.2 reduce-scatter.14
  665.2 61.4 reduce-scatter.12
  729.7 68.9 reduce-scatter.8

commit v3 on v2

v3 whole, which is shorter than its diff:
```python
import jax
import jax.numpy as jnp
from jax import lax
from jax.experimental import pallas as pl
from jax.experimental.pallas import tpu as pltpu
from jax.sharding import Mesh
from jax.sharding import PartitionSpec as P

EPSILON = 1e-06
NEGATIVE = -1e30
BF = jnp.bfloat16
F32 = jnp.float32
SEQ = ("half", "rep", "tz", "ty", "tc")
GROUPS = ("clip", "half", "rep")
TEAM = ("tc", "tz", "ty")
SHARDS = ("tz", "ty", "tc")
EVERY = ("clip",) + SEQ
KERNEL = pltpu.CompilerParams(
    vmem_limit_bytes=56 * 1024 * 1024, dimension_semantics=("arbitrary", "arbitrary")
)


def swap(block, axis):
    return lax.ppermute(block, axis, [(0, 1), (1, 0)])


def together(*values):
    return lax.optimization_barrier(values)


def after(value, *others):
    return lax.optimization_barrier((value,) + others)[0]


def dot(left, right, left_dim, right_dim):
    dims = (((left_dim,), (right_dim,)), ((), ()))
    return lax.dot_general(left, right, dims, preferred_element_type=F32)


def join(parts, axis=0):
    return jnp.concatenate(parts, axis=axis)


def upright(block):
    return jnp.transpose(block.astype(F32)).astype(BF)


def self_forward_kernel(q_ref, k_ref, v_ref, o_ref, log_ref, k_rows):
    @pl.when(pl.program_id(1) == 0)
    def _():
        k_rows[...] = upright(k_ref[0])

    scores = dot(k_rows[...], q_ref[0], 1, 0)
    peak = jnp.max(scores, axis=0, keepdims=True)
    weights = jnp.exp(scores - peak)
    total = jnp.sum(weights, axis=0, keepdims=True)
    o_ref[0] = dot(v_ref[0], weights.astype(BF), 1, 0) / total
    log_ref[0] = peak + jnp.log(total)


def self_backward_kernel(
    q_ref, g_ref, log_ref, delta_ref, k_ref, v_ref, dq_ref, dk_ref, dv_ref, k_rows, v_rows, dk, dv
):
    step = pl.program_id(1)

    @pl.when(step == 0)
    def _():
        k_rows[...] = upright(k_ref[0])
        v_rows[...] = upright(v_ref[0])
        dk[...] = jnp.zeros_like(dk)
        dv[...] = jnp.zeros_like(dv)

    q, g = q_ref[0], g_ref[0]
    probs = jnp.exp(dot(k_rows[...], q, 1, 0) - log_ref[0])
    ds = (probs * (dot(v_rows[...], g, 1, 0) - delta_ref[0])).astype(BF)
    dv[...] += dot(probs.astype(BF), g, 1, 1)
    dk[...] += dot(ds, q, 1, 1)
    dq_ref[0] = dot(k_ref[0], ds, 1, 0)

    @pl.when(step == pl.num_programs(1) - 1)
    def _():
        dk_ref[0] = jnp.transpose(dk[...])
        dv_ref[0] = jnp.transpose(dv[...])


def cross_forward_kernel(q_ref, k_ref, v_ref, mask_ref, o_ref):
    scores = dot(upright(k_ref[0]), q_ref[0], 1, 0) + mask_ref[...]
    weights = jnp.exp(scores - jnp.max(scores, axis=0, keepdims=True))
    total = jnp.sum(weights, axis=0, keepdims=True)
    o_ref[0] = dot(v_ref[0], weights.astype(BF), 1, 0) / total


def cross_backward_kernel(
    q_ref, g_ref, k_ref, v_ref, mask_ref, gate_ref, dq_ref, dk_ref, dv_ref, dg_ref
):
    q, g, gate = q_ref[0], g_ref[0], gate_ref[0, 0:1, 0:1]
    scores = dot(upright(k_ref[0]), q, 1, 0) + mask_ref[...]
    weights = jnp.exp(scores - jnp.max(scores, axis=0, keepdims=True))
    probs = weights / jnp.sum(weights, axis=0, keepdims=True)
    dp = dot(upright(v_ref[0]), g, 1, 0)
    inner = jnp.sum(probs * dp, axis=0, keepdims=True)
    ds = (probs * (gate * (dp - inner))).astype(BF)
    dg_ref[0] = inner
    dq_ref[0] = dot(k_ref[0], ds, 1, 0)
    dk = dot(q, ds, 1, 1)
    dv = dot(g, probs.astype(BF), 1, 1) * gate

    @pl.when(pl.program_id(1) == 0)
    def _():
        dk_ref[0] = dk
        dv_ref[0] = dv

    @pl.when(pl.program_id(1) > 0)
    def _():
        dk_ref[0] += dk
        dv_ref[0] += dv


def place_weight_kernel(bit_ref, mine_ref, other_ref, scale_ref, shift_ref, w_ref, scaled_ref, bias_ref):
    step = pl.program_id(0)

    def run(ref):
        values = ref[...].astype(F32)
        w_ref[...] = ref[...]
        scaled_ref[...] = (values * scale_ref[...]).astype(BF)
        bias = jnp.sum(values * shift_ref[...], axis=0, keepdims=True)

        @pl.when(step == 0)
        def _():
            bias_ref[...] = bias

        @pl.when(step > 0)
        def _():
            bias_ref[...] += bias

    @pl.when(step == bit_ref[0])
    def _():
        run(mine_ref)

    @pl.when(step != bit_ref[0])
    def _():
        run(other_ref)


def place_weight(bit, mine, other, scale, shift):
    rows, columns = mine.shape
    part = pl.BlockSpec((rows, columns), lambda i: (0, 0))
    out = pl.BlockSpec((rows, columns), lambda i: (i, 0))
    column = pl.BlockSpec((rows, 1), lambda i: (i, 0))
    return pl.pallas_call(
        place_weight_kernel,
        grid=(2,),
        in_specs=[pl.BlockSpec(memory_space=pltpu.SMEM), part, part, column, column],
        out_specs=[out, out, pl.BlockSpec((1, columns), lambda i: (0, 0))],
        out_shape=[
            jax.ShapeDtypeStruct((2 * rows, columns), BF),
            jax.ShapeDtypeStruct((2 * rows, columns), BF),
            f32(1, columns),
        ],
        compiler_params=pltpu.CompilerParams(vmem_limit_bytes=48 * 1024 * 1024),
    )(jnp.reshape(bit, (1,)).astype(jnp.int32), mine, other, scale, shift)


def norm_rows_kernel(rows_ref, core_ref, places_ref):
    rows = core_ref.shape[0] // 2
    for part in (0, 1):
        start = part * (rows + 8)
        values = rows_ref[start : start + rows].astype(F32)
        square = jnp.mean(values * values, axis=-1, keepdims=True)
        core_ref[part * rows : (part + 1) * rows] = (values * lax.rsqrt(square + EPSILON)).astype(BF)
        places_ref[0, part] = rows_ref[start + rows : start + rows + 8, :rows].astype(F32)


def norm_rows(blocks, rows):
    width = blocks.shape[1]
    pair = 2 * (rows + 8)
    count = blocks.shape[0] // pair
    return pl.pallas_call(
        norm_rows_kernel,
        grid=(count,),
        in_specs=[pl.BlockSpec((pair, width), lambda i: (i, 0))],
        out_specs=[
            pl.BlockSpec((2 * rows, width), lambda i: (i, 0)),
            pl.BlockSpec((1, 2, 8, rows), lambda i: (i, 0, 0, 0)),
        ],
        out_shape=[
            jax.ShapeDtypeStruct((2 * count * rows, width), BF),
            f32(count, 2, 8, rows),
        ],
        compiler_params=pltpu.CompilerParams(vmem_limit_bytes=32 * 1024 * 1024),
    )(blocks)


def by_query(rows, block, first=0):
    return pl.BlockSpec((1, rows, block), lambda h, i: (h + first, 0, i))


def whole_head(rows, columns, first=0):
    return pl.BlockSpec((1, rows, columns), lambda h, i: (h + first, 0, 0))


def mask_spec(rows):
    return pl.BlockSpec((rows, 1), lambda h, i: (0, 0))


def f32(*shape):
    return jax.ShapeDtypeStruct(shape, F32)


def query_block(rows, keys, most):
    block = rows
    while block > 128 and block * keys > most:
        block //= 2
    return block


def attention_cost(scores, products, heads=1):
    return pl.CostEstimate(
        flops=heads * scores * products * 2 * 256,
        transcendentals=heads * scores,
        bytes_accessed=heads * scores // 2,
    )


def one_head(kernel, head, kept, inputs, in_specs, out_specs, out_shape, scratch, steps, cost):
    extra = len(kept) if kept else 0

    def body(*refs):
        kernel(*refs[: len(inputs)], *refs[len(inputs) + extra :])

    return pl.pallas_call(
        body,
        grid=(1, steps),
        in_specs=in_specs + [pl.BlockSpec(memory_space=pl.ANY)] * extra,
        out_specs=out_specs,
        out_shape=out_shape,
        scratch_shapes=scratch,
        input_output_aliases={len(inputs) + i: i for i in range(extra)},
        compiler_params=KERNEL,
        cost_estimate=cost,
    )(*inputs, *(kept or ()))


def self_forward(q, k, v, head, kept):
    heads, dim, rows = q.shape
    keys = k.shape[2]
    block = query_block(rows, keys, 1 << 21)
    return one_head(
        self_forward_kernel,
        head,
        kept,
        (q, k, v),
        [by_query(dim, block, head), whole_head(dim, keys, head), whole_head(dim, keys, head)],
        [by_query(dim, block, head), by_query(1, block, head)],
        [f32(heads, dim, rows), f32(heads, 1, rows)],
        [pltpu.VMEM((keys, dim), BF)],
        rows // block,
        attention_cost(rows * keys, 2),
    )


def self_backward(q, g, log_total, delta, k, v, head, kept):
    heads, dim, rows = q.shape
    keys = k.shape[2]
    block = query_block(rows, keys, 1 << 20)
    return one_head(
        self_backward_kernel,
        head,
        kept,
        (q, g, log_total, delta, k, v),
        [by_query(dim, block, head)] * 2
        + [by_query(1, block, head)] * 2
        + [whole_head(dim, keys, head)] * 2,
        [by_query(dim, block, head), whole_head(dim, keys, head), whole_head(dim, keys, head)],
        [f32(heads, dim, rows), f32(heads, dim, keys), f32(heads, dim, keys)],
        [pltpu.VMEM((keys, dim), t) for t in (BF, BF, F32, F32)],
        rows // block,
        attention_cost(rows * keys, 5),
    )


def cross_forward(q, k, v, mask):
    heads, dim, rows = q.shape
    keys = k.shape[2]
    block = query_block(rows, keys, 1 << 19)
    return pl.pallas_call(
        cross_forward_kernel,
        grid=(heads, rows // block),
        in_specs=[
            by_query(dim, block),
            whole_head(dim, keys),
            whole_head(dim, keys),
            mask_spec(keys),
        ],
        out_specs=by_query(dim, block),
        out_shape=f32(heads, dim, rows),
        compiler_params=KERNEL,
        cost_estimate=attention_cost(rows * keys, 2, heads),
    )(q, k, v, mask)


def cross_backward(q, g, k, v, mask, gate):
    heads, dim, rows = q.shape
    keys = k.shape[2]
    block = query_block(rows, keys, 1 << 19)
    return pl.pallas_call(
        cross_backward_kernel,
        grid=(heads, rows // block),
        in_specs=[
            by_query(dim, block),
            by_query(dim, block),
            whole_head(dim, keys),
            whole_head(dim, keys),
            mask_spec(keys),
            whole_head(8, 128),
        ],
        out_specs=[
            by_query(dim, block),
            whole_head(dim, keys),
            whole_head(dim, keys),
            by_query(1, block),
        ],
        out_shape=[
            f32(heads, dim, rows),
            f32(heads, dim, keys),
            f32(heads, dim, keys),
            f32(heads, 1, rows),
        ],
        compiler_params=KERNEL,
        cost_estimate=attention_cost(rows * keys, 5, heads),
    )(q, g, k, v, mask, gate)


def halves(block):
    half = block.shape[0] // 2
    return block[:half], block[half:]


def pick(block, index, dim=0, keep=False):
    return lax.dynamic_index_in_dim(block, index, dim, keepdims=keep)


def both_sides(block, axis, bit, dim):
    other = swap(block, axis)
    return jnp.where(bit == 0, jnp.stack([block, other], dim), jnp.stack([other, block], dim))


def kept_sum(block, axis, bit, dim):
    other = swap(pick(block, 1 - bit, dim).astype(BF), axis)
    return pick(block, bit, dim).astype(F32) + other.astype(F32)


def team_sum(values):
    for axis in TEAM:
        values = values + swap(values, axis)
    return values


def chips_first(first, second, bits):
    return kept_sum(first, "tz", bits[0], 0), kept_sum(second, "ty", bits[1], 1)


def chips_last(first, second, bits):
    return kept_sum(first, "ty", bits[1], 0), kept_sum(second, "tz", bits[0], 0)


def row_factor(values):
    return lax.rsqrt(jnp.mean(values * values, axis=-1, keepdims=True) + EPSILON)


def rope_tables(places, head_dim):
    pair_count = head_dim // 2
    lead_pairs = pair_count // 4
    mid_pairs = (pair_count - lead_pairs) // 2
    last_pairs = pair_count - lead_pairs - mid_pairs
    angles = []
    for which, extent in enumerate((lead_pairs, mid_pairs, last_pairs)):
        offsets = jnp.arange(extent, dtype=F32)
        angles.append(jnp.power(10000.0, -offsets / extent)[:, None] * places[which][None])
    angles = join(angles)
    cosine, sine = jnp.cos(angles), jnp.sin(angles)
    return join([cosine, cosine]), join([-sine, sine])


def turn(vectors, cosine, sine):
    half = vectors.shape[1] // 2
    crossed = join([vectors[:, half:], vectors[:, :half]], axis=1)
    return vectors * cosine + crossed * sine


def on_device(
    tokens,
    condition,
    caption,
    caption_lengths,
    positions,
    modulation_weight,
    modulation_bias,
    norm_gains,
    cross_gate,
    input_weight,
    output_weight,
    caption_key_weight,
    caption_value_weight,
    gate_weight,
    up_weight,
    down_weight,
    cotangent,
):
    clips_here, clip_rows, width = tokens.shape
    head_count = cross_gate.shape[0]
    head_dim = width // head_count
    scale = head_dim ** (-0.5)
    team = 8
    heads = head_count // team
    rows_in = input_weight.shape[0]
    part = heads * head_dim
    groups = lax.axis_size(GROUPS)
    reps = lax.axis_size("rep")
    half = lax.axis_index("half")
    bits = tuple(lax.axis_index(axis) for axis in SHARDS)
    rank = lax.axis_index(TEAM)
    clip_pair = lax.axis_index("clip")
    device = lax.axis_index(EVERY)

    def own_clip(block):
        return pick(block, half), swap(pick(block, 1 - half), "half")

    def back_clip(block):
        rows = block.shape[0] // 2
        kept, other = block[:rows], block[rows:]
        other = swap(other.astype(BF), "half").astype(block.dtype)
        return jnp.where(half == 0, jnp.stack([kept, other]), jnp.stack([other, kept]))

    def own_columns(table):
        return lax.dynamic_slice_in_dim(table, rank * part, part, table.ndim - 1)

    def by_rank(weight, split, by_shard=False):
        rows = weight.shape[0]
        if by_shard:
            tiled = weight.reshape(rows, split, team, -1)
            return jnp.transpose(tiled, (2, 0, 1, 3)).reshape(team, rows, -1)
        tiled = weight.reshape(rows, split, 2, 2, 2, -1)
        return jnp.transpose(tiled, (3, 4, 2, 0, 1, 5)).reshape(team, rows, -1)

    def from_team(blocks):
        mine = lax.all_to_all(blocks, SHARDS, split_axis=0, concat_axis=0, tiled=True)
        return mine.reshape(-1, blocks.shape[2])

    def all_reps(block):
        return lax.all_gather(block, "rep", axis=0, tiled=True) if reps > 1 else block

    def across_half(block):
        return both_sides(all_reps(block), "half", half, 0)

    def across_clip(block):
        return both_sides(block, "clip", clip_pair, 0).reshape(-1, block.shape[-1])

    places = jnp.pad(
        jnp.transpose(positions, (1, 0, 2)).astype(BF),
        ((0, 0), (0, 5), (0, width - clip_rows)),
    )
    rows_a, rows_b = own_clip(join([tokens, places], axis=1))
    in_team = from_team(by_rank(input_weight, 3))
    shard_rows = modulation_weight.shape[0]
    silu_all = jax.nn.silu(condition).astype(BF)
    silu_rows = lax.dynamic_slice_in_dim(silu_all, device * shard_rows, shard_rows, 1)
    mod_part = dot(silu_rows, modulation_weight, 1, 0)
    mod_part = mod_part.reshape(lax.axis_size("clip"), clips_here, -1)
    mod_pair = pick(mod_part, clip_pair) + swap(pick(mod_part, 1 - clip_pair), "clip")
    mod_own = pick(mod_pair, half, keep=True) + swap(pick(mod_pair, 1 - half, keep=True), "half")
    rows_a, rows_b, mod_own, in_team = together(rows_a, rows_b, mod_own, in_team)

    rows_all = lax.all_gather(join([rows_a, rows_b]), TEAM, axis=0, tiled=True)
    in_half = across_half(in_team).reshape(-1, 3 * part)
    if reps > 1:
        mod_own = lax.psum(mod_own, "rep")
    mod_own = team_sum(mod_own)
    in_half, mod_own, caption = together(in_half, mod_own, caption)

    in_other = swap(in_half, "clip")
    rows_cap = caption_key_weight.shape[0]
    slots_here = caption.shape[1]
    cap_a, cap_b = own_clip(caption)
    modulation = mod_own + modulation_bias
    shift_attn, scale_attn, gate_attn, shift_ffn, scale_ffn, gate_ffn = (
        modulation[:, i * width : (i + 1) * width] for i in range(6)
    )
    token_vals = join([rows_a[:clip_rows], rows_b[:clip_rows]]).astype(F32)
    rows_here = token_vals.shape[0]
    team_rows = team * rows_here
    row_scale = (norm_gains[0] * (1.0 + scale_attn)).reshape(width, 1)
    row_shift = shift_attn.reshape(width, 1)
    w_in, w_scaled, bias = place_weight(clip_pair, in_half, in_other, row_scale, row_shift)
    bias = bias.reshape(3 * part, 1)
    w_scaled, bias, rows_all, cap_a, cap_b, out_shard, ckey_weight, cvalue_weight = together(
        w_scaled,
        bias,
        rows_all,
        cap_a,
        cap_b,
        output_weight,
        caption_key_weight,
        caption_value_weight,
    )
    cap_team = from_team(join([by_rank(ckey_weight, 1), by_rank(cvalue_weight, 1)], axis=2))
    w_out = both_sides(out_shard, "half", half, 0)
    cap_rows = jnp.where(half == 0, join([cap_a, cap_b]), join([cap_b, cap_a]))
    core_all, all_places = norm_rows(rows_all, clip_rows)
    all_places = jnp.transpose(all_places[:, :, :3], (2, 0, 1, 3)).reshape(3, team_rows)

    def by_head(block):
        return block.reshape(heads, head_dim, block.shape[-1])

    raw_qk = dot(w_scaled[:, : 2 * part], core_all, 0, 1) + bias[: 2 * part]
    raw_qk = raw_qk.reshape(2, heads, head_dim, team_rows)
    squares = jnp.sum(raw_qk * raw_qk, axis=(1, 2))
    squares, raw_qk, cap_team, cap_rows, cotangent, w_out = together(
        team_sum(squares), raw_qk, cap_team, cap_rows, cotangent, w_out
    )
    cap_half = across_half(cap_team)
    cap_all = lax.all_gather(cap_rows, TEAM, axis=0, tiled=True)
    cot_a, cot_b = own_clip(cotangent)
    w_out = both_sides(w_out, "clip", clip_pair, 0)
    w_out = lax.all_gather(w_out, "rep", axis=2) if reps > 1 else w_out[:, :, None]
    factors = lax.rsqrt(squares / width + EPSILON)[:, None, None]
    cosine, sine = rope_tables(all_places, head_dim)
    values = by_head((dot(w_scaled[:, 2 * part :], core_all, 0, 1) + bias[2 * part :]).astype(BF))
    gains = jnp.stack([own_columns(norm_gains[i]) for i in (1, 2, 3)])
    gains = gains.reshape(3, heads, head_dim, 1)
    normed_qk = raw_qk * factors
    turned = normed_qk * gains[:2]
    queries = (turn(turned[0], cosine, sine) * scale).astype(BF)
    keys = turn(turned[1], cosine, sine).astype(BF)
    all_keys, all_values = keys, values
    if reps > 1:
        all_keys, all_values = (lax.all_gather(v, "rep", axis=2, tiled=True) for v in (keys, values))

    queries, all_keys, all_values, gate_shard, up_shard, w_out = together(
        queries, all_keys, all_values, gate_weight, up_weight, w_out
    )
    w_out = both_sides(w_out, "tz", bits[0], 3)
    ff_block = down_weight.shape[0]
    ff_part = groups * ff_block
    up_team = from_team(
        join([by_rank(gate_shard, groups, True), by_rank(up_shard, groups, True)], axis=2)
    )
    o_self, logs = self_forward(queries, all_keys, all_values, 0, None)
    o_self, logs = self_forward(queries, all_keys, all_values, 1, (o_self, logs))
    o_self, logs, cap_half, cot_a, cot_b, up_team, w_out, cap_all = together(
        o_self, logs, cap_half, cot_a, cot_b, up_team, w_out, cap_all
    )
    w_cap = across_clip(cap_half)
    grad_out = join([cot_a, cot_b]).astype(F32)
    d_ffn = (gate_ffn * grad_out).astype(BF)
    d_ffn_all = lax.all_gather(d_ffn, TEAM, axis=0, tiled=True)
    up_half = across_half(up_team)
    w_out = both_sides(w_out, "ty", bits[1], 4)
    o_self, logs = self_forward(queries, all_keys, all_values, 2, (o_self, logs))
    o_self, w_cap, down_shard = together(o_self, w_cap, down_weight)
    craw = dot(w_cap, cap_all, 0, 1)
    craw_key = by_head(craw[:part])
    square_c = jnp.sum(craw_key * craw_key, axis=(0, 1))[None]
    square_c = team_sum(square_c)
    factor_c = lax.rsqrt(square_c / width + EPSILON)[None]
    normed_c = craw_key * factor_c
    ckeys = (normed_c * gains[2]).astype(BF)
    cvalues = by_head(craw[part:]).astype(BF)
    all_ckeys, all_cvalues = ckeys, cvalues
    step = lax.axis_index("rep")
    order = jnp.arange(team * clips_here * slots_here, dtype=jnp.int32)
    in_rank = order // slots_here % clips_here
    from_rank = order // (slots_here * clips_here)
    from_shard = from_rank % 4 * 2 + from_rank // 4
    slots = ((in_rank * reps + step) * team + from_shard) * slots_here + order % slots_here
    if reps > 1:
        all_ckeys, all_cvalues = (
            lax.all_gather(v, "rep", axis=2, tiled=True) for v in (ckeys, cvalues)
        )
        slots = join([slots + (r - step) * team * slots_here for r in range(reps)])
    mask = jnp.where(slots < pick(caption_lengths, half), 0.0, NEGATIVE).astype(F32)[:, None]
    o_cross = cross_forward(queries, all_ckeys, all_cvalues, mask)
    tanh_gate = jnp.tanh(lax.dynamic_slice_in_dim(cross_gate, rank * heads, heads))
    tanh_wide = tanh_gate[:, None, None]
    mixed = (o_self + tanh_wide * o_cross).astype(BF).reshape(part, team, rows_here)
    mixed, w_out, up_half, d_ffn_all = together(
        jnp.transpose(mixed, (1, 0, 2)), w_out, up_half, d_ffn_all
    )
    w_gate_up = lax.all_gather(up_half.reshape(-1, 2 * ff_part), "clip", axis=0, tiled=True)
    down_half = across_half(down_shard)
    w_out = both_sides(w_out, "tc", bits[2], 5)
    mixed = lax.all_to_all(mixed, TEAM, split_axis=0, concat_axis=0, tiled=True)
    mixed, w_out, down_half = together(mixed, w_out, down_half)
    combined = mixed.reshape(width, rows_here)
    w_out = w_out.reshape(-1, width)
    w_down = across_clip(down_half)

    branch = dot(combined, w_out, 0, 0)
    middle = token_vals + gate_attn * branch
    factor_f = row_factor(middle)
    core_f = middle * factor_f
    ffn_in = (core_f * norm_gains[4] * (1.0 + scale_ffn) + shift_ffn).astype(BF)
    ffn_all = lax.all_gather(after(ffn_in, w_gate_up), TEAM, axis=0, tiled=True)
    w_gate_up, w_down, ffn_all = together(w_gate_up, w_down, ffn_all)
    gate_up = dot(ffn_all, w_gate_up, 1, 0)
    gate_vals, up_vals = gate_up[:, :ff_part], gate_up[:, ff_part:]
    d_hidden = dot(d_ffn_all, w_down, 1, 1)
    sig = jax.nn.sigmoid(gate_vals)
    silu_gate = gate_vals * sig
    hidden = (silu_gate * up_vals).astype(BF)
    d_gate = (d_hidden * up_vals * (sig + silu_gate * (1.0 - sig))).astype(BF)
    d_up = (d_hidden * silu_gate).astype(BF)
    d_gate_up = join([d_gate, d_up], axis=1)

    def core_side(block, which, dim=0):
        count = block.shape[dim] // 2
        return lax.dynamic_slice_in_dim(block, which * count, count, dim)

    def ffn_side(which):
        return dot(core_side(d_gate_up, which), w_gate_up, 1, 1).astype(BF)

    def by_chip(mine):
        tiled = mine.reshape(2, 2, 2, clip_rows, width)
        return tiled[:, :, 0], tiled[:, :, 1]

    def add_core(kept, sent):
        return (kept.astype(F32) + swap(sent, "tc").astype(F32)).astype(BF)

    def team_parts(slice_grad):
        tiled = slice_grad.reshape(lax.axis_size("clip"), clips_here, -1, slice_grad.shape[-1])
        return kept_sum(tiled, "clip", clip_pair, 0).astype(BF)

    def half_parts(tiled):
        summed = kept_sum(tiled, "half", half, 0)
        if reps > 1:
            summed = lax.psum_scatter(summed, "rep", scatter_dimension=0, tiled=True)
        return summed

    def to_shards(summed):
        ranked = summed.astype(BF).reshape(team, -1, summed.shape[-1])
        return lax.all_to_all(ranked, SHARDS, split_axis=0, concat_axis=0, tiled=True)

    def head_columns(blocks, split):
        rows = blocks.shape[1]
        tiled = blocks.reshape(2, 2, 2, rows, split, part)
        return jnp.transpose(tiled, (3, 4, 2, 0, 1, 5)).reshape(rows, -1).astype(F32)

    def ff_columns(blocks):
        rows = blocks.shape[1]
        tiled = blocks.reshape(team, rows, groups, ff_block)
        return jnp.transpose(tiled, (1, 2, 0, 3)).reshape(rows, -1).astype(F32)

    def all_parts(slice_grad):
        return lax.psum_scatter(slice_grad, GROUPS, scatter_dimension=0, tiled=True)

    side_sent = ffn_side(1 - bits[2])
    mine = add_core(ffn_side(bits[2]), side_sent)
    pair = chips_first(*by_chip(mine), bits)
    grad_down = dot(after(hidden, mine), d_ffn_all, 0, 0).astype(BF)
    *pair, grad_down = together(*pair, grad_down)
    sum_down = all_parts(grad_down)
    d_ffn_in = join(chips_last(*pair, bits))
    late_hidden = after(hidden, grad_down)
    out_sent = dot(core_side(late_hidden, 1 - bits[2]), w_down, 1, 0).astype(BF)
    out_kept = dot(core_side(late_hidden, bits[2]), w_down, 1, 0).astype(BF)
    d_ffn_in, out_sent, out_kept = together(d_ffn_in, out_sent, out_kept)

    out_mine = add_core(out_kept, out_sent)
    d_shift_ffn = jnp.sum(d_ffn_in, axis=0, keepdims=True)
    moment_f = jnp.sum(d_ffn_in * core_f, axis=0, keepdims=True)
    d_scale_ffn = moment_f * norm_gains[4]
    d_gain_ffn = moment_f * (1.0 + scale_ffn)
    d_core = d_ffn_in * (norm_gains[4] * (1.0 + scale_ffn))
    d_middle = grad_out + factor_f * (
        d_core - core_f * jnp.mean(d_core * core_f, axis=-1, keepdims=True)
    )
    d_branch = (gate_attn * d_middle).astype(BF)
    d_gate_attn = jnp.sum(d_middle * branch, axis=0, keepdims=True)
    d_combined = dot(w_out, d_branch, 1, 1).astype(BF)
    d_mixed = lax.all_to_all(
        d_combined.reshape(team, part, rows_here), TEAM, split_axis=0, concat_axis=0, tiled=True
    )
    late_ffn, late_gate, out_mine = together(ffn_all, d_gate_up, out_mine, d_combined)[:3]
    grad_gate_up = dot(late_ffn, late_gate, 0, 0).astype(BF)
    d_mixed, grad_gate_up = together(d_mixed, grad_gate_up)
    up_rows = all_parts(grad_gate_up)
    d_self = by_head(jnp.transpose(d_mixed, (1, 0, 2)).reshape(part, team_rows))

    out_pair = chips_first(*by_chip(out_mine), bits)
    gate_tile = jnp.broadcast_to(tanh_wide, (heads, 8, 128))
    dq_cross, d_ckeys, d_cvalues, gate_rows = cross_backward(
        queries, d_self, all_ckeys, all_cvalues, mask, gate_tile
    )
    d_cross_gate = jnp.sum(gate_rows, axis=(1, 2)) * (1.0 - tanh_gate * tanh_gate)
    if reps > 1:
        d_ckeys, d_cvalues = (
            lax.psum_scatter(v, "rep", scatter_dimension=2, tiled=True)
            for v in (d_ckeys, d_cvalues)
        )

    def team_mean(block):
        return jnp.sum(block, axis=(-3, -2))

    scaled_c = d_ckeys * gains[2]
    mean_c = team_mean(scaled_c * normed_c)[None]
    mean_c = mean_c + swap(mean_c, "tc")
    grad_output = dot(after(combined, dq_cross), d_branch, 1, 0).astype(BF)
    delta = jnp.sum(d_self.astype(F32) * o_self, axis=1, keepdims=True)
    delta, grad_output, mean_c, *out_pair = together(delta, grad_output, mean_c, *out_pair)
    sum_output = lax.psum_scatter(
        after(grad_output, up_rows), EVERY, scatter_dimension=0, tiled=True
    )
    ffn_out = join(chips_last(*out_pair, bits))
    mean_c = mean_c + swap(mean_c, "ty")
    mean_c = mean_c + swap(mean_c, "tz")
    backs = self_backward(queries, d_self, logs, delta, all_keys, all_values, 0, None)
    *backs, delta, mean_c, ffn_out = together(*backs, delta, mean_c, ffn_out)
    result = back_clip((middle + gate_ffn * ffn_out).astype(BF))
    d_gate_ffn = jnp.sum(grad_out * ffn_out, axis=0, keepdims=True)
    mean_c = mean_c[None] / width
    d_craw = factor_c * (scaled_c - normed_c * mean_c)
    d_gain_c = jnp.sum(d_ckeys * normed_c, axis=2).reshape(1, part)
    cap_low = join([d_craw, d_cvalues]).reshape(2 * part, -1).astype(BF)
    cap_half = team_parts(dot(cap_all, cap_low, 0, 1).astype(BF))
    d_cap = dot(cap_low, w_cap, 0, 1).astype(BF)
    d_cap = lax.psum_scatter(d_cap, TEAM, scatter_dimension=0, tiled=True).astype(F32)
    backs = self_backward(queries, d_self, logs, delta, all_keys, all_values, 1, backs)
    *backs, delta, up_rows = together(*backs, delta, up_rows)
    sum_gate_up = to_shards(up_rows)
    backs = self_backward(queries, d_self, logs, delta, all_keys, all_values, 2, backs)
    *backs, result, sum_gate_up, cap_half = together(*backs, result, sum_gate_up, cap_half)
    cap_rows = half_parts(cap_half)
    dq_self, dk, dv = backs
    if reps > 1:
        dk, dv = (lax.psum_scatter(v, "rep", scatter_dimension=2, tiled=True) for v in (dk, dv))

    turned_grad = jnp.stack(
        [turn((dq_self + dq_cross) * scale, cosine, -sine), turn(dk, cosine, -sine)]
    )
    scaled_qk = turned_grad * gains[:2]
    mean_qk = team_sum(team_mean(scaled_qk * normed_qk))[:, None, None] / width
    d_gain_qk = jnp.sum(turned_grad * normed_qk, axis=3).reshape(2, part)
    d_qk = (factors * (scaled_qk - normed_qk * mean_qk)).reshape(2 * part, team_rows)
    d_projected = join([d_qk, dv.reshape(part, team_rows)]).astype(BF)
    d_projected, cap_rows = together(d_projected, cap_rows)

    def attn_side(which):
        return dot(core_side(d_projected, which, 1), w_in, 0, 1).astype(BF)

    side_sent = attn_side(1 - bits[2])
    mine = add_core(attn_side(bits[2]), side_sent)
    core_grad = dot(core_all, d_projected, 0, 1)
    column_sum = dot(d_projected, jnp.ones((team_rows, 128), BF), 1, 0)[:, 0][None]
    mine, core_grad = together(mine, core_grad)
    pair = chips_first(*by_chip(mine), bits)
    in_half = team_parts((core_grad * row_scale + row_shift * column_sum).astype(BF))
    w_in_f = w_in.astype(F32)
    d_shift_attn = jnp.sum(column_sum * w_in_f, axis=1)[None]
    moment_a = jnp.sum(core_grad * w_in_f, axis=1)[None]
    d_scale_attn = moment_a * norm_gains[0]
    d_gain_attn = moment_a * (1.0 + scale_attn)

    def placed(values):
        wide = jnp.tile(values, (1, width // values.shape[1]))
        spot = jnp.arange(width, dtype=jnp.int32) // values.shape[1]
        return jnp.where(spot == rank, wide, 0.0)

    gate_row = jnp.pad(d_cross_gate[None], ((0, 0), (0, width // team - heads)))
    sums = join(
        [
            d_shift_attn,
            d_scale_attn,
            d_gate_attn,
            d_shift_ffn,
            d_scale_ffn,
            d_gate_ffn,
            d_gain_attn,
            d_gain_ffn,
            placed(join([d_gain_qk, d_gain_c, gate_row])),
        ]
    )
    sums = sums + swap(sums, "tc")
    sums = both_sides(sums, "clip", clip_pair, 0)
    *pair, sums, in_half = together(*pair, sums, in_half)
    d_attn_in = join(chips_last(*pair, bits))
    for axis in ("ty", "tz"):
        sums = sums + swap(sums, axis)
    if reps > 1:
        sums = lax.psum(sums, "rep")
    sums = both_sides(sums, "half", half, 1)
    d_attn_in, sums = together(d_attn_in, sums)
    sum_gate, sum_up = ff_columns(sum_gate_up[..., :ff_part]), ff_columns(sum_gate_up[..., ff_part:])
    in_rows = half_parts(in_half)
    sum_cap = to_shards(cap_rows)
    factor_a = row_factor(token_vals)
    core_a = token_vals * factor_a
    d_core = d_attn_in * (norm_gains[0] * (1.0 + scale_attn))
    d_tokens = back_clip(
        d_middle
        + factor_a * (d_core - core_a * jnp.mean(d_core * core_a, axis=-1, keepdims=True))
    )
    mod_low = sums[:, :, :6].astype(BF).reshape(condition.shape[0], -1)
    small = jnp.sum(sums[:, :, 6:], axis=(0, 1))
    gain_sum = join([small[:1], small[2:5], small[1:2]])
    gate_sum = small[5].reshape(team, -1)[:, :heads].reshape(-1)
    d_bias = jnp.sum(mod_low.astype(F32), axis=0)
    d_silu = dot(mod_low, modulation_weight, 1, 1)
    d_silu = lax.dynamic_update_slice_in_dim(
        jnp.zeros(condition.shape, F32), d_silu, device * shard_rows, 1
    )
    sum_input = to_shards(in_rows)
    if reps > 1:
        d_silu = lax.psum(d_silu, "rep")
    for axis in ("tc", "ty", "tz", "half", "clip"):
        d_silu = d_silu + swap(d_silu, axis)
    _, silu_back = jax.vjp(jax.nn.silu, condition)
    d_condition = silu_back(d_silu)[0]
    grad_mod = dot(silu_rows, mod_low, 0, 0)

    sum_input = head_columns(sum_input, 3)
    sum_ckey = head_columns(sum_cap[..., :part], 1)
    sum_cvalue = head_columns(sum_cap[..., part:], 1)
    sum_down, sum_output, d_cap = together(sum_down, sum_output, d_cap, d_attn_in)[:3]
    sum_down, sum_output = sum_down.astype(F32), sum_output.astype(F32)
    d_cap = d_cap.reshape(clips_here, slots_here, -1)
    d_caption = back_clip(join([pick(d_cap, half), pick(d_cap, 1 - half)]))
    return (
        result,
        d_tokens,
        d_caption,
        d_condition,
        grad_mod,
        d_bias,
        gain_sum,
        gate_sum,
        sum_input,
        sum_output,
        sum_ckey,
        sum_cvalue,
        sum_gate,
        sum_up,
        sum_down,
    )


def solution(mesh):
    clip_count, seq_count = mesh.shape["clip"], mesh.shape["seq"]

    def program(*arrays):
        halves = arrays[0].shape[0] // clip_count
        shape = (clip_count, halves, seq_count // (halves * 8), 2, 2, 2)
        fine = Mesh(mesh.devices.reshape(shape), EVERY)
        rows = P("clip", SEQ, None)
        shard = P(EVERY, None)
        mapped = jax.shard_map(
            on_device,
            mesh=fine,
            in_specs=(
                rows,
                P(),
                rows,
                P("clip"),
                P(None, "clip", SEQ),
                shard,
                P(),
                P(),
                P(),
                shard,
                shard,
                shard,
                shard,
                shard,
                shard,
                shard,
                rows,
            ),
            out_specs=(rows, rows, rows, P(), shard, P(), P(), P()) + (shard,) * 7,
            check_vma=False,
        )
        return mapped(*arrays)

    return program
```

time: 959 us -> 880 us (0.918)
  matrix products: 131 us -> 102 us
  other arithmetic: 146 us -> 120 us
  local copies, waits for them, and re-layouts: 131 us -> 106 us
  Pallas kernels: 71.8 us -> 83.8 us
  starting transfers between devices: 122 us -> 111 us
    another operation x28 -> x0, other arithmetic: 30 us -> none  [the longest x6 12.3 us: gather_rows(): return jnp.stack([both, swap(both, 'tc')]).reshape(-1, block.shape[1])]
    dot_general x27 -> x23, matrix products: 131 us -> 102 us  [dot(): return lax.dot_general(left, right, dims, preferred_element_type=F32)]
    select_n x6 -> x13, other arithmetic: 9.45 us -> 25.9 us  [both_sides(): jnp.where(bit == 0, jnp.stack([block, other], dim), jnp.stack([other, blo...]
    ppermute x86 -> x64, starting transfers between devices: 89.1 us -> 73.5 us  [swap(): return lax.ppermute(block, axis, [(0, 1), (1, 0)])]
    another operation x11 -> x3, local copies, waits for them, and re-layouts: 12.6 us -> 0.16 us  [the longest x2 0.09 us: placed(): wide = jnp.tile(values, (1, width // values.shape[1]))]
    reshape x24 -> x14, local copies, waits for them, and re-layouts: 19.3 us -> 7.24 us  [the longest x1 1.37 us: by_rank(): return jnp.transpose(tiled, (3, 4, 2, 0, 1, 5)).reshape(team, rows, -1)]
    convert_element_type x8 -> x10, local copies, waits for them, and re-layouts: 2.13 us -> 14.1 us  [the longest x4 7.75 us: ff_columns(): return jnp.transpose(tiled, (1, 2, 0, 3)).reshape(rows, -1).astype(F32)]
    pallas_call x2 -> x8, Pallas kernels: 57.5 us -> 69.3 us  [the longest x6 65.3 us: one_head(): pl.pallas_call(body, grid=(1, steps), in_specs=in_specs + [pl.BlockSpec(m...]
  transfers between devices with their start and end apart: 102 -> 81, of which waited for: 40 -> 40; matrix products, arithmetic and copies ran while one was open for 38% -> 30% of each run, Pallas kernels for 8% -> 10%
where the time goes in v3:
time: 880 us; the launch traced here: 866 us
  waiting for transfers between devices  329 us (37%)
  other arithmetic  120 us (14%)
  starting transfers between devices  111 us (13%)
  local copies, waits for them, and re-layouts  106 us (12%)
  matrix products  102 us (12%)
  Pallas kernels  83.8 us (10%)
  between operations  16.1 us (2%)
    ppermute x64, waiting for transfers between devices, swap(): return lax.ppermute(block, axis, [(0, 1), (1, 0)])  304 us
    dot_general x23, matrix products, dot(): return lax.dot_general(left, right, dims, preferred_element_type=F32)  102 us
    ppermute x64, starting transfers between devices, swap(): return lax.ppermute(block, axis, [(0, 1), (1, 0)])  73.5 us
    pallas_call x6, Pallas kernels, one_head(): pl.pallas_call(body, grid=(1, steps), in_specs=in_specs + [pl.BlockSpec(m...  65.3 us
    unnamed x256, local copies, waits for them, and re-layouts  28.9 us
    select_n x13, other arithmetic, both_sides(): jnp.where(bit == 0, jnp.stack([block, other], dim), jnp.stack([other, blo...  25.9 us
    all_gather x1, waiting for transfers between devices, on_device(): ffn_all = lax.all_gather(after(ffn_in, w_gate_up), TEAM, axis=0, tiled=True)  17.8 us
  transfers between devices with their start and end apart: 81, of which 40 were waited for; matrix products, arithmetic and copies ran while one was open for 30% of the time, Pallas kernels for 10%

profile of v3, /device:TPU:0, one launch (start us, length us, event | category | flops | bytes accessed | tf_op | source)
XLA Modules:
  0.0 866.4 jit_solution(2979505482415744976)
XLA Ops:
  25.6 14.0 %collective-permute-done = bf16[136,1536]{1,0:T(8,128)(2,1)S(1)} collective-permute-done((bf16[136,1536]{1,0:T(8,128)(2,1)}, bf16[136,1536]{1,0:T(8,128)(2,1)S(1)}, u32[]{:S(2)}, u32[]{:S(2)}) %collective-permute-start) | collective-permute-done | bytes 417824 | tf_op jit(solution)/shard_map/ppermute | solution.py:24
  49.1 10.8 %collective-permute-done.5 = f32[1,9216]{1,0:T(1,128)S(1)} collective-permute-done((f32[1,9216]{1,0:T(1,128)S(1)}, f32[1,9216]{1,0:T(1,128)S(1)}, u32[]{:S(2)}, u32[]{:S(2)}) %collective-permute-start.5) | collective-permute-done | bytes 36896 | tf_op jit(solution)/shard_map/ppermute | solution.py:24
  73.6 15.2 %collective-permute-done.7 = bf16[768,576]{0,1:T(8,128)(2,1)} collective-permute-done((bf16[768,576]{0,1:T(8,128)(2,1)S(1)}, bf16[768,576]{0,1:T(8,128)(2,1)}, u32[]{:S(2)}, u32[]{:S(2)}) %collective-permute-start.7) | collective-permute-done | bytes 884768 | tf_op jit(solution)/shard_map/ppermute | solution.py:24
  147.6 7.6 shard_map.282
  155.3 7.6 shard_map.283
  162.9 12.2 %collective-permute-done.14 = bf16[1024,384]{1,0:T(8,128)(2,1)} collective-permute-done((bf16[1024,384]{1,0:T(8,128)(2,1)}, bf16[1024,384]{1,0:T(8,128)(2,1)}, u32[]{:S(2)}, u32[]{:S(2)}) %collective-permute-start.14) | collective-permute-done | bytes 786464 | tf_op jit(solution)/shard_map/ppermute | solution.py:24
  177.3 15.5 %collective-permute-done.16 = bf16[2,2,1,48,1536]{4,3,1,0,2:T(8,128)(2,1)S(1)} collective-permute-done((bf16[2,2,1,48,1536]{4,3,1,0,2:T(8,128)(2,1)}, bf16[2,2,1,48,1536]{4,3,1,0,2:T(8,128)(2,1)S(1)}, u32[]{:S(2)}, u32[]{:S(2)}) %collective-permute-start.16) | collective-permute-done | bytes 589856 | tf_op jit(solution)/shard_map/ppermute | solution.py:24
  203.3 7.7 shard_map.284
  210.9 22.2 %collective-permute-done.17 = bf16[2,1024,384]{2,1,0:T(8,128)(2,1)} collective-permute-done((bf16[2,1024,384]{2,1,0:T(8,128)(2,1)S(1)}, bf16[2,1024,384]{2,1,0:T(8,128)(2,1)}, u32[]{:S(2)}, u32[]{:S(2)}) %collective-permute-start.17) | collective-permute-done | bytes 1572896 | tf_op jit(solution)/shard_map/ppermute | solution.py:24
  245.5 6.6 collective-permute-done.21
  274.8 17.5 %collective-permute-done.24 = bf16[128,1536]{1,0:T(8,128)(2,1)} collective-permute-done((bf16[128,1536]{1,0:T(8,128)(2,1)}, bf16[128,1536]{1,0:T(8,128)(2,1)}, u32[]{:S(2)}, u32[]{:S(2)}) %collective-permute-start.24) | collective-permute-done | bytes 393248 | tf_op jit(solution)/shard_map/ppermute | solution.py:24
  300.0 6.0 multiply_reduce_fusion.7
  310.5 19.1 %collective-permute-done.25 = bf16[2,128,1536]{2,1,0:T(8,128)(2,1)} collective-permute-done((bf16[2,128,1536]{2,1,0:T(8,128)(2,1)S(1)}, bf16[2,128,1536]{2,1,0:T(8,128)(2,1)}, u32[]{:S(2)}, u32[]{:S(2)}) %collective-permute-start.25) | collective-permute-done | bytes 786464 | tf_op jit(solution)/shard_map/ppermute | solution.py:24
  332.4 17.8 %all-gather.14.cloned.1.call-done = bf16[2048,1536]{1,0:T(8,128)(2,1)} async-done(((bf16[256,1536]{1,0:T(8,128)(2,1)}), bf16[2048,1536]{1,0:T(8,128)(2,1)}) %all-gather.14.cloned.1.call-update) | async-done | bytes 6291472 | tf_op jit(solution)/shard_map/all_gather | solution.py:603
  350.2 9.9 %fusion.106 = f32[2048,1024]{0,1:T(8,128)S(1)} fusion(bf16[2048,1536]{1,0:T(8,128)(2,1)} %all-gather.14.cloned.1.call-done, bf16[1536,1024]{1,0:T(8,128)(2,1)} %all-gather.12.cloned.1.call-done), kind=kOutput, calls=%fused_computation.327 | convolution fusion | flops 6442450944 | bytes 17825792 | tf_op jit(solution)/shard_map/dot_general | solution.py:37
  360.1 8.5 multiply_convert_fusion.1
  379.8 6.9 add_convert_fusion.2
  390.3 7.3 convolution_convert_fusion.10
  397.6 10.5 %collective-permute-done.28 = bf16[2,128,1536]{2,1,0:T(8,128)(2,1)} collective-permute-done((bf16[2,128,1536]{2,1,0:T(8,128)(2,1)}, bf16[2,128,1536]{2,1,0:T(8,128)(2,1)}, u32[]{:S(2)}, u32[]{:S(2)}) %collective-permute-start.28) | collective-permute-done | bytes 786464 | tf_op jit(solution)/shard_map/ppermute | solution.py:24
  448.3 10.1 %convolution_convert_fusion.3 = bf16[1536,1024]{1,0:T(8,128)(2,1)} fusion(bf16[2048,1536]{1,0:T(8,128)(2,1)} %all-gather.14.cloned.1.call-done, bf16[2048,1024]{0,1:T(8,128)(2,1)S(1)} %copy-done.42), kind=kOutput, calls=%fused_computation.22 | convolution fusion | flops 6444023808 | bytes 13631488 | tf_op jit(solution)/shard_map/dot_general | solution.py:37
  470.8 9.4 %shard_map.286 = (f32[3,64,2048]{2,1,0:T(8,128)}, f32[3,64,256]{2,1,0:T(8,128)}, f32[3,64,256]{2,1,0:T(8,128)}, f32[3,1,2048]{2,1,0:T(1,128)}) custom-call(bf16[3,64,2048]{2,1,0:T(8,128)(2,1)} %get-tuple-element.160.refs_0_.q_ref, bf16[3,64,2048]{2,1,0:T(8,128)(2,1)} %reshape_reshape.3.g_ref.refs_1_, bf16[3,64,256]{2,1,0:T(8,128)(2,1)} %multiply_convert_fusion.8.k_ref, ...), custom_call_target="tpu_custom_call" | custom-call | flops 4026531840 | bytes 786432 | tf_op jit(solution)/shard_map/pallas_call | solution.py:306
  491.5 7.9 collective-permute-done.33
  512.5 14.1 %shard_map.287 = (f32[3,64,2048]{2,1,0:T(8,128)}, f32[3,64,2048]{2,1,0:T(8,128)}, f32[3,64,2048]{2,1,0:T(8,128)}) custom-call(bf16[3,64,2048]{2,1,0:T(8,128)(2,1)} %get-tuple-element.160.refs_0_.q_ref, bf16[3,64,2048]{2,1,0:T(8,128)(2,1)} %reshape_reshape.3.g_ref.refs_1_, f32[3,1,2048]{2,1,0:T(1,128)} %get-tuple-element.207.refs_2_, ...), custom_call_target="tpu_custom_call" | custom-call | flops 10737418240 | bytes 2097152 | tf_op jit(solution)/shard_map/pallas_call | solution.py:231
  542.3 14.1 %shard_map.288 = (f32[3,64,2048]{2,1,0:T(8,128)}, f32[3,64,2048]{2,1,0:T(8,128)}, f32[3,64,2048]{2,1,0:T(8,128)}) custom-call(bf16[3,64,2048]{2,1,0:T(8,128)(2,1)} %get-tuple-element.160.refs_0_.q_ref, bf16[3,64,2048]{2,1,0:T(8,128)(2,1)} %reshape_reshape.3.g_ref.refs_1_, ...), custom_call_target="tpu_custom_call", output_to_operand_aliasing={{0}: (6, {}), {1}: (7, {}), {2}: (8, {})} | custom-call | flops 10737418240 | bytes 2097152 | tf_op jit(solution)/shard_map/pallas_call | solution.py:231
  561.2 11.2 %collective-permute-done.40 = bf16[2,1024,384]{2,1,0:T(8,128)(2,1)} collective-permute-done((bf16[2,1024,384]{2,1,0:T(8,128)(2,1)}, bf16[2,1024,384]{2,1,0:T(8,128)(2,1)}, u32[]{:S(2)}, u32[]{:S(2)}) %collective-permute-start.40) | collective-permute-done | bytes 1572896 | tf_op jit(solution)/shard_map/ppermute | solution.py:24
  575.9 14.2 %shard_map.289 = (f32[3,64,2048]{2,1,0:T(8,128)}, f32[3,64,2048]{2,1,0:T(8,128)}, f32[3,64,2048]{2,1,0:T(8,128)}) custom-call(bf16[3,64,2048]{2,1,0:T(8,128)(2,1)} %get-tuple-element.160.refs_0_.q_ref, bf16[3,64,2048]{2,1,0:T(8,128)(2,1)} %reshape_reshape.3.g_ref.refs_1_, ...), custom_call_target="tpu_custom_call", output_to_operand_aliasing={{0}: (6, {}), {1}: (7, {}), {2}: (8, {})} | custom-call | flops 10737418240 | bytes 2097152 | tf_op jit(solution)/shard_map/pallas_call | solution.py:231
  611.2 46.9 %collective-permute-done.44 = bf16[1024,384]{1,0:T(8,128)(2,1)S(1)} collective-permute-done((bf16[1024,384]{1,0:T(8,128)(2,1)S(1)}, bf16[1024,384]{1,0:T(8,128)(2,1)S(1)}, u32[]{:S(2)}, u32[]{:S(2)}) %collective-permute-start.44) | collective-permute-done | bytes 786464 | tf_op jit(solution)/shard_map/ppermute | solution.py:24
  689.5 8.5 fusion.109
  732.3 9.9 %collective-permute-done.47 = bf16[2,128,1536]{2,1,0:T(8,128)(2,1)} collective-permute-done((bf16[2,128,1536]{2,1,0:T(8,128)(2,1)}, bf16[2,128,1536]{2,1,0:T(8,128)(2,1)}, u32[]{:S(2)}, u32[]{:S(2)}) %collective-permute-start.47) | collective-permute-done | bytes 786464 | tf_op jit(solution)/shard_map/ppermute | solution.py:24
  769.8 12.8 %collective-permute-done.54 = f32[2,12,1536]{2,1,0:T(8,128)S(1)} collective-permute-done((f32[2,12,1536]{2,1,0:T(8,128)S(1)}, f32[2,12,1536]{2,1,0:T(8,128)S(1)}, u32[]{:S(2)}, u32[]{:S(2)}) %collective-permute-start.54) | collective-permute-done | bytes 147488 | tf_op jit(solution)/shard_map/ppermute | solution.py:24
  786.2 10.8 %collective-permute-done.52 = bf16[128,1536]{1,0:T(8,128)(2,1)S(1)} collective-permute-done((bf16[128,1536]{1,0:T(8,128)(2,1)S(1)}, bf16[128,1536]{1,0:T(8,128)(2,1)S(1)}, u32[]{:S(2)}, u32[]{:S(2)}) %collective-permute-start.52) | collective-permute-done | bytes 393248 | tf_op jit(solution)/shard_map/ppermute | solution.py:24
  839.3 15.2 %collective-permute-done.56 = bf16[128,1536]{1,0:T(8,128)(2,1)S(1)} collective-permute-done((bf16[128,1536]{1,0:T(8,128)(2,1)S(1)}, bf16[128,1536]{1,0:T(8,128)(2,1)S(1)}, u32[]{:S(2)}, u32[]{:S(2)}) %collective-permute-start.56) | collective-permute-done | bytes 393248 | tf_op jit(solution)/shard_map/ppermute | solution.py:24
  (657 shorter events, 442.4 us)
Async XLA Ops:
  25.5 70.5 %all-gather.6.cloned.1.call-start = ((), (), s32[]{:S(2)}) async-start(), calls=%async_computation.12 | async-start | bytes 7520256 | tf_op jit(solution)/shard_map/all_gather | solution.py:474
  96.0 31.8 %collective-permute-start.12 = (bf16[48,1536]{1,0:T(8,128)(2,1)}, bf16[48,1536]{1,0:T(8,128)(2,1)S(1)}, u32[]{:S(2)}, u32[]{:S(2)}) collective-permute-start(bf16[48,1536]{1,0:T(8,128)(2,1)} %param.27), channel_id=1, source_target_pairs={{0,8},{8,0},{1,9},{9,1},{2,10},{10,2},{3,11},{11,3},{4,12},{12,4},... | collective-permute-start | bytes 442376 | tf_op jit(solution)/shard_map/ppermute | solution.py:24
  99.0 28.8 %all-to-all-start.1 = ((bf16[8,128,384]{1,2,0:T(8,128)(2,1)}), bf16[8,128,384]{1,2,0:T(8,128)(2,1)S(1)}, u32[]{:S(2)}, u32[]{:S(2)}) async-start(bf16[8,128,384]{1,2,0:T(8,128)(2,1)} %pad_maximum_fusion.7), calls=%async_computation.1 | async-start | bytes 1572864 | tf_op jit(solution)/shard_map/all_to_all | solution.py:447
  104.9 90.4 %all-gather.8.cloned.1.call-start = ((), (), s32[]{:S(2)}) async-start(), calls=%async_computation.13 | async-start | bytes 2359296 | tf_op jit(solution)/shard_map/all_gather | solution.py:522
  133.1 41.9 %collective-permute-start.14 = (bf16[1024,384]{1,0:T(8,128)(2,1)}, bf16[1024,384]{1,0:T(8,128)(2,1)}, u32[]{:S(2)}, u32[]{:S(2)}) collective-permute-start(bf16[1024,384]{1,0:T(8,128)(2,1)} %bitcast.24), channel_id=1, source_target_pairs={{0,8},{8,0},{1,9},{9,1},{2,10},{10,2},{3,11},{11,3},{4,12},{12,4},... | collective-permute-start | bytes 2359304 | tf_op jit(solution)/shard_map/ppermute | solution.py:24
  138.7 56.6 %all-to-all-start.2 = ((bf16[8,48,1024]{2,1,0:T(8,128)(2,1)}), bf16[8,48,1024]{2,1,0:T(8,128)(2,1)}, u32[]{:S(2)}, u32[]{:S(2)}) async-start(bf16[8,48,1024]{2,1,0:T(8,128)(2,1)} %pad_maximum_fusion.8), calls=%async_computation.2 | async-start | bytes 1572864 | tf_op jit(solution)/shard_map/all_to_all | solution.py:447
  142.9 121.6 %all-gather.10.cloned.1.call-start = ((), (), s32[]{:S(2)}) async-start(), calls=%async_computation.14 | async-start | bytes 7077888 | tf_op jit(solution)/shard_map/all_gather | solution.py:556
  143.2 52.0 %collective-permute-start.15 = (bf16[128,1536]{1,0:T(8,128)(2,1)S(1)}, bf16[128,1536]{1,0:T(8,128)(2,1)S(1)}, u32[]{:S(2)}, u32[]{:S(2)}) collective-permute-start(bf16[128,1536]{1,0:T(8,128)(2,1)S(1)} %get-tuple-element.410), channel_id=1, source_target_pairs={{0,8},{8,0},{1,9},{9,1},{2,10},{10,2},{3,11},{11,3},{4,12},{12,4},... | collective-permute-start | bytes 1179656 | tf_op jit(solution)/shard_map/ppermute | solution.py:24
  145.8 47.0 %collective-permute-start.16 = (bf16[2,2,1,48,1536]{4,3,1,0,2:T(8,128)(2,1)}, bf16[2,2,1,48,1536]{4,3,1,0,2:T(8,128)(2,1)S(1)}, u32[]{:S(2)}, u32[]{:S(2)}) collective-permute-start(bf16[2,2,1,48,1536]{4,3,1,0,2:T(8,128)(2,1)} %maximum_select_fusion.11), channel_id=1, source_target_pairs={{0,4},{4,0},{1,5},{5,1},{2,6},{6,2},{3,7},{7,3},{8,12},{12,8},{9,1... | collective-permute-start | bytes 1769480 | tf_op jit(solution)/shard_map/ppermute | solution.py:24
  196.3 113.8 %all-gather.12.cloned.1.call-start = ((), (), s32[]{:S(2)}) async-start(), calls=%async_computation.15 | async-start | bytes 4718592 | tf_op jit(solution)/shard_map/all_gather | solution.py:589
  196.6 36.5 %collective-permute-start.17 = (bf16[2,1024,384]{2,1,0:T(8,128)(2,1)S(1)}, bf16[2,1024,384]{2,1,0:T(8,128)(2,1)}, u32[]{:S(2)}, u32[]{:S(2)}) collective-permute-start(bf16[2,1024,384]{2,1,0:T(8,128)(2,1)S(1)} %maximum_select_fusion.3), channel_id=1, source_target_pairs={{0,16},{16,0},{1,17},{17,1},{2,18},{18,2},{3,19},{19,3},{4,20},{20... | collective-permute-start | bytes 4718600 | tf_op jit(solution)/shard_map/ppermute | solution.py:24
  200.1 39.9 %collective-permute-start.22 = (bf16[384,1024]{1,0:T(8,128)(2,1)}, bf16[384,1024]{1,0:T(8,128)(2,1)}, u32[]{:S(2)}, u32[]{:S(2)}) collective-permute-start(bf16[384,1024]{1,0:T(8,128)(2,1)} %bitcast.43), channel_id=1, source_target_pairs={{0,8},{8,0},{1,9},{9,1},{2,10},{10,2},{3,11},{11,3},{4,12},{12,4},... | collective-permute-start | bytes 2359304 | tf_op jit(solution)/shard_map/ppermute | solution.py:24
  201.9 50.2 %collective-permute-start.21 = (bf16[2,2,1,2,48,1536]{5,4,3,1,0,2:T(8,128)(2,1)}, bf16[2,2,1,2,48,1536]{5,4,3,1,0,2:T(8,128)(2,1)}, u32[]{:S(2)}, u32[]{:S(2)}) collective-permute-start(bf16[2,2,1,2,48,1536]{5,4,3,1,0,2:T(8,128)(2,1)} %maximum_select_fusion.7), channel_id=1, source_target_pairs={{0,2},{2,0},{1,3},{3,1},{4,6},{6,4},{5,7},{7,5},{8,10},{10,8},{9,1... | collective-permute-start | bytes 3538952 | tf_op jit(solution)/shard_map/ppermute | solution.py:24
  264.5 29.8 %collective-permute-start.23 = (bf16[2,2,1,2,2,48,1536]{6,5,4,3,1,0,2:T(8,128)(2,1)S(1)}, bf16[2,2,1,2,2,48,1536]{6,5,4,3,1,0,2:T(8,128)(2,1)}, u32[]{:S(2)}, u32[]{:S(2)}) collective-permute-start(bf16[2,2,1,2,2,48,1536]{6,5,4,3,1,0,2:T(8,128)(2,1)S(1)} %maximum_select_fusion.2), channel_id=1, source_target_pairs={{0,1},{1,0},{2,3},{3,2},{4,5},{5,4},{6,7},{7,6},{8,9},{9,8},{10,11... | collective-permute-start | bytes 7077896 | tf_op jit(solution)/shard_map/ppermute | solution.py:24
  264.5 35.4 %all-to-all-start.3 = ((bf16[8,192,256]{2,1,0:T(8,128)(2,1)}), bf16[8,192,256]{2,1,0:T(8,128)(2,1)}, u32[]{:S(2)}, u32[]{:S(2)}) async-start(bf16[8,192,256]{2,1,0:T(8,128)(2,1)} %bitcast.333), calls=%async_computation.3 | async-start | bytes 1572864 | tf_op jit(solution)/shard_map/all_to_all | solution.py:592
  270.5 79.7 %all-gather.14.cloned.1.call-start = ((), (), s32[]{:S(2)}) async-start(), calls=%async_computation.16 | async-start | bytes 7077888 | tf_op jit(solution)/shard_map/all_gather | solution.py:603
  441.3 115.1 %reduce-scatter.5.cloned.1.call-start = ((), (), s32[]{:S(2)}) async-start(), calls=%async_computation.17 | async-start | bytes 3932160 | tf_op jit(solution)/shard_map/reduce_scatter | solution.py:654
  458.4 204.3 %reduce-scatter.11.cloned.1.call-start = ((), (), s32[]{:S(2)}) async-start(), calls=%async_computation.20 | async-start | bytes 2359296 | tf_op jit(solution)/shard_map/reduce_scatter | solution.py:726
  461.1 28.9 %collective-permute-start.34 = (bf16[2,128,1536]{2,1,0:T(8,128)(2,1)}, bf16[2,128,1536]{2,1,0:T(8,128)(2,1)}, u32[]{:S(2)}, u32[]{:S(2)}) collective-permute-start(bf16[2,128,1536]{2,1,0:T(8,128)(2,1)} %dynamic-slice_bitcast_fusion.4), channel_id=1, source_target_pairs={{0,2},{2,0},{1,3},{3,1},{4,6},{6,4},{5,7},{7,5},{8,10},{10,8},{9,1... | collective-permute-start | bytes 2359304 | tf_op jit(solution)/shard_map/ppermute | solution.py:24
  463.9 35.5 %collective-permute-start.33 = (bf16[2,128,1536]{2,1,0:T(8,128)(2,1)}, bf16[2,128,1536]{2,1,0:T(8,128)(2,1)}, u32[]{:S(2)}, u32[]{:S(2)}) collective-permute-start(bf16[2,128,1536]{2,1,0:T(8,128)(2,1)} %dynamic-slice_bitcast_fusion.5), channel_id=1, source_target_pairs={{0,4},{4,0},{1,5},{5,1},{2,6},{6,2},{3,7},{7,3},{8,12},{12,8},{9,1... | collective-permute-start | bytes 2359304 | tf_op jit(solution)/shard_map/ppermute | solution.py:24
  533.1 272.0 %reduce-scatter.7.cloned.1.call-start = ((), (), s32[]{:S(2)}) async-start(), calls=%async_computation.18 | async-start | bytes 1966080 | tf_op jit(solution)/shard_map/reduce_scatter | solution.py:654
  538.9 33.5 %collective-permute-start.40 = (bf16[2,1024,384]{2,1,0:T(8,128)(2,1)}, bf16[2,1024,384]{2,1,0:T(8,128)(2,1)}, u32[]{:S(2)}, u32[]{:S(2)}) collective-permute-start(bf16[2,1024,384]{2,1,0:T(8,128)(2,1)} %dynamic-slice_bitcast_fusion), channel_id=1, source_target_pairs={{0,16},{16,0},{1,17},{17,1},{2,18},{18,2},{3,19},{19,3},{4,20},{20... | collective-permute-start | bytes 4718600 | tf_op jit(solution)/shard_map/ppermute | solution.py:24
  556.4 33.7 %all-to-all-start.5 = ((bf16[8,48,1024]{2,1,0:T(8,128)(2,1)}), bf16[8,48,1024]{2,1,0:T(8,128)(2,1)S(1)}, u32[]{:S(2)}, u32[]{:S(2)}) async-start(bf16[8,48,1024]{2,1,0:T(8,128)(2,1)} %bitcast.369), calls=%async_computation.6 | async-start | bytes 1572864 | tf_op jit(solution)/shard_map/all_to_all | solution.py:641
  560.0 245.1 %reduce-scatter.9.cloned.1.call-start = ((), (), s32[]{:S(2)}) async-start(), calls=%async_computation.19 | async-start | bytes 4866048 | tf_op jit(solution)/shard_map/reduce_scatter | solution.py:710
  605.5 52.5 %collective-permute-start.44 = (bf16[1024,384]{1,0:T(8,128)(2,1)S(1)}, bf16[1024,384]{1,0:T(8,128)(2,1)S(1)}, u32[]{:S(2)}, u32[]{:S(2)}) collective-permute-start(bf16[1024,384]{1,0:T(8,128)(2,1)S(1)} %dynamic-slice_bitcast_fusion.3), channel_id=1, source_target_pairs={{0,8},{8,0},{1,9},{9,1},{2,10},{10,2},{3,11},{11,3},{4,12},{12,4},... | collective-permute-start | bytes 2359304 | tf_op jit(solution)/shard_map/ppermute | solution.py:24
  662.4 37.3 %collective-permute-start.45 = (bf16[1024,1536]{1,0:T(8,128)(2,1)}, bf16[1024,1536]{1,0:T(8,128)(2,1)}, u32[]{:S(2)}, u32[]{:S(2)}) collective-permute-start(bf16[1024,1536]{1,0:T(8,128)(2,1)} %convolution_convert_fusion.4), channel_id=1, source_target_pairs={{0,1},{1,0},{2,3},{3,2},{4,5},{5,4},{6,7},{7,6},{8,9},{9,8},{10,11... | collective-permute-start | bytes 9437192 | tf_op jit(solution)/shard_map/ppermute | solution.py:24
  715.0 27.2 %collective-permute-start.47 = (bf16[2,128,1536]{2,1,0:T(8,128)(2,1)}, bf16[2,128,1536]{2,1,0:T(8,128)(2,1)}, u32[]{:S(2)}, u32[]{:S(2)}) collective-permute-start(bf16[2,128,1536]{2,1,0:T(8,128)(2,1)} %dynamic-slice_bitcast_fusion.1), channel_id=1, source_target_pairs={{0,2},{2,0},{1,3},{3,1},{4,6},{6,4},{5,7},{7,5},{8,10},{10,8},{9,1... | collective-permute-start | bytes 2359304 | tf_op jit(solution)/shard_map/ppermute | solution.py:24
  723.2 27.4 %collective-permute-start.46 = (bf16[2,128,1536]{2,1,0:T(8,128)(2,1)}, bf16[2,128,1536]{2,1,0:T(8,128)(2,1)}, u32[]{:S(2)}, u32[]{:S(2)}) collective-permute-start(bf16[2,128,1536]{2,1,0:T(8,128)(2,1)} %dynamic-slice_bitcast_fusion.2), channel_id=1, source_target_pairs={{0,4},{4,0},{1,5},{5,1},{2,6},{6,2},{3,7},{7,3},{8,12},{12,8},{9,1... | collective-permute-start | bytes 2359304 | tf_op jit(solution)/shard_map/ppermute | solution.py:24
  758.0 28.1 %collective-permute-start.51 = (bf16[128,1536]{1,0:T(8,128)(2,1)}, bf16[128,1536]{1,0:T(8,128)(2,1)S(1)}, u32[]{:S(2)}, u32[]{:S(2)}) collective-permute-start(bf16[128,1536]{1,0:T(8,128)(2,1)} %fusion.40), channel_id=1, source_target_pairs={{0,2},{2,0},{1,3},{3,1},{4,6},{6,4},{5,7},{7,5},{8,10},{10,8},{9,1... | collective-permute-start | bytes 1179656 | tf_op jit(solution)/shard_map/ppermute | solution.py:24
  765.2 53.4 %collective-permute-start.63 = (bf16[384,576]{1,0:T(8,128)(2,1)}, bf16[384,576]{1,0:T(8,128)(2,1)}, u32[]{:S(2)}, u32[]{:S(2)}) collective-permute-start(bf16[384,576]{1,0:T(8,128)(2,1)} %dynamic-slice_bitcast_fusion.8), channel_id=1, source_target_pairs={{0,8},{8,0},{1,9},{9,1},{2,10},{10,2},{3,11},{11,3},{4,12},{12,4},... | collective-permute-start | bytes 1327112 | tf_op jit(solution)/shard_map/ppermute | solution.py:24
  769.0 27.9 %collective-permute-start.52 = (bf16[128,1536]{1,0:T(8,128)(2,1)S(1)}, bf16[128,1536]{1,0:T(8,128)(2,1)S(1)}, u32[]{:S(2)}, u32[]{:S(2)}) collective-permute-start(bf16[128,1536]{1,0:T(8,128)(2,1)S(1)} %fusion.41), channel_id=1, source_target_pairs={{0,4},{4,0},{1,5},{5,1},{2,6},{6,2},{3,7},{7,3},{8,12},{12,8},{9,1... | collective-permute-start | bytes 1179656 | tf_op jit(solution)/shard_map/ppermute | solution.py:24
  824.3 31.6 %all-to-all-start.6 = ((bf16[8,48,576]{2,1,0:T(8,128)(2,1)}), bf16[8,48,576]{2,1,0:T(8,128)(2,1)S(1)}, u32[]{:S(2)}, u32[]{:S(2)}) async-start(bf16[8,48,576]{2,1,0:T(8,128)(2,1)} %bitcast.130), calls=%async_computation.10 | async-start | bytes 983040 | tf_op jit(solution)/shard_map/all_to_all | solution.py:641
  (172 other events, 1415.4 us)
Sparse Core Ops, SparseCore 0:
  43.3 52.6 all-gather.5
  130.6 33.4 all-gather.7
  196.4 59.9 all-gather.9
  264.7 45.3 all-gather.11
  312.1 38.0 all-gather.13
  458.6 71.2 reduce-scatter.4
  533.2 55.1 reduce-scatter.10
  591.3 69.8 reduce-scatter.6
  666.7 135.7 reduce-scatter.8

commit v4 on v3

--- a/solution.py
+++ b/solution.py
@@ -504,7 +504,7 @@
         caption_value_weight,
     )
     cap_team = from_team(join([by_rank(ckey_weight, 1), by_rank(cvalue_weight, 1)], axis=2))
-    w_out = both_sides(out_shard, "half", half, 0)
+    w_out = across_half(out_shard)
     cap_rows = jnp.where(half == 0, join([cap_a, cap_b]), join([cap_b, cap_a]))
     core_all, all_places = norm_rows(rows_all, clip_rows)
     all_places = jnp.transpose(all_places[:, :, :3], (2, 0, 1, 3)).reshape(3, team_rows)
@@ -521,8 +521,7 @@
     cap_half = across_half(cap_team)
     cap_all = lax.all_gather(cap_rows, TEAM, axis=0, tiled=True)
     cot_a, cot_b = own_clip(cotangent)
-    w_out = both_sides(w_out, "clip", clip_pair, 0)
-    w_out = lax.all_gather(w_out, "rep", axis=2) if reps > 1 else w_out[:, :, None]
+    w_out = both_sides(w_out, "clip", clip_pair, 0).reshape(-1, width)
     factors = lax.rsqrt(squares / width + EPSILON)[:, None, None]
     cosine, sine = rope_tables(all_places, head_dim)
     values = by_head((dot(w_scaled[:, 2 * part :], core_all, 0, 1) + bias[2 * part :]).astype(BF))
@@ -539,7 +538,7 @@
     queries, all_keys, all_values, gate_shard, up_shard, w_out = together(
         queries, all_keys, all_values, gate_weight, up_weight, w_out
     )
-    w_out = both_sides(w_out, "tz", bits[0], 3)
+    w_out = lax.all_gather(w_out, SHARDS, axis=0, tiled=True)
     ff_block = down_weight.shape[0]
     ff_part = groups * ff_block
     up_team = from_team(
@@ -547,15 +546,14 @@
     )
     o_self, logs = self_forward(queries, all_keys, all_values, 0, None)
     o_self, logs = self_forward(queries, all_keys, all_values, 1, (o_self, logs))
-    o_self, logs, cap_half, cot_a, cot_b, up_team, w_out, cap_all = together(
-        o_self, logs, cap_half, cot_a, cot_b, up_team, w_out, cap_all
+    o_self, logs, cap_half, cot_a, cot_b, up_team, cap_all = together(
+        o_self, logs, cap_half, cot_a, cot_b, up_team, cap_all
     )
     w_cap = across_clip(cap_half)
     grad_out = join([cot_a, cot_b]).astype(F32)
     d_ffn = (gate_ffn * grad_out).astype(BF)
     d_ffn_all = lax.all_gather(d_ffn, TEAM, axis=0, tiled=True)
     up_half = across_half(up_team)
-    w_out = both_sides(w_out, "ty", bits[1], 4)
     o_self, logs = self_forward(queries, all_keys, all_values, 2, (o_self, logs))
     o_self, w_cap, down_shard = together(o_self, w_cap, down_weight)
     craw = dot(w_cap, cap_all, 0, 1)
@@ -583,24 +581,30 @@
     tanh_gate = jnp.tanh(lax.dynamic_slice_in_dim(cross_gate, rank * heads, heads))
     tanh_wide = tanh_gate[:, None, None]
     mixed = (o_self + tanh_wide * o_cross).astype(BF).reshape(part, team, rows_here)
-    mixed, w_out, up_half, d_ffn_all = together(
-        jnp.transpose(mixed, (1, 0, 2)), w_out, up_half, d_ffn_all
-    )
-    w_gate_up = lax.all_gather(up_half.reshape(-1, 2 * ff_part), "clip", axis=0, tiled=True)
+    mixed, up_half, w_out = together(jnp.transpose(mixed, (1, 0, 2)), up_half, w_out)
+    w_gate_up = across_clip(up_half)
     down_half = across_half(down_shard)
-    w_out = both_sides(w_out, "tc", bits[2], 5)
     mixed = lax.all_to_all(mixed, TEAM, split_axis=0, concat_axis=0, tiled=True)
-    mixed, w_out, down_half = together(mixed, w_out, down_half)
-    combined = mixed.reshape(width, rows_here)
-    w_out = w_out.reshape(-1, width)
-    w_down = across_clip(down_half)
+    out_rows = output_weight.shape[0]
+
+    def by_shard(features):
+        tiled = features.reshape(groups, team, out_rows, -1)
+        return jnp.transpose(tiled, (1, 0, 2, 3)).reshape(width, -1)
+
+    def by_group(features):
+        tiled = features.reshape(team, groups, out_rows, -1)
+        return jnp.transpose(tiled, (1, 0, 2, 3)).reshape(width, -1)
+
+    combined = by_shard(mixed.reshape(width, rows_here))
 
     branch = dot(combined, w_out, 0, 0)
     middle = token_vals + gate_attn * branch
     factor_f = row_factor(middle)
     core_f = middle * factor_f
     ffn_in = (core_f * norm_gains[4] * (1.0 + scale_ffn) + shift_ffn).astype(BF)
-    ffn_all = lax.all_gather(after(ffn_in, w_gate_up), TEAM, axis=0, tiled=True)
+    ffn_in, down_half, d_ffn_all = together(ffn_in, down_half, d_ffn_all)
+    ffn_all = lax.all_gather(ffn_in, TEAM, axis=0, tiled=True)
+    w_down = across_clip(down_half)
     w_gate_up, w_down, ffn_all = together(w_gate_up, w_down, ffn_all)
     gate_up = dot(ffn_all, w_gate_up, 1, 0)
     gate_vals, up_vals = gate_up[:, :ff_part], gate_up[:, ff_part:]
@@ -676,7 +680,7 @@
     )
     d_branch = (gate_attn * d_middle).astype(BF)
     d_gate_attn = jnp.sum(d_middle * branch, axis=0, keepdims=True)
-    d_combined = dot(w_out, d_branch, 1, 1).astype(BF)
+    d_combined = by_group(dot(w_out, d_branch, 1, 1).astype(BF))
     d_mixed = lax.all_to_all(
         d_combined.reshape(team, part, rows_here), TEAM, split_axis=0, concat_axis=0, tiled=True
     )
@@ -707,9 +711,7 @@
     grad_output = dot(after(combined, dq_cross), d_branch, 1, 0).astype(BF)
     delta = jnp.sum(d_self.astype(F32) * o_self, axis=1, keepdims=True)
     delta, grad_output, mean_c, *out_pair = together(delta, grad_output, mean_c, *out_pair)
-    sum_output = lax.psum_scatter(
-        after(grad_output, up_rows), EVERY, scatter_dimension=0, tiled=True
-    )
+    sum_output = lax.psum_scatter(grad_output, SHARDS, scatter_dimension=0, tiled=True)
     ffn_out = join(chips_last(*out_pair, bits))
     mean_c = mean_c + swap(mean_c, "ty")
     mean_c = mean_c + swap(mean_c, "tz")
@@ -723,13 +725,16 @@
     cap_low = join([d_craw, d_cvalues]).reshape(2 * part, -1).astype(BF)
     cap_half = team_parts(dot(cap_all, cap_low, 0, 1).astype(BF))
     d_cap = dot(cap_low, w_cap, 0, 1).astype(BF)
-    d_cap = lax.psum_scatter(d_cap, TEAM, scatter_dimension=0, tiled=True).astype(F32)
     backs = self_backward(queries, d_self, logs, delta, all_keys, all_values, 1, backs)
     *backs, delta, up_rows = together(*backs, delta, up_rows)
     sum_gate_up = to_shards(up_rows)
     backs = self_backward(queries, d_self, logs, delta, all_keys, all_values, 2, backs)
-    *backs, result, sum_gate_up, cap_half = together(*backs, result, sum_gate_up, cap_half)
+    *backs, result, sum_gate_up, sum_output, cap_half = together(
+        *backs, result, sum_gate_up, sum_output, cap_half
+    )
     cap_rows = half_parts(cap_half)
+    sum_output = sum_output.reshape(lax.axis_size("clip"), clips_here, -1, width)
+    sum_output = kept_sum(sum_output, "clip", clip_pair, 0)
     dq_self, dk, dv = backs
     if reps > 1:
         dk, dv = (lax.psum_scatter(v, "rep", scatter_dimension=2, tiled=True) for v in (dk, dv))
@@ -742,7 +747,8 @@
     d_gain_qk = jnp.sum(turned_grad * normed_qk, axis=3).reshape(2, part)
     d_qk = (factors * (scaled_qk - normed_qk * mean_qk)).reshape(2 * part, team_rows)
     d_projected = join([d_qk, dv.reshape(part, team_rows)]).astype(BF)
-    d_projected, cap_rows = together(d_projected, cap_rows)
+    d_projected, sum_output = together(d_projected, sum_output)
+    sum_output = half_parts(sum_output)
 
     def attn_side(which):
         return dot(core_side(d_projected, which, 1), w_in, 0, 1).astype(BF)
@@ -783,12 +789,13 @@
     sums = both_sides(sums, "clip", clip_pair, 0)
     *pair, sums, in_half = together(*pair, sums, in_half)
     d_attn_in = join(chips_last(*pair, bits))
+    d_cap = lax.psum_scatter(after(d_cap, *pair), TEAM, scatter_dimension=0, tiled=True)
     for axis in ("ty", "tz"):
         sums = sums + swap(sums, axis)
     if reps > 1:
         sums = lax.psum(sums, "rep")
     sums = both_sides(sums, "half", half, 1)
-    d_attn_in, sums = together(d_attn_in, sums)
+    d_attn_in, sums, sum_gate_up = together(d_attn_in, sums, sum_gate_up)
     sum_gate, sum_up = ff_columns(sum_gate_up[..., :ff_part]), ff_columns(sum_gate_up[..., ff_part:])
     in_rows = half_parts(in_half)
     sum_cap = to_shards(cap_rows)
@@ -820,8 +827,8 @@
     sum_input = head_columns(sum_input, 3)
     sum_ckey = head_columns(sum_cap[..., :part], 1)
     sum_cvalue = head_columns(sum_cap[..., part:], 1)
-    sum_down, sum_output, d_cap = together(sum_down, sum_output, d_cap, d_attn_in)[:3]
-    sum_down, sum_output = sum_down.astype(F32), sum_output.astype(F32)
+    sum_down, d_cap = together(sum_down, d_cap, d_attn_in)[:2]
+    sum_down, d_cap = sum_down.astype(F32), d_cap.astype(F32)
     d_cap = d_cap.reshape(clips_here, slots_here, -1)
     d_caption = back_clip(join([pick(d_cap, half), pick(d_cap, 1 - half)]))
     return (

time: 880 us -> 845 us (0.960)
  starting transfers between devices: 111 us -> 96.5 us
    all_gather x2, waiting for transfers between devices: 20.2 us -> 0.01 us  [the longest x1 0.01 us: on_device(): w_out = lax.all_gather(w_out, SHARDS, axis=0, tiled=True)]
    ppermute x64, waiting for transfers between devices: 304 us -> 322 us  [swap(): return lax.ppermute(block, axis, [(0, 1), (1, 0)])]
    ppermute x64, starting transfers between devices: 73.5 us -> 62.6 us  [swap(): return lax.ppermute(block, axis, [(0, 1), (1, 0)])]
    select_n x13 -> x11, other arithmetic: 25.9 us -> 17.3 us  [both_sides(): jnp.where(bit == 0, jnp.stack([block, other], dim), jnp.stack([other, blo...]
    add x13 -> x14, other arithmetic: 13 us -> 19.7 us  [kept_sum(): return pick(block, bit, dim).astype(F32) + other.astype(F32)]
    unnamed x256 -> x290, local copies, waits for them, and re-layouts: 28.9 us -> 29.9 us
  transfers between devices with their start and end apart: 81 -> 81, of which waited for: 40 -> 41; matrix products, arithmetic and copies ran while one was open for 30% -> 30% of each run, Pallas kernels for 10% -> 10%
where the time goes in v4:
time: 845 us; the launch traced here: 837 us
  waiting for transfers between devices  327 us (39%)
  other arithmetic  118 us (14%)
  local copies, waits for them, and re-layouts  99.2 us (12%)
  starting transfers between devices  96.5 us (11%)
  matrix products  95.5 us (11%)
  Pallas kernels  84.9 us (10%)
  between operations  16.2 us (2%)
    ppermute x64, waiting for transfers between devices, swap(): return lax.ppermute(block, axis, [(0, 1), (1, 0)])  322 us
    dot_general x23, matrix products, dot(): return lax.dot_general(left, right, dims, preferred_element_type=F32)  95.5 us
    pallas_call x6, Pallas kernels, one_head(): pl.pallas_call(body, grid=(1, steps), in_specs=in_specs + [pl.BlockSpec(m...  66.3 us
    ppermute x64, starting transfers between devices, swap(): return lax.ppermute(block, axis, [(0, 1), (1, 0)])  62.6 us
    unnamed x290, local copies, waits for them, and re-layouts  29.9 us
    add x14, other arithmetic, kept_sum(): return pick(block, bit, dim).astype(F32) + other.astype(F32)  19.7 us
    select_n x11, other arithmetic, both_sides(): jnp.where(bit == 0, jnp.stack([block, other], dim), jnp.stack([other, blo...  17.3 us
  transfers between devices with their start and end apart: 81, of which 41 were waited for; matrix products, arithmetic and copies ran while one was open for 30% of the time, Pallas kernels for 10%

profile of v4, /device:TPU:0, one launch (start us, length us, event | category | flops | bytes accessed | tf_op | source)
XLA Modules:
  0.0 837.5 jit_solution(16349192285624695906)
XLA Ops:
  25.7 14.0 %collective-permute-done = bf16[136,1536]{1,0:T(8,128)(2,1)S(1)} collective-permute-done((bf16[136,1536]{1,0:T(8,128)(2,1)}, bf16[136,1536]{1,0:T(8,128)(2,1)S(1)}, u32[]{:S(2)}, u32[]{:S(2)}) %collective-permute-start) | collective-permute-done | bytes 417824 | tf_op jit(solution)/shard_map/ppermute | solution.py:24
  49.1 10.8 %collective-permute-done.5 = f32[1,9216]{1,0:T(1,128)S(1)} collective-permute-done((f32[1,9216]{1,0:T(1,128)S(1)}, f32[1,9216]{1,0:T(1,128)S(1)}, u32[]{:S(2)}, u32[]{:S(2)}) %collective-permute-start.5) | collective-permute-done | bytes 36896 | tf_op jit(solution)/shard_map/ppermute | solution.py:24
  73.6 15.2 %collective-permute-done.7 = bf16[768,576]{0,1:T(8,128)(2,1)} collective-permute-done((bf16[768,576]{0,1:T(8,128)(2,1)S(1)}, bf16[768,576]{0,1:T(8,128)(2,1)}, u32[]{:S(2)}, u32[]{:S(2)}) %collective-permute-start.7) | collective-permute-done | bytes 884768 | tf_op jit(solution)/shard_map/ppermute | solution.py:24
  147.1 8.2 shard_map.282
  155.3 7.7 shard_map.283
  163.0 27.7 %collective-permute-done.14 = bf16[1024,384]{1,0:T(8,128)(2,1)S(1)} collective-permute-done((bf16[1024,384]{1,0:T(8,128)(2,1)S(1)}, bf16[1024,384]{1,0:T(8,128)(2,1)S(1)}, u32[]{:S(2)}, u32[]{:S(2)}) %collective-permute-start.14) | collective-permute-done | bytes 786464 | tf_op jit(solution)/shard_map/ppermute | solution.py:24
  191.0 7.5 collective-permute-done.15
  201.7 7.6 shard_map.284
  209.4 26.1 %collective-permute-done.16 = bf16[2,1024,384]{2,1,0:T(8,128)(2,1)S(1)} collective-permute-done((bf16[2,1024,384]{2,1,0:T(8,128)(2,1)S(1)}, bf16[2,1024,384]{2,1,0:T(8,128)(2,1)S(1)}, u32[]{:S(2)}, u32[]{:S(2)}) %collective-permute-start.16) | collective-permute-done | bytes 1572896 | tf_op jit(solution)/shard_map/ppermute | solution.py:24
  263.1 19.5 %collective-permute-done.21 = bf16[128,1536]{1,0:T(8,128)(2,1)S(1)} collective-permute-done((bf16[128,1536]{1,0:T(8,128)(2,1)}, bf16[128,1536]{1,0:T(8,128)(2,1)S(1)}, u32[]{:S(2)}, u32[]{:S(2)}) %collective-permute-start.21) | collective-permute-done | bytes 393248 | tf_op jit(solution)/shard_map/ppermute | solution.py:24
  294.6 35.6 %collective-permute-done.22 = bf16[2,384,1024]{2,1,0:T(8,128)(2,1)} collective-permute-done((bf16[2,384,1024]{2,1,0:T(8,128)(2,1)}, bf16[2,384,1024]{2,1,0:T(8,128)(2,1)}, u32[]{:S(2)}, u32[]{:S(2)}) %collective-permute-start.22) | collective-permute-done | bytes 1572896 | tf_op jit(solution)/shard_map/ppermute | solution.py:24
  335.3 10.5 %collective-permute-done.23 = bf16[2,128,1536]{2,1,0:T(8,128)(2,1)} collective-permute-done((bf16[2,128,1536]{2,1,0:T(8,128)(2,1)}, bf16[2,128,1536]{2,1,0:T(8,128)(2,1)}, u32[]{:S(2)}, u32[]{:S(2)}) %collective-permute-start.23) | collective-permute-done | bytes 786464 | tf_op jit(solution)/shard_map/ppermute | solution.py:24
  348.6 9.9 %fusion.108 = f32[2048,1024]{0,1:T(8,128)S(1)} fusion(bf16[2048,1536]{1,0:T(8,128)(2,1)} %all-gather.14.cloned.1.call-done, bf16[1536,1024]{1,0:T(8,128)(2,1)} %bitcast.343), kind=kOutput, calls=%fused_computation.331 | convolution fusion | flops 6442450944 | bytes 17825792 | tf_op jit(solution)/shard_map/dot_general | solution.py:37
  358.5 8.5 %multiply_convert_fusion.1 = (bf16[2048,512]{0,1:T(8,128)(2,1)S(1)}, bf16[2048,512]{0,1:T(8,128)(2,1)S(1)}, bf16[2048,512]{0,1:T(8,128)(2,1)}) fusion(f32[2048,1024]{0,1:T(8,128)S(1)} %fusion.108, bf16[2048,1536]{1,0:T(8,128)(2,1)} %all-gather.12.cloned.1.call-done, bf16[512,1536]{1,0:T(8,128)(2,1)S(1)} %bitcast.376), kind=kOutput, calls=%fused_computation.14 | convolution fusion | flops 3235905536 | bytes 22544384 | tf_op jit(solution)/shard_map/dot_general | solution.py:37
  372.0 6.0 collective-permute-done.24
  378.0 6.9 add_convert_fusion.2
  388.5 7.6 convolution_convert_fusion.10
  396.1 10.1 %collective-permute-done.26 = bf16[2,128,1536]{2,1,0:T(8,128)(2,1)} collective-permute-done((bf16[2,128,1536]{2,1,0:T(8,128)(2,1)}, bf16[2,128,1536]{2,1,0:T(8,128)(2,1)}, u32[]{:S(2)}, u32[]{:S(2)}) %collective-permute-start.26) | collective-permute-done | bytes 786464 | tf_op jit(solution)/shard_map/ppermute | solution.py:24
  444.8 10.5 %convolution_convert_fusion.3 = bf16[1536,1024]{1,0:T(8,128)(2,1)} fusion(bf16[2048,1536]{1,0:T(8,128)(2,1)} %all-gather.14.cloned.1.call-done, bf16[2048,1024]{0,1:T(8,128)(2,1)S(1)} %copy-done.42), kind=kOutput, calls=%fused_computation.21 | convolution fusion | flops 6444023808 | bytes 13631488 | tf_op jit(solution)/shard_map/dot_general | solution.py:37
  468.0 9.4 %shard_map.286 = (f32[3,64,2048]{2,1,0:T(8,128)}, f32[3,64,256]{2,1,0:T(8,128)}, f32[3,64,256]{2,1,0:T(8,128)}, f32[3,1,2048]{2,1,0:T(1,128)}) custom-call(bf16[3,64,2048]{2,1,0:T(8,128)(2,1)} %get-tuple-element.158.refs_0_.q_ref, bf16[3,64,2048]{2,1,0:T(8,128)(2,1)} %reshape_reshape.11.g_ref.refs_1_, bf16[3,64,256]{2,1,0:T(8,128)(2,1)} %multiply_convert_fusion.8.k_ref, ...), custom_call_target="tpu_custom_call" | custom-call | flops 4026531840 | bytes 786432 | tf_op jit(solution)/shard_map/pallas_call | solution.py:306
  488.7 8.5 %collective-permute-done.31 = bf16[2,128,1536]{2,1,0:T(8,128)(2,1)} collective-permute-done((bf16[2,128,1536]{2,1,0:T(8,128)(2,1)}, bf16[2,128,1536]{2,1,0:T(8,128)(2,1)}, u32[]{:S(2)}, u32[]{:S(2)}) %collective-permute-start.31) | collective-permute-done | bytes 786464 | tf_op jit(solution)/shard_map/ppermute | solution.py:24
  509.1 6.8 collective-permute-done.33
  516.5 14.4 %shard_map.287 = (f32[3,64,2048]{2,1,0:T(8,128)}, f32[3,64,2048]{2,1,0:T(8,128)}, f32[3,64,2048]{2,1,0:T(8,128)}) custom-call(bf16[3,64,2048]{2,1,0:T(8,128)(2,1)} %get-tuple-element.158.refs_0_.q_ref, bf16[3,64,2048]{2,1,0:T(8,128)(2,1)} %reshape_reshape.11.g_ref.refs_1_, f32[3,1,2048]{2,1,0:T(1,128)} %get-tuple-element.202.refs_2_, ...), custom_call_target="tpu_custom_call" | custom-call | flops 10737418240 | bytes 2097152 | tf_op jit(solution)/shard_map/pallas_call | solution.py:231
  540.2 14.3 %shard_map.288 = (f32[3,64,2048]{2,1,0:T(8,128)}, f32[3,64,2048]{2,1,0:T(8,128)}, f32[3,64,2048]{2,1,0:T(8,128)}) custom-call(bf16[3,64,2048]{2,1,0:T(8,128)(2,1)} %get-tuple-element.158.refs_0_.q_ref, bf16[3,64,2048]{2,1,0:T(8,128)(2,1)} %reshape_reshape.11.g_ref.refs_1_, ...), custom_call_target="tpu_custom_call", output_to_operand_aliasing={{0}: (6, {}), {1}: (7, {}), {2}: (8, {})} | custom-call | flops 10737418240 | bytes 2097152 | tf_op jit(solution)/shard_map/pallas_call | solution.py:231
  561.9 11.1 %collective-permute-done.38 = bf16[2,1024,384]{2,1,0:T(8,128)(2,1)} collective-permute-done((bf16[2,1024,384]{2,1,0:T(8,128)(2,1)}, bf16[2,1024,384]{2,1,0:T(8,128)(2,1)}, u32[]{:S(2)}, u32[]{:S(2)}) %collective-permute-start.38) | collective-permute-done | bytes 1572896 | tf_op jit(solution)/shard_map/ppermute | solution.py:24
  576.4 14.1 %shard_map.289 = (f32[3,64,2048]{2,1,0:T(8,128)}, f32[3,64,2048]{2,1,0:T(8,128)}, f32[3,64,2048]{2,1,0:T(8,128)}) custom-call(bf16[3,64,2048]{2,1,0:T(8,128)(2,1)} %get-tuple-element.158.refs_0_.q_ref, bf16[3,64,2048]{2,1,0:T(8,128)(2,1)} %reshape_reshape.11.g_ref.refs_1_, ...), custom_call_target="tpu_custom_call", output_to_operand_aliasing={{0}: (6, {}), {1}: (7, {}), {2}: (8, {})} | custom-call | flops 10737418240 | bytes 2097152 | tf_op jit(solution)/shard_map/pallas_call | solution.py:231
  603.8 15.7 %collective-permute-done.40 = f32[2,2048]{1,0:T(2,128)S(1)} collective-permute-done((f32[2,2048]{1,0:T(2,128)S(1)}, f32[2,2048]{1,0:T(2,128)S(1)}, u32[]{:S(2)}, u32[]{:S(2)}) %collective-permute-start.40) | collective-permute-done | bytes 16416 | tf_op jit(solution)/shard_map/ppermute | solution.py:24
  639.5 11.7 %collective-permute-done.63 = bf16[1024,384]{1,0:T(8,128)(2,1)} collective-permute-done((bf16[1024,384]{1,0:T(8,128)(2,1)}, bf16[1024,384]{1,0:T(8,128)(2,1)}, u32[]{:S(2)}, u32[]{:S(2)}) %collective-permute-start.63) | collective-permute-done | bytes 786464 | tf_op jit(solution)/shard_map/ppermute | solution.py:24
  710.9 5.9 collective-permute-done.44
  740.3 15.7 %collective-permute-done.52 = f32[2,12,1536]{2,1,0:T(8,128)S(1)} collective-permute-done((f32[2,12,1536]{2,1,0:T(8,128)S(1)}, f32[2,12,1536]{2,1,0:T(8,128)S(1)}, u32[]{:S(2)}, u32[]{:S(2)}) %collective-permute-start.52) | collective-permute-done | bytes 147488 | tf_op jit(solution)/shard_map/ppermute | solution.py:24
  759.7 13.6 %collective-permute-done.50 = bf16[128,1536]{1,0:T(8,128)(2,1)} collective-permute-done((bf16[128,1536]{1,0:T(8,128)(2,1)}, bf16[128,1536]{1,0:T(8,128)(2,1)}, u32[]{:S(2)}, u32[]{:S(2)}) %collective-permute-start.50) | collective-permute-done | bytes 393248 | tf_op jit(solution)/shard_map/ppermute | solution.py:24
  822.5 7.5 collective-permute-done.55
  (695 shorter events, 422.8 us)
Async XLA Ops:
  25.5 70.5 %all-gather.6.cloned.1.call-start = ((), (), s32[]{:S(2)}) async-start(), calls=%async_computation.12 | async-start | bytes 7520256 | tf_op jit(solution)/shard_map/all_gather | solution.py:474
  43.2 24.3 %collective-permute-start.3 = (bf16[384,576]{1,0:T(8,128)(2,1)S(1)}, bf16[384,576]{1,0:T(8,128)(2,1)S(1)}, u32[]{:S(2)}, u32[]{:S(2)}) collective-permute-start(bf16[384,576]{1,0:T(8,128)(2,1)S(1)} %bitcast.364), channel_id=1, source_target_pairs={{0,8},{8,0},{1,9},{9,1},{2,10},{10,2},{3,11},{11,3},{4,12},{12,4},... | collective-permute-start | bytes 1327112 | tf_op jit(solution)/shard_map/ppermute | solution.py:24
  96.0 31.8 %collective-permute-start.12 = (bf16[48,1536]{1,0:T(8,128)(2,1)}, bf16[48,1536]{1,0:T(8,128)(2,1)S(1)}, u32[]{:S(2)}, u32[]{:S(2)}) collective-permute-start(bf16[48,1536]{1,0:T(8,128)(2,1)} %param.27), channel_id=1, source_target_pairs={{0,8},{8,0},{1,9},{9,1},{2,10},{10,2},{3,11},{11,3},{4,12},{12,4},... | collective-permute-start | bytes 442376 | tf_op jit(solution)/shard_map/ppermute | solution.py:24
  99.1 28.9 %all-to-all-start.1 = ((bf16[8,128,384]{1,2,0:T(8,128)(2,1)}), bf16[8,128,384]{1,2,0:T(8,128)(2,1)S(1)}, u32[]{:S(2)}, u32[]{:S(2)}) async-start(bf16[8,128,384]{1,2,0:T(8,128)(2,1)} %pad_maximum_fusion.7), calls=%async_computation.1 | async-start | bytes 1572864 | tf_op jit(solution)/shard_map/all_to_all | solution.py:447
  104.9 93.7 %all-gather.8.cloned.1.call-start = ((), (), s32[]{:S(2)}) async-start(), calls=%async_computation.13 | async-start | bytes 2359296 | tf_op jit(solution)/shard_map/all_gather | solution.py:522
  128.3 129.3 %all-gather.10.cloned.1.call-start = ((), (), s32[]{:S(2)}) async-start(), calls=%async_computation.14 | async-start | bytes 5308416 | tf_op jit(solution)/shard_map/all_gather | solution.py:541
  139.7 58.9 %all-to-all-start.2 = ((bf16[8,48,1024]{2,1,0:T(8,128)(2,1)}), bf16[8,48,1024]{2,1,0:T(8,128)(2,1)}, u32[]{:S(2)}, u32[]{:S(2)}) async-start(bf16[8,48,1024]{2,1,0:T(8,128)(2,1)} %pad_maximum_fusion.8), calls=%async_computation.2 | async-start | bytes 1572864 | tf_op jit(solution)/shard_map/all_to_all | solution.py:447
  143.9 148.6 %all-gather.12.cloned.1.call-start = ((), (), s32[]{:S(2)}) async-start(), calls=%async_computation.15 | async-start | bytes 7077888 | tf_op jit(solution)/shard_map/all_gather | solution.py:555
  144.0 46.7 %collective-permute-start.14 = (bf16[1024,384]{1,0:T(8,128)(2,1)S(1)}, bf16[1024,384]{1,0:T(8,128)(2,1)S(1)}, u32[]{:S(2)}, u32[]{:S(2)}) collective-permute-start(bf16[1024,384]{1,0:T(8,128)(2,1)S(1)} %bitcast.360), channel_id=1, source_target_pairs={{0,8},{8,0},{1,9},{9,1},{2,10},{10,2},{3,11},{11,3},{4,12},{12,4},... | collective-permute-start | bytes 2359304 | tf_op jit(solution)/shard_map/ppermute | solution.py:24
  144.2 54.3 %collective-permute-start.15 = (bf16[128,1536]{1,0:T(8,128)(2,1)S(1)}, bf16[128,1536]{1,0:T(8,128)(2,1)S(1)}, u32[]{:S(2)}, u32[]{:S(2)}) collective-permute-start(bf16[128,1536]{1,0:T(8,128)(2,1)S(1)} %get-tuple-element.406), channel_id=1, source_target_pairs={{0,8},{8,0},{1,9},{9,1},{2,10},{10,2},{3,11},{11,3},{4,12},{12,4},... | collective-permute-start | bytes 1179656 | tf_op jit(solution)/shard_map/ppermute | solution.py:24
  199.6 35.8 %collective-permute-start.16 = (bf16[2,1024,384]{2,1,0:T(8,128)(2,1)S(1)}, bf16[2,1024,384]{2,1,0:T(8,128)(2,1)S(1)}, u32[]{:S(2)}, u32[]{:S(2)}) collective-permute-start(bf16[2,1024,384]{2,1,0:T(8,128)(2,1)S(1)} %maximum_select_fusion.2), channel_id=1, source_target_pairs={{0,16},{16,0},{1,17},{17,1},{2,18},{18,2},{3,19},{19,3},{4,20},{20... | collective-permute-start | bytes 4718600 | tf_op jit(solution)/shard_map/ppermute | solution.py:24
  201.7 42.9 %collective-permute-start.20 = (bf16[384,1024]{1,0:T(8,128)(2,1)}, bf16[384,1024]{1,0:T(8,128)(2,1)}, u32[]{:S(2)}, u32[]{:S(2)}) collective-permute-start(bf16[384,1024]{1,0:T(8,128)(2,1)} %bitcast.44), channel_id=1, source_target_pairs={{0,8},{8,0},{1,9},{9,1},{2,10},{10,2},{3,11},{11,3},{4,12},{12,4},... | collective-permute-start | bytes 2359304 | tf_op jit(solution)/shard_map/ppermute | solution.py:24
  257.6 27.3 %all-to-all-start.3 = ((bf16[8,192,256]{2,1,0:T(8,128)(2,1)}), bf16[8,192,256]{2,1,0:T(8,128)(2,1)S(1)}, u32[]{:S(2)}, u32[]{:S(2)}) async-start(bf16[8,192,256]{2,1,0:T(8,128)(2,1)} %bitcast.314), calls=%async_computation.3 | async-start | bytes 1572864 | tf_op jit(solution)/shard_map/all_to_all | solution.py:587
  261.5 87.1 %all-gather.14.cloned.1.call-start = ((), (), s32[]{:S(2)}) async-start(), calls=%async_computation.16 | async-start | bytes 7077888 | tf_op jit(solution)/shard_map/all_gather | solution.py:606
  292.6 37.7 %collective-permute-start.22 = (bf16[2,384,1024]{2,1,0:T(8,128)(2,1)}, bf16[2,384,1024]{2,1,0:T(8,128)(2,1)}, u32[]{:S(2)}, u32[]{:S(2)}) collective-permute-start(bf16[2,384,1024]{2,1,0:T(8,128)(2,1)} %maximum_select_fusion.3), channel_id=1, source_target_pairs={{0,16},{16,0},{1,17},{17,1},{2,18},{18,2},{3,19},{19,3},{4,20},{20... | collective-permute-start | bytes 4718600 | tf_op jit(solution)/shard_map/ppermute | solution.py:24
  294.0 51.7 %collective-permute-start.23 = (bf16[2,128,1536]{2,1,0:T(8,128)(2,1)}, bf16[2,128,1536]{2,1,0:T(8,128)(2,1)}, u32[]{:S(2)}, u32[]{:S(2)}) collective-permute-start(bf16[2,128,1536]{2,1,0:T(8,128)(2,1)} %maximum_select_fusion.7), channel_id=1, source_target_pairs={{0,16},{16,0},{1,17},{17,1},{2,18},{18,2},{3,19},{19,3},{4,20},{20... | collective-permute-start | bytes 2359304 | tf_op jit(solution)/shard_map/ppermute | solution.py:24
  439.2 117.9 %reduce-scatter.5.cloned.1.call-start = ((), (), s32[]{:S(2)}) async-start(), calls=%async_computation.17 | async-start | bytes 3932160 | tf_op jit(solution)/shard_map/reduce_scatter | solution.py:658
  455.2 135.3 %reduce-scatter.7.cloned.1.call-start = ((), (), s32[]{:S(2)}) async-start(), calls=%async_computation.18 | async-start | bytes 5308416 | tf_op jit(solution)/shard_map/reduce_scatter | solution.py:714
  458.4 27.6 %collective-permute-start.32 = (bf16[2,128,1536]{2,1,0:T(8,128)(2,1)}, bf16[2,128,1536]{2,1,0:T(8,128)(2,1)}, u32[]{:S(2)}, u32[]{:S(2)}) collective-permute-start(bf16[2,128,1536]{2,1,0:T(8,128)(2,1)} %dynamic-slice_bitcast_fusion.4), channel_id=1, source_target_pairs={{0,2},{2,0},{1,3},{3,1},{4,6},{6,4},{5,7},{7,5},{8,10},{10,8},{9,1... | collective-permute-start | bytes 2359304 | tf_op jit(solution)/shard_map/ppermute | solution.py:24
  461.2 35.9 %collective-permute-start.31 = (bf16[2,128,1536]{2,1,0:T(8,128)(2,1)}, bf16[2,128,1536]{2,1,0:T(8,128)(2,1)}, u32[]{:S(2)}, u32[]{:S(2)}) collective-permute-start(bf16[2,128,1536]{2,1,0:T(8,128)(2,1)} %dynamic-slice_bitcast_fusion.5), channel_id=1, source_target_pairs={{0,4},{4,0},{1,5},{5,1},{2,6},{6,2},{3,7},{7,3},{8,12},{12,8},{9,1... | collective-permute-start | bytes 2359304 | tf_op jit(solution)/shard_map/ppermute | solution.py:24
  499.8 319.8 %reduce-scatter.9.cloned.1.call-start = ((), (), s32[]{:S(2)}) async-start(), calls=%async_computation.19 | async-start | bytes 1966080 | tf_op jit(solution)/shard_map/reduce_scatter | solution.py:658
  505.3 25.6 %collective-permute-start.35 = (bf16[128,1536]{1,0:T(8,128)(2,1)S(1)}, bf16[128,1536]{1,0:T(8,128)(2,1)S(1)}, u32[]{:S(2)}, u32[]{:S(2)}) collective-permute-start(bf16[128,1536]{1,0:T(8,128)(2,1)S(1)} %fusion.39), channel_id=1, source_target_pairs={{0,2},{2,0},{1,3},{3,1},{4,6},{6,4},{5,7},{7,5},{8,10},{10,8},{9,1... | collective-permute-start | bytes 1179656 | tf_op jit(solution)/shard_map/ppermute | solution.py:24
  538.0 34.9 %collective-permute-start.38 = (bf16[2,1024,384]{2,1,0:T(8,128)(2,1)}, bf16[2,1024,384]{2,1,0:T(8,128)(2,1)}, u32[]{:S(2)}, u32[]{:S(2)}) collective-permute-start(bf16[2,1024,384]{2,1,0:T(8,128)(2,1)} %dynamic-slice_bitcast_fusion), channel_id=1, source_target_pairs={{0,16},{16,0},{1,17},{17,1},{2,18},{18,2},{3,19},{19,3},{4,20},{20... | collective-permute-start | bytes 4718600 | tf_op jit(solution)/shard_map/ppermute | solution.py:24
  557.1 33.4 %all-to-all-start.5 = ((bf16[8,48,1024]{2,1,0:T(8,128)(2,1)}), bf16[8,48,1024]{2,1,0:T(8,128)(2,1)S(1)}, u32[]{:S(2)}, u32[]{:S(2)}) async-start(bf16[8,48,1024]{2,1,0:T(8,128)(2,1)} %bitcast.384), calls=%async_computation.6 | async-start | bytes 1572864 | tf_op jit(solution)/shard_map/all_to_all | solution.py:645
  600.2 51.1 %collective-permute-start.63 = (bf16[1024,384]{1,0:T(8,128)(2,1)}, bf16[1024,384]{1,0:T(8,128)(2,1)}, u32[]{:S(2)}, u32[]{:S(2)}) collective-permute-start(bf16[1024,384]{1,0:T(8,128)(2,1)} %dynamic-slice_bitcast_fusion.1), channel_id=1, source_target_pairs={{0,8},{8,0},{1,9},{9,1},{2,10},{10,2},{3,11},{11,3},{4,12},{12,4},... | collective-permute-start | bytes 2359304 | tf_op jit(solution)/shard_map/ppermute | solution.py:24
  602.2 24.8 %collective-permute-start.42 = (bf16[2,48,1536]{2,1,0:T(8,128)(2,1)}, bf16[2,48,1536]{2,1,0:T(8,128)(2,1)}, u32[]{:S(2)}, u32[]{:S(2)}) collective-permute-start(bf16[2,48,1536]{2,1,0:T(8,128)(2,1)} %dynamic-slice_bitcast_fusion.13), channel_id=1, source_target_pairs={{0,16},{16,0},{1,17},{17,1},{2,18},{18,2},{3,19},{19,3},{4,20},{20... | collective-permute-start | bytes 884744 | tf_op jit(solution)/shard_map/ppermute | solution.py:24
  633.8 40.0 %collective-permute-start.43 = (bf16[1024,1536]{1,0:T(8,128)(2,1)}, bf16[1024,1536]{1,0:T(8,128)(2,1)}, u32[]{:S(2)}, u32[]{:S(2)}) collective-permute-start(bf16[1024,1536]{1,0:T(8,128)(2,1)} %convolution_convert_fusion.4), channel_id=1, source_target_pairs={{0,1},{1,0},{2,3},{3,2},{4,5},{5,4},{6,7},{7,6},{8,9},{9,8},{10,11... | collective-permute-start | bytes 9437192 | tf_op jit(solution)/shard_map/ppermute | solution.py:24
  657.3 162.2 %reduce-scatter.11.cloned.1.call-start = ((), (), s32[]{:S(2)}) async-start(), calls=%async_computation.20 | async-start | bytes 2359296 | tf_op jit(solution)/shard_map/reduce_scatter | solution.py:792
  728.5 29.9 %collective-permute-start.49 = (bf16[128,1536]{1,0:T(8,128)(2,1)}, bf16[128,1536]{1,0:T(8,128)(2,1)}, u32[]{:S(2)}, u32[]{:S(2)}) collective-permute-start(bf16[128,1536]{1,0:T(8,128)(2,1)} %fusion.41), channel_id=1, source_target_pairs={{0,2},{2,0},{1,3},{3,1},{4,6},{6,4},{5,7},{7,5},{8,10},{10,8},{9,1... | collective-permute-start | bytes 1179656 | tf_op jit(solution)/shard_map/ppermute | solution.py:24
  735.4 55.7 %collective-permute-start.61 = (bf16[384,576]{1,0:T(8,128)(2,1)}, bf16[384,576]{1,0:T(8,128)(2,1)}, u32[]{:S(2)}, u32[]{:S(2)}) collective-permute-start(bf16[384,576]{1,0:T(8,128)(2,1)} %dynamic-slice_bitcast_fusion.8), channel_id=1, source_target_pairs={{0,8},{8,0},{1,9},{9,1},{2,10},{10,2},{3,11},{11,3},{4,12},{12,4},... | collective-permute-start | bytes 1327112 | tf_op jit(solution)/shard_map/ppermute | solution.py:24
  740.0 33.3 %collective-permute-start.50 = (bf16[128,1536]{1,0:T(8,128)(2,1)}, bf16[128,1536]{1,0:T(8,128)(2,1)}, u32[]{:S(2)}, u32[]{:S(2)}) collective-permute-start(bf16[128,1536]{1,0:T(8,128)(2,1)} %fusion.42), channel_id=1, source_target_pairs={{0,4},{4,0},{1,5},{5,1},{2,6},{6,2},{3,7},{7,3},{8,12},{12,8},{9,1... | collective-permute-start | bytes 1179656 | tf_op jit(solution)/shard_map/ppermute | solution.py:24
  780.2 33.2 %collective-permute-start.54 = (bf16[128,1536]{1,0:T(8,128)(2,1)S(1)}, bf16[128,1536]{1,0:T(8,128)(2,1)}, u32[]{:S(2)}, u32[]{:S(2)}) collective-permute-start(bf16[128,1536]{1,0:T(8,128)(2,1)S(1)} %slice.346), channel_id=1, source_target_pairs={{0,8},{8,0},{1,9},{9,1},{2,10},{10,2},{3,11},{11,3},{4,12},{12,4},... | collective-permute-start | bytes 1179656 | tf_op jit(solution)/shard_map/ppermute | solution.py:24
  (189 other events, 1377.8 us)
Sparse Core Ops, SparseCore 0:
  43.3 52.6 all-gather.5
  128.4 31.0 all-gather.7
  161.8 50.6 all-gather.9
  214.5 50.3 all-gather.11
  292.7 36.9 all-gather.13
  455.4 69.3 reduce-scatter.4
  527.1 60.1 reduce-scatter.6
  590.2 70.4 reduce-scatter.8
  740.4 60.6 reduce-scatter.10

commit v5 on v4

--- a/solution.py
+++ b/solution.py
@@ -159,6 +159,52 @@
         ],
         compiler_params=pltpu.CompilerParams(vmem_limit_bytes=48 * 1024 * 1024),
     )(jnp.reshape(bit, (1,)).astype(jnp.int32), mine, other, scale, shift)
+
+
+def input_grad_kernel(
+    core_ref, grad_ref, w_ref, scale_ref, shift_ref, out_ref, moment_ref, sum_ref, column_sum
+):
+    @pl.when(pl.program_id(0) == 0)
+    def _():
+        column_sum[...] = jnp.sum(grad_ref[...].astype(F32), axis=1, keepdims=True)
+
+    weight = w_ref[...].astype(F32)
+    product = dot(grad_ref[...], core_ref[...], 1, 0)
+    moment_ref[...] = jnp.sum(product * weight, axis=0, keepdims=True)
+    sum_ref[...] = jnp.sum(column_sum[...] * weight, axis=0, keepdims=True)
+    out_ref[...] = jnp.transpose(
+        product * scale_ref[...] + column_sum[...] * shift_ref[...]
+    ).astype(BF)
+
+
+def input_grad(core, grad, weight_t, scale, shift):
+    rows, width = core.shape
+    columns = grad.shape[0]
+    block = width // 4
+
+    def across(count):
+        return pl.BlockSpec((count, block), lambda i: (0, i))
+
+    return pl.pallas_call(
+        input_grad_kernel,
+        grid=(4,),
+        in_specs=[
+            across(rows),
+            pl.BlockSpec((columns, rows), lambda i: (0, 0)),
+            across(columns),
+            across(1),
+            across(1),
+        ],
+        out_specs=[pl.BlockSpec((block, columns), lambda i: (i, 0)), across(1), across(1)],
+        out_shape=[jax.ShapeDtypeStruct((width, columns), BF), f32(1, width), f32(1, width)],
+        scratch_shapes=[pltpu.VMEM((columns, 1), F32)],
+        compiler_params=pltpu.CompilerParams(vmem_limit_bytes=48 * 1024 * 1024),
+        cost_estimate=pl.CostEstimate(
+            flops=2 * rows * width * columns,
+            transcendentals=0,
+            bytes_accessed=2 * (rows * width + rows * columns + 2 * width * columns),
+        ),
+    )(core, grad, weight_t, scale, shift)
 
 
 def norm_rows_kernel(rows_ref, core_ref, places_ref):
@@ -476,12 +522,13 @@
     if reps > 1:
         mod_own = lax.psum(mod_own, "rep")
     mod_own = team_sum(mod_own)
-    in_half, mod_own, caption = together(in_half, mod_own, caption)
+    in_half, mod_own, caption, cotangent = together(in_half, mod_own, caption, cotangent)
 
     in_other = swap(in_half, "clip")
     rows_cap = caption_key_weight.shape[0]
     slots_here = caption.shape[1]
     cap_a, cap_b = own_clip(caption)
+    cot_a, cot_b = own_clip(cotangent)
     modulation = mod_own + modulation_bias
     shift_attn, scale_attn, gate_attn, shift_ffn, scale_ffn, gate_ffn = (
         modulation[:, i * width : (i + 1) * width] for i in range(6)
@@ -515,12 +562,11 @@
     raw_qk = dot(w_scaled[:, : 2 * part], core_all, 0, 1) + bias[: 2 * part]
     raw_qk = raw_qk.reshape(2, heads, head_dim, team_rows)
     squares = jnp.sum(raw_qk * raw_qk, axis=(1, 2))
-    squares, raw_qk, cap_team, cap_rows, cotangent, w_out = together(
-        team_sum(squares), raw_qk, cap_team, cap_rows, cotangent, w_out
+    squares, raw_qk, cap_team, cap_rows, cot_a, cot_b, w_out = together(
+        team_sum(squares), raw_qk, cap_team, cap_rows, cot_a, cot_b, w_out
     )
     cap_half = across_half(cap_team)
     cap_all = lax.all_gather(cap_rows, TEAM, axis=0, tiled=True)
-    cot_a, cot_b = own_clip(cotangent)
     w_out = both_sides(w_out, "clip", clip_pair, 0).reshape(-1, width)
     factors = lax.rsqrt(squares / width + EPSILON)[:, None, None]
     cosine, sine = rope_tables(all_places, head_dim)
@@ -535,8 +581,8 @@
     if reps > 1:
         all_keys, all_values = (lax.all_gather(v, "rep", axis=2, tiled=True) for v in (keys, values))
 
-    queries, all_keys, all_values, gate_shard, up_shard, w_out = together(
-        queries, all_keys, all_values, gate_weight, up_weight, w_out
+    queries, all_keys, all_values, gate_shard, up_shard, w_out, w_in_t = together(
+        queries, all_keys, all_values, gate_weight, up_weight, w_out, jnp.transpose(w_in)
     )
     w_out = lax.all_gather(w_out, SHARDS, axis=0, tiled=True)
     ff_block = down_weight.shape[0]
@@ -546,16 +592,16 @@
     )
     o_self, logs = self_forward(queries, all_keys, all_values, 0, None)
     o_self, logs = self_forward(queries, all_keys, all_values, 1, (o_self, logs))
-    o_self, logs, cap_half, cot_a, cot_b, up_team, cap_all = together(
-        o_self, logs, cap_half, cot_a, cot_b, up_team, cap_all
-    )
+    o_self, logs, cap_half, up_team, cap_all = together(o_self, logs, cap_half, up_team, cap_all)
     w_cap = across_clip(cap_half)
     grad_out = join([cot_a, cot_b]).astype(F32)
     d_ffn = (gate_ffn * grad_out).astype(BF)
     d_ffn_all = lax.all_gather(d_ffn, TEAM, axis=0, tiled=True)
     up_half = across_half(up_team)
     o_self, logs = self_forward(queries, all_keys, all_values, 2, (o_self, logs))
-    o_self, w_cap, down_shard = together(o_self, w_cap, down_weight)
+    o_self, w_cap, up_half, down_shard = together(o_self, w_cap, up_half, down_weight)
+    w_gate_up = across_clip(up_half)
+    down_half = across_half(down_shard)
     craw = dot(w_cap, cap_all, 0, 1)
     craw_key = by_head(craw[:part])
     square_c = jnp.sum(craw_key * craw_key, axis=(0, 1))[None]
@@ -581,9 +627,8 @@
     tanh_gate = jnp.tanh(lax.dynamic_slice_in_dim(cross_gate, rank * heads, heads))
     tanh_wide = tanh_gate[:, None, None]
     mixed = (o_self + tanh_wide * o_cross).astype(BF).reshape(part, team, rows_here)
-    mixed, up_half, w_out = together(jnp.transpose(mixed, (1, 0, 2)), up_half, w_out)
-    w_gate_up = across_clip(up_half)
-    down_half = across_half(down_shard)
+    mixed, w_out, down_half = together(jnp.transpose(mixed, (1, 0, 2)), w_out, down_half)
+    w_down = across_clip(down_half)
     mixed = lax.all_to_all(mixed, TEAM, split_axis=0, concat_axis=0, tiled=True)
     out_rows = output_weight.shape[0]
 
@@ -602,9 +647,8 @@
     factor_f = row_factor(middle)
     core_f = middle * factor_f
     ffn_in = (core_f * norm_gains[4] * (1.0 + scale_ffn) + shift_ffn).astype(BF)
-    ffn_in, down_half, d_ffn_all = together(ffn_in, down_half, d_ffn_all)
+    ffn_in, w_down, d_ffn_all = together(ffn_in, w_down, d_ffn_all)
     ffn_all = lax.all_gather(ffn_in, TEAM, axis=0, tiled=True)
-    w_down = across_clip(down_half)
     w_gate_up, w_down, ffn_all = together(w_gate_up, w_down, ffn_all)
     gate_up = dot(ffn_all, w_gate_up, 1, 0)
     gate_vals, up_vals = gate_up[:, :ff_part], gate_up[:, ff_part:]
@@ -662,7 +706,6 @@
     pair = chips_first(*by_chip(mine), bits)
     grad_down = dot(after(hidden, mine), d_ffn_all, 0, 0).astype(BF)
     *pair, grad_down = together(*pair, grad_down)
-    sum_down = all_parts(grad_down)
     d_ffn_in = join(chips_last(*pair, bits))
     late_hidden = after(hidden, grad_down)
     out_sent = dot(core_side(late_hidden, 1 - bits[2]), w_down, 1, 0).astype(BF)
@@ -670,6 +713,7 @@
     d_ffn_in, out_sent, out_kept = together(d_ffn_in, out_sent, out_kept)
 
     out_mine = add_core(out_kept, out_sent)
+    down_half = team_parts(after(grad_down, d_ffn_in))
     d_shift_ffn = jnp.sum(d_ffn_in, axis=0, keepdims=True)
     moment_f = jnp.sum(d_ffn_in * core_f, axis=0, keepdims=True)
     d_scale_ffn = moment_f * norm_gains[4]
@@ -710,7 +754,10 @@
     mean_c = mean_c + swap(mean_c, "tc")
     grad_output = dot(after(combined, dq_cross), d_branch, 1, 0).astype(BF)
     delta = jnp.sum(d_self.astype(F32) * o_self, axis=1, keepdims=True)
-    delta, grad_output, mean_c, *out_pair = together(delta, grad_output, mean_c, *out_pair)
+    delta, grad_output, mean_c, down_half, *out_pair = together(
+        delta, grad_output, mean_c, down_half, *out_pair
+    )
+    sum_down = half_parts(down_half)
     sum_output = lax.psum_scatter(grad_output, SHARDS, scatter_dimension=0, tiled=True)
     ffn_out = join(chips_last(*out_pair, bits))
     mean_c = mean_c + swap(mean_c, "ty")
@@ -725,16 +772,18 @@
     cap_low = join([d_craw, d_cvalues]).reshape(2 * part, -1).astype(BF)
     cap_half = team_parts(dot(cap_all, cap_low, 0, 1).astype(BF))
     d_cap = dot(cap_low, w_cap, 0, 1).astype(BF)
+    d_cap = d_cap.reshape(2, 2, 2, clips_here * slots_here, -1)
+    d_cap = kept_sum(d_cap, "tc", bits[2], 0).astype(BF)
     backs = self_backward(queries, d_self, logs, delta, all_keys, all_values, 1, backs)
-    *backs, delta, up_rows = together(*backs, delta, up_rows)
+    *backs, delta, up_rows, sum_down, d_cap, cap_half = together(
+        *backs, delta, up_rows, sum_down, d_cap, cap_half
+    )
+    cap_rows = half_parts(cap_half)
+    d_cap = kept_sum(d_cap, "tz", bits[0], 0).astype(BF)
     sum_gate_up = to_shards(up_rows)
     backs = self_backward(queries, d_self, logs, delta, all_keys, all_values, 2, backs)
-    *backs, result, sum_gate_up, sum_output, cap_half = together(
-        *backs, result, sum_gate_up, sum_output, cap_half
-    )
-    cap_rows = half_parts(cap_half)
-    sum_output = sum_output.reshape(lax.axis_size("clip"), clips_here, -1, width)
-    sum_output = kept_sum(sum_output, "clip", clip_pair, 0)
+    *backs, result, sum_gate_up, d_cap = together(*backs, result, sum_gate_up, d_cap)
+    d_cap = kept_sum(d_cap, "ty", bits[1], 0).astype(BF)
     dq_self, dk, dv = backs
     if reps > 1:
         dk, dv = (lax.psum_scatter(v, "rep", scatter_dimension=2, tiled=True) for v in (dk, dv))
@@ -747,22 +796,18 @@
     d_gain_qk = jnp.sum(turned_grad * normed_qk, axis=3).reshape(2, part)
     d_qk = (factors * (scaled_qk - normed_qk * mean_qk)).reshape(2 * part, team_rows)
     d_projected = join([d_qk, dv.reshape(part, team_rows)]).astype(BF)
-    d_projected, sum_output = together(d_projected, sum_output)
-    sum_output = half_parts(sum_output)
 
     def attn_side(which):
         return dot(core_side(d_projected, which, 1), w_in, 0, 1).astype(BF)
 
     side_sent = attn_side(1 - bits[2])
     mine = add_core(attn_side(bits[2]), side_sent)
-    core_grad = dot(core_all, d_projected, 0, 1)
-    column_sum = dot(d_projected, jnp.ones((team_rows, 128), BF), 1, 0)[:, 0][None]
-    mine, core_grad = together(mine, core_grad)
+    in_grad, moment_a, d_shift_attn = input_grad(
+        core_all, d_projected, w_in_t, row_scale.reshape(1, width), row_shift.reshape(1, width)
+    )
+    mine, in_grad, cap_rows = together(mine, in_grad, cap_rows)
+    in_half = team_parts(in_grad)
     pair = chips_first(*by_chip(mine), bits)
-    in_half = team_parts((core_grad * row_scale + row_shift * column_sum).astype(BF))
-    w_in_f = w_in.astype(F32)
-    d_shift_attn = jnp.sum(column_sum * w_in_f, axis=1)[None]
-    moment_a = jnp.sum(core_grad * w_in_f, axis=1)[None]
     d_scale_attn = moment_a * norm_gains[0]
     d_gain_attn = moment_a * (1.0 + scale_attn)
 
@@ -785,19 +830,20 @@
             placed(join([d_gain_qk, d_gain_c, gate_row])),
         ]
     )
-    sums = sums + swap(sums, "tc")
+    for axis in ("tc", "ty"):
+        sums = sums + swap(sums, axis)
     sums = both_sides(sums, "clip", clip_pair, 0)
     *pair, sums, in_half = together(*pair, sums, in_half)
+    in_rows = half_parts(in_half)
     d_attn_in = join(chips_last(*pair, bits))
-    d_cap = lax.psum_scatter(after(d_cap, *pair), TEAM, scatter_dimension=0, tiled=True)
-    for axis in ("ty", "tz"):
-        sums = sums + swap(sums, axis)
+    sum_output = after(sum_output, *pair).reshape(lax.axis_size("clip"), clips_here, -1, width)
+    sum_output = kept_sum(sum_output, "clip", clip_pair, 0)
+    sums = sums + swap(sums, "tz")
     if reps > 1:
         sums = lax.psum(sums, "rep")
     sums = both_sides(sums, "half", half, 1)
     d_attn_in, sums, sum_gate_up = together(d_attn_in, sums, sum_gate_up)
     sum_gate, sum_up = ff_columns(sum_gate_up[..., :ff_part]), ff_columns(sum_gate_up[..., ff_part:])
-    in_rows = half_parts(in_half)
     sum_cap = to_shards(cap_rows)
     factor_a = row_factor(token_vals)
     core_a = token_vals * factor_a
@@ -827,8 +873,8 @@
     sum_input = head_columns(sum_input, 3)
     sum_ckey = head_columns(sum_cap[..., :part], 1)
     sum_cvalue = head_columns(sum_cap[..., part:], 1)
-    sum_down, d_cap = together(sum_down, d_cap, d_attn_in)[:2]
-    sum_down, d_cap = sum_down.astype(F32), d_cap.astype(F32)
+    sum_output = half_parts(after(sum_output, d_attn_in))
+    d_cap = after(d_cap, d_attn_in).astype(F32)
     d_cap = d_cap.reshape(clips_here, slots_here, -1)
     d_caption = back_clip(join([pick(d_cap, half), pick(d_cap, 1 - half)]))
     return (

time: 845 us -> 823 us (0.974)
  starting transfers between devices: 96.5 us -> 109 us
  local copies, waits for them, and re-layouts: 99.2 us -> 87.5 us
  other arithmetic: 118 us -> 107 us
  waiting for transfers between devices: 327 us -> 317 us
  matrix products: 95.5 us -> 86.1 us
    ppermute x64 -> x69, waiting for transfers between devices: 322 us -> 288 us  [swap(): return lax.ppermute(block, axis, [(0, 1), (1, 0)])]
    reduce_scatter x2 -> x1, waiting for transfers between devices: 0.01 us -> 18.8 us  [all_parts(): return lax.psum_scatter(slice_grad, GROUPS, scatter_dimension=0, tiled=True)]
    ppermute x64 -> x69, starting transfers between devices: 62.6 us -> 73.8 us  [swap(): return lax.ppermute(block, axis, [(0, 1), (1, 0)])]
    dot_general x23 -> x21, matrix products: 95.5 us -> 86.1 us  [dot(): return lax.dot_general(left, right, dims, preferred_element_type=F32)]
    add x14 -> x16, other arithmetic: 19.7 us -> 15.5 us  [kept_sum(): return pick(block, bit, dim).astype(F32) + other.astype(F32)]
    unnamed x290 -> x254, local copies, waits for them, and re-layouts: 29.9 us -> 26.1 us
  transfers between devices with their start and end apart: 81 -> 84, of which waited for: 41 -> 44; matrix products, arithmetic and copies ran while one was open for 30% -> 26% of each run, Pallas kernels for 10% -> 11%
where the time goes in v5:
time: 823 us; the launch traced here: 815 us
  waiting for transfers between devices  317 us (39%)
  starting transfers between devices  109 us (13%)
  other arithmetic  107 us (13%)
  Pallas kernels  92.1 us (11%)
  local copies, waits for them, and re-layouts  87.5 us (11%)
  matrix products  86.1 us (10%)
  between operations  16.4 us (2%)
    ppermute x69, waiting for transfers between devices, swap(): return lax.ppermute(block, axis, [(0, 1), (1, 0)])  288 us
    dot_general x21, matrix products, dot(): return lax.dot_general(left, right, dims, preferred_element_type=F32)  86.1 us
    ppermute x69, starting transfers between devices, swap(): return lax.ppermute(block, axis, [(0, 1), (1, 0)])  73.8 us
    pallas_call x6, Pallas kernels, one_head(): pl.pallas_call(body, grid=(1, steps), in_specs=in_specs + [pl.BlockSpec(m...  65.4 us
    unnamed x254, local copies, waits for them, and re-layouts  26.1 us
    reduce_scatter x1, waiting for transfers between devices, all_parts(): return lax.psum_scatter(slice_grad, GROUPS, scatter_dimension=0, tiled=True)  18.8 us
  transfers between devices with their start and end apart: 84, of which 44 were waited for; matrix products, arithmetic and copies ran while one was open for 26% of the time, Pallas kernels for 11%

profile of v5, /device:TPU:0, one launch (start us, length us, event | category | flops | bytes accessed | tf_op | source)
XLA Modules:
  0.0 815.3 jit_solution(8945530291817409058)
XLA Ops:
  25.6 14.0 %collective-permute-done = bf16[136,1536]{1,0:T(8,128)(2,1)S(1)} collective-permute-done((bf16[136,1536]{1,0:T(8,128)(2,1)}, bf16[136,1536]{1,0:T(8,128)(2,1)S(1)}, u32[]{:S(2)}, u32[]{:S(2)}) %collective-permute-start) | collective-permute-done | bytes 417824 | tf_op jit(solution)/shard_map/ppermute | solution.py:24
  49.1 10.8 %collective-permute-done.5 = f32[1,9216]{1,0:T(1,128)S(1)} collective-permute-done((f32[1,9216]{1,0:T(1,128)S(1)}, f32[1,9216]{1,0:T(1,128)S(1)}, u32[]{:S(2)}, u32[]{:S(2)}) %collective-permute-start.5) | collective-permute-done | bytes 36896 | tf_op jit(solution)/shard_map/ppermute | solution.py:24
  79.6 9.3 %collective-permute-done.7 = bf16[768,576]{0,1:T(8,128)(2,1)} collective-permute-done((bf16[768,576]{0,1:T(8,128)(2,1)S(1)}, bf16[768,576]{0,1:T(8,128)(2,1)}, u32[]{:S(2)}, u32[]{:S(2)}) %collective-permute-start.7) | collective-permute-done | bytes 884768 | tf_op jit(solution)/shard_map/ppermute | solution.py:24
  98.7 5.7 all-gather.6.cloned.1.call-done.rows_ref
  106.5 5.8 all-to-all-start.1
  155.2 7.6 shard_map.282
  162.8 7.6 shard_map.283
  170.4 22.4 %collective-permute-done.15 = bf16[1024,384]{1,0:T(8,128)(2,1)S(1)} collective-permute-done((bf16[1024,384]{1,0:T(8,128)(2,1)S(1)}, bf16[1024,384]{1,0:T(8,128)(2,1)S(1)}, u32[]{:S(2)}, u32[]{:S(2)}) %collective-permute-start.15) | collective-permute-done | bytes 786464 | tf_op jit(solution)/shard_map/ppermute | solution.py:24
  194.7 7.6 shard_map.284
  202.3 28.6 %collective-permute-done.17 = bf16[384,1024]{1,0:T(8,128)(2,1)S(1)} collective-permute-done((bf16[384,1024]{1,0:T(8,128)(2,1)}, bf16[384,1024]{1,0:T(8,128)(2,1)S(1)}, u32[]{:S(2)}, u32[]{:S(2)}) %collective-permute-start.17) | collective-permute-done | bytes 786464 | tf_op jit(solution)/shard_map/ppermute | solution.py:24
  253.6 9.7 %collective-permute-done.21 = bf16[128,1536]{1,0:T(8,128)(2,1)S(1)} collective-permute-done((bf16[128,1536]{1,0:T(8,128)(2,1)S(1)}, bf16[128,1536]{1,0:T(8,128)(2,1)S(1)}, u32[]{:S(2)}, u32[]{:S(2)}) %collective-permute-start.21) | collective-permute-done | bytes 393248 | tf_op jit(solution)/shard_map/ppermute | solution.py:24
  269.9 17.2 %collective-permute-done.22 = bf16[2,128,1536]{2,1,0:T(8,128)(2,1)S(1)} collective-permute-done((bf16[2,128,1536]{2,1,0:T(8,128)(2,1)S(1)}, bf16[2,128,1536]{2,1,0:T(8,128)(2,1)S(1)}, u32[]{:S(2)}, u32[]{:S(2)}) %collective-permute-start.22) | collective-permute-done | bytes 786464 | tf_op jit(solution)/shard_map/ppermute | solution.py:24
  297.3 35.8 %collective-permute-done.23 = bf16[2,384,1024]{2,1,0:T(8,128)(2,1)} collective-permute-done((bf16[2,384,1024]{2,1,0:T(8,128)(2,1)}, bf16[2,384,1024]{2,1,0:T(8,128)(2,1)}, u32[]{:S(2)}, u32[]{:S(2)}) %collective-permute-start.23) | collective-permute-done | bytes 1572896 | tf_op jit(solution)/shard_map/ppermute | solution.py:24
  337.9 9.9 %fusion.112 = f32[2048,1024]{0,1:T(8,128)S(1)} fusion(bf16[2048,1536]{1,0:T(8,128)(2,1)} %all-gather.14.cloned.1.call-done, bf16[1536,1024]{1,0:T(8,128)(2,1)} %bitcast.372), kind=kOutput, calls=%fused_computation.341 | convolution fusion | flops 6442450944 | bytes 17825792 | tf_op jit(solution)/shard_map/dot_general | solution.py:37
  347.8 8.5 %multiply_convert_fusion.1 = (bf16[2048,512]{0,1:T(8,128)(2,1)S(1)}, bf16[2048,512]{0,1:T(8,128)(2,1)S(1)}, bf16[2048,512]{0,1:T(8,128)(2,1)}) fusion(f32[2048,1024]{0,1:T(8,128)S(1)} %fusion.112, bf16[2048,1536]{1,0:T(8,128)(2,1)} %all-gather.12.cloned.1.call-done, bf16[512,1536]{1,0:T(8,128)(2,1)S(1)} %bitcast.409), kind=kOutput, calls=%fused_computation.12 | convolution fusion | flops 3235905536 | bytes 22544384 | tf_op jit(solution)/shard_map/dot_general | solution.py:37
  361.3 6.0 collective-permute-done.24
  367.3 6.9 add_convert_fusion.2
  377.8 7.5 convolution_convert_fusion.10
  385.4 9.0 %collective-permute-done.26 = bf16[2,128,1536]{2,1,0:T(8,128)(2,1)S(1)} collective-permute-done((bf16[2,128,1536]{2,1,0:T(8,128)(2,1)S(1)}, bf16[2,128,1536]{2,1,0:T(8,128)(2,1)S(1)}, u32[]{:S(2)}, u32[]{:S(2)}) %collective-permute-start.26) | collective-permute-done | bytes 786464 | tf_op jit(solution)/shard_map/ppermute | solution.py:24
  429.8 8.8 %collective-permute-done.31 = bf16[2,128,1536]{2,1,0:T(8,128)(2,1)} collective-permute-done((bf16[2,128,1536]{2,1,0:T(8,128)(2,1)}, bf16[2,128,1536]{2,1,0:T(8,128)(2,1)}, u32[]{:S(2)}, u32[]{:S(2)}) %collective-permute-start.31) | collective-permute-done | bytes 786464 | tf_op jit(solution)/shard_map/ppermute | solution.py:24
  448.9 10.5 %convolution_convert_fusion.3 = bf16[1536,1024]{1,0:T(8,128)(2,1)} fusion(bf16[2048,1536]{1,0:T(8,128)(2,1)} %all-gather.14.cloned.1.call-done, bf16[2048,1024]{0,1:T(8,128)(2,1)S(1)} %copy-done.43), kind=kOutput, calls=%fused_computation.16 | convolution fusion | flops 6444023808 | bytes 13631488 | tf_op jit(solution)/shard_map/dot_general | solution.py:37
  464.7 9.4 %shard_map.286 = (f32[3,64,2048]{2,1,0:T(8,128)}, f32[3,64,256]{2,1,0:T(8,128)}, f32[3,64,256]{2,1,0:T(8,128)}, f32[3,1,2048]{2,1,0:T(1,128)}) custom-call(bf16[3,64,2048]{2,1,0:T(8,128)(2,1)} %get-tuple-element.168.refs_0_.q_ref, bf16[3,64,2048]{2,1,0:T(8,128)(2,1)} %reshape_reshape.11.g_ref.refs_1_, bf16[3,64,256]{2,1,0:T(8,128)(2,1)} %multiply_convert_fusion.8.k_ref, ...), custom_call_target="tpu_custom_call" | custom-call | flops 4026531840 | bytes 786432 | tf_op jit(solution)/shard_map/pallas_call | solution.py:352
  499.5 14.2 %shard_map.287 = (f32[3,64,2048]{2,1,0:T(8,128)}, f32[3,64,2048]{2,1,0:T(8,128)}, f32[3,64,2048]{2,1,0:T(8,128)}) custom-call(bf16[3,64,2048]{2,1,0:T(8,128)(2,1)} %get-tuple-element.168.refs_0_.q_ref, bf16[3,64,2048]{2,1,0:T(8,128)(2,1)} %reshape_reshape.11.g_ref.refs_1_, f32[3,1,2048]{2,1,0:T(1,128)} %get-tuple-element.212.refs_2_, ...), custom_call_target="tpu_custom_call" | custom-call | flops 10737418240 | bytes 2097152 | tf_op jit(solution)/shard_map/pallas_call | solution.py:277
  531.9 14.0 %shard_map.288 = (f32[3,64,2048]{2,1,0:T(8,128)}, f32[3,64,2048]{2,1,0:T(8,128)}, f32[3,64,2048]{2,1,0:T(8,128)}) custom-call(bf16[3,64,2048]{2,1,0:T(8,128)(2,1)} %get-tuple-element.168.refs_0_.q_ref, bf16[3,64,2048]{2,1,0:T(8,128)(2,1)} %reshape_reshape.11.g_ref.refs_1_, ...), custom_call_target="tpu_custom_call", output_to_operand_aliasing={{0}: (6, {}), {1}: (7, {}), {2}: (8, {})} | custom-call | flops 10737418240 | bytes 2097152 | tf_op jit(solution)/shard_map/pallas_call | solution.py:277
  548.1 10.4 %collective-permute-done.41 = bf16[128,1536]{1,0:T(8,128)(2,1)S(1)} collective-permute-done((bf16[128,1536]{1,0:T(8,128)(2,1)S(1)}, bf16[128,1536]{1,0:T(8,128)(2,1)S(1)}, u32[]{:S(2)}, u32[]{:S(2)}) %collective-permute-start.41) | collective-permute-done | bytes 393248 | tf_op jit(solution)/shard_map/ppermute | solution.py:24
  564.9 18.8 %reduce-scatter.3.cloned.1.call-done = bf16[384,1024]{1,0:T(8,128)(2,1)} async-done(((bf16[1536,1024]{1,0:T(8,128)(2,1)}), bf16[384,1024]{1,0:T(8,128)(2,1)}) %reduce-scatter.3.cloned.1.call-update) | async-done | bytes 786448 | tf_op jit(solution)/shard_map/reduce_scatter | solution.py:702
  588.7 14.3 %shard_map.289 = (f32[3,64,2048]{2,1,0:T(8,128)}, f32[3,64,2048]{2,1,0:T(8,128)}, f32[3,64,2048]{2,1,0:T(8,128)}) custom-call(bf16[3,64,2048]{2,1,0:T(8,128)(2,1)} %get-tuple-element.168.refs_0_.q_ref, bf16[3,64,2048]{2,1,0:T(8,128)(2,1)} %reshape_reshape.11.g_ref.refs_1_, ...), custom_call_target="tpu_custom_call", output_to_operand_aliasing={{0}: (6, {}), {1}: (7, {}), {2}: (8, {})} | custom-call | flops 10737418240 | bytes 2097152 | tf_op jit(solution)/shard_map/pallas_call | solution.py:277
  632.4 26.5 %collective-permute-done.47 = bf16[1024,384]{1,0:T(8,128)(2,1)} collective-permute-done((bf16[1024,384]{1,0:T(8,128)(2,1)}, bf16[1024,384]{1,0:T(8,128)(2,1)}, u32[]{:S(2)}, u32[]{:S(2)}) %collective-permute-start.47) | collective-permute-done | bytes 786464 | tf_op jit(solution)/shard_map/ppermute | solution.py:24
  663.6 8.2 %shard_map.290 = (bf16[1536,576]{1,0:T(8,128)(2,1)S(1)}, f32[1,1536]{1,0:T(1,128)S(1)}, f32[1,1536]{1,0:T(1,128)S(1)}) custom-call(bf16[2048,1536]{1,0:T(8,128)(2,1)} %copy-done.10, bf16[576,2048]{1,0:T(8,128)(2,1)S(1)} %pad_maximum_fusion.1.grad_ref, bf16[576,1536]{1,0:T(8,128)(2,1)S(1)} %bitcast.347, f32[1,1536]{1,0:T(1,128)S(1)} %copy-done.9, ...), custom_call_target="tpu_custom_call" | custom-call | flops 3623878656 | bytes 12189696 | tf_op jit(solution)/shard_map/pallas_call | solution.py:188
  702.9 9.4 %collective-permute-done.49 = bf16[2,128,1536]{2,1,0:T(8,128)(2,1)} collective-permute-done((bf16[2,128,1536]{2,1,0:T(8,128)(2,1)}, bf16[2,128,1536]{2,1,0:T(8,128)(2,1)}, u32[]{:S(2)}, u32[]{:S(2)}) %collective-permute-start.49) | collective-permute-done | bytes 786464 | tf_op jit(solution)/shard_map/ppermute | solution.py:24
  739.9 6.4 collective-permute-done.55
  778.2 8.8 %collective-permute-done.64 = f32[4,1024]{1,0:T(4,128)S(1)} collective-permute-done((f32[4,1024]{1,0:T(4,128)S(1)}, f32[4,1024]{1,0:T(4,128)S(1)}, u32[]{:S(2)}, u32[]{:S(2)}) %collective-permute-start.64) | collective-permute-done | bytes 16416 | tf_op jit(solution)/shard_map/ppermute | solution.py:24
  (668 shorter events, 409.3 us)
Async XLA Ops:
  25.5 78.9 %all-gather.6.cloned.1.call-start = ((), (), s32[]{:S(2)}) async-start(), calls=%async_computation.10 | async-start | bytes 7520256 | tf_op jit(solution)/shard_map/all_gather | solution.py:520
  76.5 60.2 %collective-permute-start.12 = (bf16[128,1536]{1,0:T(8,128)(2,1)}, bf16[128,1536]{1,0:T(8,128)(2,1)}, u32[]{:S(2)}, u32[]{:S(2)}) collective-permute-start(bf16[128,1536]{1,0:T(8,128)(2,1)} %get-tuple-element.418), channel_id=1, source_target_pairs={{0,8},{8,0},{1,9},{9,1},{2,10},{10,2},{3,11},{11,3},{4,12},{12,4},... | collective-permute-start | bytes 1179656 | tf_op jit(solution)/shard_map/ppermute | solution.py:24
  104.5 30.8 %collective-permute-start.13 = (bf16[48,1536]{1,0:T(8,128)(2,1)S(1)}, bf16[48,1536]{1,0:T(8,128)(2,1)}, u32[]{:S(2)}, u32[]{:S(2)}) collective-permute-start(bf16[48,1536]{1,0:T(8,128)(2,1)S(1)} %copy-done.83), channel_id=1, source_target_pairs={{0,8},{8,0},{1,9},{9,1},{2,10},{10,2},{3,11},{11,3},{4,12},{12,4},... | collective-permute-start | bytes 442376 | tf_op jit(solution)/shard_map/ppermute | solution.py:24
  106.5 29.8 %all-to-all-start.1 = ((bf16[8,128,384]{1,2,0:T(8,128)(2,1)}), bf16[8,128,384]{1,2,0:T(8,128)(2,1)S(1)}, u32[]{:S(2)}, u32[]{:S(2)}) async-start(bf16[8,128,384]{1,2,0:T(8,128)(2,1)} %pad_maximum_fusion.7), calls=%async_computation.1 | async-start | bytes 1572864 | tf_op jit(solution)/shard_map/all_to_all | solution.py:493
  112.3 80.8 %all-gather.8.cloned.1.call-start = ((), (), s32[]{:S(2)}) async-start(), calls=%async_computation.11 | async-start | bytes 2359296 | tf_op jit(solution)/shard_map/all_gather | solution.py:569
  136.7 126.7 %all-gather.10.cloned.1.call-start = ((), (), s32[]{:S(2)}) async-start(), calls=%async_computation.12 | async-start | bytes 5308416 | tf_op jit(solution)/shard_map/all_gather | solution.py:587
  145.8 151.2 %all-gather.12.cloned.1.call-start = ((), (), s32[]{:S(2)}) async-start(), calls=%async_computation.13 | async-start | bytes 7077888 | tf_op jit(solution)/shard_map/all_gather | solution.py:599
  150.3 42.9 %all-to-all-start.2 = ((bf16[8,48,1024]{2,1,0:T(8,128)(2,1)}), bf16[8,48,1024]{2,1,0:T(8,128)(2,1)}, u32[]{:S(2)}, u32[]{:S(2)}) async-start(bf16[8,48,1024]{2,1,0:T(8,128)(2,1)} %pad_maximum_fusion.8), calls=%async_computation.2 | async-start | bytes 1572864 | tf_op jit(solution)/shard_map/all_to_all | solution.py:493
  155.0 37.8 %collective-permute-start.15 = (bf16[1024,384]{1,0:T(8,128)(2,1)S(1)}, bf16[1024,384]{1,0:T(8,128)(2,1)S(1)}, u32[]{:S(2)}, u32[]{:S(2)}) collective-permute-start(bf16[1024,384]{1,0:T(8,128)(2,1)S(1)} %bitcast.391), channel_id=1, source_target_pairs={{0,8},{8,0},{1,9},{9,1},{2,10},{10,2},{3,11},{11,3},{4,12},{12,4},... | collective-permute-start | bytes 2359304 | tf_op jit(solution)/shard_map/ppermute | solution.py:24
  193.2 40.5 %collective-permute-start.16 = (bf16[2,1024,384]{2,1,0:T(8,128)(2,1)S(1)}, bf16[2,1024,384]{2,1,0:T(8,128)(2,1)S(1)}, u32[]{:S(2)}, u32[]{:S(2)}) collective-permute-start(bf16[2,1024,384]{2,1,0:T(8,128)(2,1)S(1)} %maximum_select_fusion.2), channel_id=1, source_target_pairs={{0,16},{16,0},{1,17},{17,1},{2,18},{18,2},{3,19},{19,3},{4,20},{20... | collective-permute-start | bytes 4718600 | tf_op jit(solution)/shard_map/ppermute | solution.py:24
  194.7 36.2 %collective-permute-start.17 = (bf16[384,1024]{1,0:T(8,128)(2,1)}, bf16[384,1024]{1,0:T(8,128)(2,1)S(1)}, u32[]{:S(2)}, u32[]{:S(2)}) collective-permute-start(bf16[384,1024]{1,0:T(8,128)(2,1)} %bitcast.45), channel_id=1, source_target_pairs={{0,8},{8,0},{1,9},{9,1},{2,10},{10,2},{3,11},{11,3},{4,12},{12,4},... | collective-permute-start | bytes 2359304 | tf_op jit(solution)/shard_map/ppermute | solution.py:24
  267.2 70.7 %all-gather.14.cloned.1.call-start = ((), (), s32[]{:S(2)}) async-start(), calls=%async_computation.14 | async-start | bytes 7077888 | tf_op jit(solution)/shard_map/all_gather | solution.py:651
  297.0 36.2 %collective-permute-start.23 = (bf16[2,384,1024]{2,1,0:T(8,128)(2,1)}, bf16[2,384,1024]{2,1,0:T(8,128)(2,1)}, u32[]{:S(2)}, u32[]{:S(2)}) collective-permute-start(bf16[2,384,1024]{2,1,0:T(8,128)(2,1)} %maximum_select_fusion.3), channel_id=1, source_target_pairs={{0,16},{16,0},{1,17},{17,1},{2,18},{18,2},{3,19},{19,3},{4,20},{20... | collective-permute-start | bytes 4718600 | tf_op jit(solution)/shard_map/ppermute | solution.py:24
  412.5 28.6 %collective-permute-start.29 = (bf16[1024,1536]{1,0:T(8,128)(2,1)}, bf16[1024,1536]{1,0:T(8,128)(2,1)}, u32[]{:S(2)}, u32[]{:S(2)}) collective-permute-start(bf16[1024,1536]{1,0:T(8,128)(2,1)} %convolution_convert_fusion.7), channel_id=1, source_target_pairs={{0,1},{1,0},{2,3},{3,2},{4,5},{5,4},{6,7},{7,6},{8,9},{9,8},{10,11... | collective-permute-start | bytes 9437192 | tf_op jit(solution)/shard_map/ppermute | solution.py:24
  425.5 33.9 %all-to-all-start.4 = ((bf16[8,192,256]{2,1,0:T(8,128)(2,1)}), bf16[8,192,256]{2,1,0:T(8,128)(2,1)}, u32[]{:S(2)}, u32[]{:S(2)}) async-start(bf16[8,192,256]{2,1,0:T(8,128)(2,1)} %bitcast.379), calls=%async_computation.4 | async-start | bytes 1572864 | tf_op jit(solution)/shard_map/all_to_all | solution.py:728
  429.8 153.9 %reduce-scatter.3.cloned.1.call-start = ((), (), s32[]{:S(2)}) async-start(), calls=%async_computation.15 | async-start | bytes 3932160 | tf_op jit(solution)/shard_map/reduce_scatter | solution.py:702
  445.9 37.4 %collective-permute-start.33 = (bf16[2,128,1536]{2,1,0:T(8,128)(2,1)}, bf16[2,128,1536]{2,1,0:T(8,128)(2,1)}, u32[]{:S(2)}, u32[]{:S(2)}) collective-permute-start(bf16[2,128,1536]{2,1,0:T(8,128)(2,1)} %dynamic-slice_bitcast_fusion.5), channel_id=1, source_target_pairs={{0,2},{2,0},{1,3},{3,1},{4,6},{6,4},{5,7},{7,5},{8,10},{10,8},{9,1... | collective-permute-start | bytes 2359304 | tf_op jit(solution)/shard_map/ppermute | solution.py:24
  447.4 37.7 %collective-permute-start.32 = (bf16[2,128,1536]{2,1,0:T(8,128)(2,1)}, bf16[2,128,1536]{2,1,0:T(8,128)(2,1)}, u32[]{:S(2)}, u32[]{:S(2)}) collective-permute-start(bf16[2,128,1536]{2,1,0:T(8,128)(2,1)} %dynamic-slice_bitcast_fusion.6), channel_id=1, source_target_pairs={{0,4},{4,0},{1,5},{5,1},{2,6},{6,2},{3,7},{7,3},{8,12},{12,8},{9,1... | collective-permute-start | bytes 2359304 | tf_op jit(solution)/shard_map/ppermute | solution.py:24
  486.7 31.0 %collective-permute-start.36 = (bf16[128,1536]{1,0:T(8,128)(2,1)S(1)}, bf16[128,1536]{1,0:T(8,128)(2,1)S(1)}, u32[]{:S(2)}, u32[]{:S(2)}) collective-permute-start(bf16[128,1536]{1,0:T(8,128)(2,1)S(1)} %fusion.42), channel_id=1, source_target_pairs={{0,2},{2,0},{1,3},{3,1},{4,6},{6,4},{5,7},{7,5},{8,10},{10,8},{9,1... | collective-permute-start | bytes 1179656 | tf_op jit(solution)/shard_map/ppermute | solution.py:24
  488.3 29.5 %collective-permute-start.37 = (bf16[128,1536]{1,0:T(8,128)(2,1)S(1)}, bf16[128,1536]{1,0:T(8,128)(2,1)S(1)}, u32[]{:S(2)}, u32[]{:S(2)}) collective-permute-start(bf16[128,1536]{1,0:T(8,128)(2,1)S(1)} %fusion.43), channel_id=1, source_target_pairs={{0,4},{4,0},{1,5},{5,1},{2,6},{6,2},{3,7},{7,3},{8,12},{12,8},{9,1... | collective-permute-start | bytes 1179656 | tf_op jit(solution)/shard_map/ppermute | solution.py:24
  490.9 55.1 %collective-permute-start.38 = (bf16[128,1536]{1,0:T(8,128)(2,1)}, bf16[128,1536]{1,0:T(8,128)(2,1)}, u32[]{:S(2)}, u32[]{:S(2)}) collective-permute-start(bf16[128,1536]{1,0:T(8,128)(2,1)} %dynamic-slice_bitcast_fusion.14), channel_id=1, source_target_pairs={{0,8},{8,0},{1,9},{9,1},{2,10},{10,2},{3,11},{11,3},{4,12},{12,4},... | collective-permute-start | bytes 1179656 | tf_op jit(solution)/shard_map/ppermute | solution.py:24
  522.2 40.8 %collective-permute-start.40 = (bf16[2,1024,384]{2,1,0:T(8,128)(2,1)}, bf16[2,1024,384]{2,1,0:T(8,128)(2,1)}, u32[]{:S(2)}, u32[]{:S(2)}) collective-permute-start(bf16[2,1024,384]{2,1,0:T(8,128)(2,1)} %dynamic-slice_bitcast_fusion), channel_id=1, source_target_pairs={{0,16},{16,0},{1,17},{17,1},{2,18},{18,2},{3,19},{19,3},{4,20},{20... | collective-permute-start | bytes 4718600 | tf_op jit(solution)/shard_map/ppermute | solution.py:24
  526.4 33.1 %collective-permute-start.39 = (bf16[2,2,32,4096]{3,2,1,0:T(8,128)(2,1)}, bf16[2,2,32,4096]{3,2,1,0:T(8,128)(2,1)}, u32[]{:S(2)}, u32[]{:S(2)}) collective-permute-start(bf16[2,2,32,4096]{3,2,1,0:T(8,128)(2,1)} %dynamic-slice_bitcast_fusion.1), channel_id=1, source_target_pairs={{0,1},{1,0},{2,3},{3,2},{4,5},{5,4},{6,7},{7,6},{8,9},{9,8},{10,11... | collective-permute-start | bytes 3145736 | tf_op jit(solution)/shard_map/ppermute | solution.py:24
  527.9 30.6 %collective-permute-start.41 = (bf16[128,1536]{1,0:T(8,128)(2,1)S(1)}, bf16[128,1536]{1,0:T(8,128)(2,1)S(1)}, u32[]{:S(2)}, u32[]{:S(2)}) collective-permute-start(bf16[128,1536]{1,0:T(8,128)(2,1)S(1)} %get-tuple-element.417), channel_id=1, source_target_pairs={{0,8},{8,0},{1,9},{9,1},{2,10},{10,2},{3,11},{11,3},{4,12},{12,4},... | collective-permute-start | bytes 1179656 | tf_op jit(solution)/shard_map/ppermute | solution.py:24
  588.7 132.9 %reduce-scatter.5.cloned.1.call-start = ((), (), s32[]{:S(2)}) async-start(), calls=%async_computation.16 | async-start | bytes 5308416 | tf_op jit(solution)/shard_map/reduce_scatter | solution.py:761
  622.9 36.1 %collective-permute-start.47 = (bf16[1024,384]{1,0:T(8,128)(2,1)}, bf16[1024,384]{1,0:T(8,128)(2,1)}, u32[]{:S(2)}, u32[]{:S(2)}) collective-permute-start(bf16[1024,384]{1,0:T(8,128)(2,1)} %dynamic-slice_bitcast_fusion.4), channel_id=1, source_target_pairs={{0,8},{8,0},{1,9},{9,1},{2,10},{10,2},{3,11},{11,3},{4,12},{12,4},... | collective-permute-start | bytes 2359304 | tf_op jit(solution)/shard_map/ppermute | solution.py:24
  632.1 55.5 %collective-permute-start.46 = (bf16[1024,1536]{1,0:T(8,128)(2,1)}, bf16[1024,1536]{1,0:T(8,128)(2,1)}, u32[]{:S(2)}, u32[]{:S(2)}) collective-permute-start(bf16[1024,1536]{1,0:T(8,128)(2,1)} %convolution_convert_fusion.4), channel_id=1, source_target_pairs={{0,1},{1,0},{2,3},{3,2},{4,5},{5,4},{6,7},{7,6},{8,9},{9,8},{10,11... | collective-permute-start | bytes 9437192 | tf_op jit(solution)/shard_map/ppermute | solution.py:24
  698.7 92.7 %all-to-all-start.7 = ((bf16[8,128,384]{1,2,0:T(8,128)(2,1)}), bf16[8,128,384]{1,2,0:T(8,128)(2,1)}, u32[]{:S(2)}, u32[]{:S(2)}) async-start(bf16[8,128,384]{1,2,0:T(8,128)(2,1)} %copy.236), calls=%async_computation.9 | async-start | bytes 1572864 | tf_op jit(solution)/shard_map/all_to_all | solution.py:689
  732.2 55.3 %collective-permute-start.66 = (bf16[384,576]{1,0:T(8,128)(2,1)}, bf16[384,576]{1,0:T(8,128)(2,1)}, u32[]{:S(2)}, u32[]{:S(2)}) collective-permute-start(bf16[384,576]{1,0:T(8,128)(2,1)} %dynamic-slice_bitcast_fusion.11), channel_id=1, source_target_pairs={{0,8},{8,0},{1,9},{9,1},{2,10},{10,2},{3,11},{11,3},{4,12},{12,4},... | collective-permute-start | bytes 1327112 | tf_op jit(solution)/shard_map/ppermute | solution.py:24
  751.7 48.8 %collective-permute-start.68 = (bf16[48,1536]{1,0:T(8,128)(2,1)}, bf16[48,1536]{1,0:T(8,128)(2,1)}, u32[]{:S(2)}, u32[]{:S(2)}) collective-permute-start(bf16[48,1536]{1,0:T(8,128)(2,1)} %fusion.52), channel_id=1, source_target_pairs={{0,8},{8,0},{1,9},{9,1},{2,10},{10,2},{3,11},{11,3},{4,12},{12,4},... | collective-permute-start | bytes 442376 | tf_op jit(solution)/shard_map/ppermute | solution.py:24
  752.6 46.1 %collective-permute-start.60 = (bf16[16,4096]{1,0:T(8,128)(2,1)}, bf16[16,4096]{1,0:T(8,128)(2,1)}, u32[]{:S(2)}, u32[]{:S(2)}) collective-permute-start(bf16[16,4096]{1,0:T(8,128)(2,1)} %fusion.63), channel_id=1, source_target_pairs={{0,8},{8,0},{1,9},{9,1},{2,10},{10,2},{3,11},{11,3},{4,12},{12,4},... | collective-permute-start | bytes 393224 | tf_op jit(solution)/shard_map/ppermute | solution.py:24
  755.2 46.9 %collective-permute-start.58 = (bf16[128,1536]{1,0:T(8,128)(2,1)}, bf16[128,1536]{1,0:T(8,128)(2,1)}, u32[]{:S(2)}, u32[]{:S(2)}) collective-permute-start(bf16[128,1536]{1,0:T(8,128)(2,1)} %slice.339), channel_id=1, source_target_pairs={{0,8},{8,0},{1,9},{9,1},{2,10},{10,2},{3,11},{11,3},{4,12},{12,4},... | collective-permute-start | bytes 1179656 | tf_op jit(solution)/shard_map/ppermute | solution.py:24
  (174 other events, 1355.1 us)
Sparse Core Ops, SparseCore 0:
  43.3 61.0 all-gather.5
  136.9 20.7 all-gather.7
  159.9 59.1 all-gather.9
  221.1 46.3 all-gather.11
  297.1 37.7 all-gather.13
  482.8 100.7 reduce-scatter.2
  617.0 57.5 reduce-scatter.4

commit v6 on v5

--- a/solution.py
+++ b/solution.py
@@ -763,7 +763,7 @@
     mean_c = mean_c + swap(mean_c, "ty")
     mean_c = mean_c + swap(mean_c, "tz")
     backs = self_backward(queries, d_self, logs, delta, all_keys, all_values, 0, None)
-    *backs, delta, mean_c, ffn_out = together(*backs, delta, mean_c, ffn_out)
+    *backs, delta, mean_c, ffn_out, up_rows = together(*backs, delta, mean_c, ffn_out, up_rows)
     result = back_clip((middle + gate_ffn * ffn_out).astype(BF))
     d_gate_ffn = jnp.sum(grad_out * ffn_out, axis=0, keepdims=True)
     mean_c = mean_c[None] / width
@@ -861,6 +861,7 @@
     d_silu = lax.dynamic_update_slice_in_dim(
         jnp.zeros(condition.shape, F32), d_silu, device * shard_rows, 1
     )
+    d_silu, in_rows = together(d_silu, in_rows)
     sum_input = to_shards(in_rows)
     if reps > 1:
         d_silu = lax.psum(d_silu, "rep")

time: 823 us -> 823 us (level)
    reduce_scatter x1, waiting for transfers between devices: 18.8 us -> 0.01 us  [all_parts(): return lax.psum_scatter(slice_grad, GROUPS, scatter_dimension=0, tiled=True)]
    ppermute x69, waiting for transfers between devices: 288 us -> 303 us  [swap(): return lax.ppermute(block, axis, [(0, 1), (1, 0)])]
    add x16 -> x17, other arithmetic: 15.5 us -> 18.1 us  [kept_sum(): return pick(block, bit, dim).astype(F32) + other.astype(F32)]
    unnamed x254 -> x264, local copies, waits for them, and re-layouts: 26.1 us -> 25.1 us
  transfers between devices with their start and end apart: 84 -> 84, of which waited for: 44 -> 45; matrix products, arithmetic and copies ran while one was open for 26% -> 26% of each run, Pallas kernels for 11% -> 11%
where the time goes in v6:
time: 823 us; the launch traced here: 813 us
  waiting for transfers between devices  312 us (38%)
  other arithmetic  110 us (13%)
  starting transfers between devices  106 us (13%)
  Pallas kernels  92.5 us (11%)
  local copies, waits for them, and re-layouts  88.3 us (11%)
  matrix products  87.8 us (11%)
  between operations  16.3 us (2%)
    ppermute x69, waiting for transfers between devices, swap(): return lax.ppermute(block, axis, [(0, 1), (1, 0)])  303 us
    dot_general x21, matrix products, dot(): return lax.dot_general(left, right, dims, preferred_element_type=F32)  87.8 us
    ppermute x69, starting transfers between devices, swap(): return lax.ppermute(block, axis, [(0, 1), (1, 0)])  70.3 us
    pallas_call x6, Pallas kernels, one_head(): pl.pallas_call(body, grid=(1, steps), in_specs=in_specs + [pl.BlockSpec(m...  65.7 us
    unnamed x264, local copies, waits for them, and re-layouts  25.1 us
    add x17, other arithmetic, kept_sum(): return pick(block, bit, dim).astype(F32) + other.astype(F32)  18.1 us
  transfers between devices with their start and end apart: 84, of which 45 were waited for; matrix products, arithmetic and copies ran while one was open for 26% of the time, Pallas kernels for 11%

profile of v6, /device:TPU:0, one launch (start us, length us, event | category | flops | bytes accessed | tf_op | source)
XLA Modules:
  0.0 813.4 jit_solution(6819878244233506410)
XLA Ops:
  25.7 14.0 %collective-permute-done = bf16[136,1536]{1,0:T(8,128)(2,1)S(1)} collective-permute-done((bf16[136,1536]{1,0:T(8,128)(2,1)}, bf16[136,1536]{1,0:T(8,128)(2,1)S(1)}, u32[]{:S(2)}, u32[]{:S(2)}) %collective-permute-start) | collective-permute-done | bytes 417824 | tf_op jit(solution)/shard_map/ppermute | solution.py:24
  49.1 10.8 %collective-permute-done.5 = f32[1,9216]{1,0:T(1,128)S(1)} collective-permute-done((f32[1,9216]{1,0:T(1,128)S(1)}, f32[1,9216]{1,0:T(1,128)S(1)}, u32[]{:S(2)}, u32[]{:S(2)}) %collective-permute-start.5) | collective-permute-done | bytes 36896 | tf_op jit(solution)/shard_map/ppermute | solution.py:24
  79.6 9.2 %collective-permute-done.7 = bf16[768,576]{0,1:T(8,128)(2,1)} collective-permute-done((bf16[768,576]{0,1:T(8,128)(2,1)S(1)}, bf16[768,576]{0,1:T(8,128)(2,1)}, u32[]{:S(2)}, u32[]{:S(2)}) %collective-permute-start.7) | collective-permute-done | bytes 884768 | tf_op jit(solution)/shard_map/ppermute | solution.py:24
  106.5 5.8 all-to-all-start.1
  155.2 7.6 shard_map.282
  162.8 7.7 shard_map.283
  170.5 22.4 %collective-permute-done.15 = bf16[1024,384]{1,0:T(8,128)(2,1)S(1)} collective-permute-done((bf16[1024,384]{1,0:T(8,128)(2,1)S(1)}, bf16[1024,384]{1,0:T(8,128)(2,1)S(1)}, u32[]{:S(2)}, u32[]{:S(2)}) %collective-permute-start.15) | collective-permute-done | bytes 786464 | tf_op jit(solution)/shard_map/ppermute | solution.py:24
  194.8 7.6 shard_map.284
  202.4 28.5 %collective-permute-done.17 = bf16[384,1024]{1,0:T(8,128)(2,1)S(1)} collective-permute-done((bf16[384,1024]{1,0:T(8,128)(2,1)}, bf16[384,1024]{1,0:T(8,128)(2,1)S(1)}, u32[]{:S(2)}, u32[]{:S(2)}) %collective-permute-start.17) | collective-permute-done | bytes 786464 | tf_op jit(solution)/shard_map/ppermute | solution.py:24
  253.7 9.7 %collective-permute-done.21 = bf16[128,1536]{1,0:T(8,128)(2,1)S(1)} collective-permute-done((bf16[128,1536]{1,0:T(8,128)(2,1)S(1)}, bf16[128,1536]{1,0:T(8,128)(2,1)S(1)}, u32[]{:S(2)}, u32[]{:S(2)}) %collective-permute-start.21) | collective-permute-done | bytes 393248 | tf_op jit(solution)/shard_map/ppermute | solution.py:24
  270.0 17.1 %collective-permute-done.22 = bf16[2,128,1536]{2,1,0:T(8,128)(2,1)S(1)} collective-permute-done((bf16[2,128,1536]{2,1,0:T(8,128)(2,1)S(1)}, bf16[2,128,1536]{2,1,0:T(8,128)(2,1)S(1)}, u32[]{:S(2)}, u32[]{:S(2)}) %collective-permute-start.22) | collective-permute-done | bytes 786464 | tf_op jit(solution)/shard_map/ppermute | solution.py:24
  297.4 35.8 %collective-permute-done.23 = bf16[2,384,1024]{2,1,0:T(8,128)(2,1)} collective-permute-done((bf16[2,384,1024]{2,1,0:T(8,128)(2,1)}, bf16[2,384,1024]{2,1,0:T(8,128)(2,1)}, u32[]{:S(2)}, u32[]{:S(2)}) %collective-permute-start.23) | collective-permute-done | bytes 1572896 | tf_op jit(solution)/shard_map/ppermute | solution.py:24
  337.9 9.9 %fusion.110 = f32[2048,1024]{0,1:T(8,128)S(1)} fusion(bf16[2048,1536]{1,0:T(8,128)(2,1)} %all-gather.14.cloned.1.call-done, bf16[1536,1024]{1,0:T(8,128)(2,1)} %bitcast.372), kind=kOutput, calls=%fused_computation.338 | convolution fusion | flops 6442450944 | bytes 17825792 | tf_op jit(solution)/shard_map/dot_general | solution.py:37
  347.8 8.5 %multiply_convert_fusion.1 = (bf16[2048,512]{0,1:T(8,128)(2,1)S(1)}, bf16[2048,512]{0,1:T(8,128)(2,1)S(1)}, bf16[2048,512]{0,1:T(8,128)(2,1)}) fusion(f32[2048,1024]{0,1:T(8,128)S(1)} %fusion.110, bf16[2048,1536]{1,0:T(8,128)(2,1)} %all-gather.12.cloned.1.call-done, bf16[512,1536]{1,0:T(8,128)(2,1)S(1)} %bitcast.409), kind=kOutput, calls=%fused_computation.12 | convolution fusion | flops 3235905536 | bytes 22544384 | tf_op jit(solution)/shard_map/dot_general | solution.py:37
  361.4 6.0 collective-permute-done.24
  367.4 6.9 add_convert_fusion.2
  377.9 7.5 convolution_convert_fusion.10
  385.4 9.0 %collective-permute-done.26 = bf16[2,128,1536]{2,1,0:T(8,128)(2,1)S(1)} collective-permute-done((bf16[2,128,1536]{2,1,0:T(8,128)(2,1)S(1)}, bf16[2,128,1536]{2,1,0:T(8,128)(2,1)S(1)}, u32[]{:S(2)}, u32[]{:S(2)}) %collective-permute-start.26) | collective-permute-done | bytes 786464 | tf_op jit(solution)/shard_map/ppermute | solution.py:24
  430.0 8.8 %collective-permute-done.31 = bf16[2,128,1536]{2,1,0:T(8,128)(2,1)} collective-permute-done((bf16[2,128,1536]{2,1,0:T(8,128)(2,1)}, bf16[2,128,1536]{2,1,0:T(8,128)(2,1)}, u32[]{:S(2)}, u32[]{:S(2)}) %collective-permute-start.31) | collective-permute-done | bytes 786464 | tf_op jit(solution)/shard_map/ppermute | solution.py:24
  446.8 10.4 %convolution_convert_fusion.3 = bf16[1536,1024]{1,0:T(8,128)(2,1)} fusion(bf16[2048,1536]{1,0:T(8,128)(2,1)} %all-gather.14.cloned.1.call-done, bf16[2048,1024]{0,1:T(8,128)(2,1)S(1)} %copy-done.44), kind=kOutput, calls=%fused_computation.16 | convolution fusion | flops 6444023808 | bytes 13631488 | tf_op jit(solution)/shard_map/dot_general | solution.py:37
  468.6 9.4 %shard_map.286 = (f32[3,64,2048]{2,1,0:T(8,128)}, f32[3,64,256]{2,1,0:T(8,128)}, f32[3,64,256]{2,1,0:T(8,128)}, f32[3,1,2048]{2,1,0:T(1,128)}) custom-call(bf16[3,64,2048]{2,1,0:T(8,128)(2,1)} %get-tuple-element.171.refs_0_.q_ref, bf16[3,64,2048]{2,1,0:T(8,128)(2,1)} %reshape_reshape.11.g_ref.refs_1_, bf16[3,64,256]{2,1,0:T(8,128)(2,1)} %multiply_convert_fusion.8.k_ref, ...), custom_call_target="tpu_custom_call" | custom-call | flops 4026531840 | bytes 786432 | tf_op jit(solution)/shard_map/pallas_call | solution.py:352
  488.9 8.3 %collective-permute-done.32 = bf16[2,128,1536]{2,1,0:T(8,128)(2,1)} collective-permute-done((bf16[2,128,1536]{2,1,0:T(8,128)(2,1)}, bf16[2,128,1536]{2,1,0:T(8,128)(2,1)}, u32[]{:S(2)}, u32[]{:S(2)}) %collective-permute-start.32) | collective-permute-done | bytes 786464 | tf_op jit(solution)/shard_map/ppermute | solution.py:24
  510.8 14.2 %shard_map.287 = (f32[3,64,2048]{2,1,0:T(8,128)}, f32[3,64,2048]{2,1,0:T(8,128)}, f32[3,64,2048]{2,1,0:T(8,128)}) custom-call(bf16[3,64,2048]{2,1,0:T(8,128)(2,1)} %get-tuple-element.171.refs_0_.q_ref, bf16[3,64,2048]{2,1,0:T(8,128)(2,1)} %reshape_reshape.11.g_ref.refs_1_, f32[3,1,2048]{2,1,0:T(1,128)} %get-tuple-element.215.refs_2_, ...), custom_call_target="tpu_custom_call" | custom-call | flops 10737418240 | bytes 2097152 | tf_op jit(solution)/shard_map/pallas_call | solution.py:277
  529.8 9.5 %collective-permute-done.38 = bf16[128,1536]{1,0:T(8,128)(2,1)} collective-permute-done((bf16[128,1536]{1,0:T(8,128)(2,1)}, bf16[128,1536]{1,0:T(8,128)(2,1)}, u32[]{:S(2)}, u32[]{:S(2)}) %collective-permute-start.38) | collective-permute-done | bytes 393248 | tf_op jit(solution)/shard_map/ppermute | solution.py:24
  550.4 14.2 %shard_map.288 = (f32[3,64,2048]{2,1,0:T(8,128)}, f32[3,64,2048]{2,1,0:T(8,128)}, f32[3,64,2048]{2,1,0:T(8,128)}) custom-call(bf16[3,64,2048]{2,1,0:T(8,128)(2,1)} %get-tuple-element.171.refs_0_.q_ref, bf16[3,64,2048]{2,1,0:T(8,128)(2,1)} %reshape_reshape.11.g_ref.refs_1_, ...), custom_call_target="tpu_custom_call", output_to_operand_aliasing={{0}: (6, {}), {1}: (7, {}), {2}: (8, {})} | custom-call | flops 10737418240 | bytes 2097152 | tf_op jit(solution)/shard_map/pallas_call | solution.py:277
  571.5 11.7 %collective-permute-done.40 = bf16[2,1024,384]{2,1,0:T(8,128)(2,1)} collective-permute-done((bf16[2,1024,384]{2,1,0:T(8,128)(2,1)}, bf16[2,1024,384]{2,1,0:T(8,128)(2,1)}, u32[]{:S(2)}, u32[]{:S(2)}) %collective-permute-start.40) | collective-permute-done | bytes 1572896 | tf_op jit(solution)/shard_map/ppermute | solution.py:24
  590.3 14.3 %shard_map.289 = (f32[3,64,2048]{2,1,0:T(8,128)}, f32[3,64,2048]{2,1,0:T(8,128)}, f32[3,64,2048]{2,1,0:T(8,128)}) custom-call(bf16[3,64,2048]{2,1,0:T(8,128)(2,1)} %get-tuple-element.171.refs_0_.q_ref, bf16[3,64,2048]{2,1,0:T(8,128)(2,1)} %reshape_reshape.11.g_ref.refs_1_, ...), custom_call_target="tpu_custom_call", output_to_operand_aliasing={{0}: (6, {}), {1}: (7, {}), {2}: (8, {})} | custom-call | flops 10737418240 | bytes 2097152 | tf_op jit(solution)/shard_map/pallas_call | solution.py:277
  632.9 26.5 %collective-permute-done.47 = bf16[1024,384]{1,0:T(8,128)(2,1)} collective-permute-done((bf16[1024,384]{1,0:T(8,128)(2,1)}, bf16[1024,384]{1,0:T(8,128)(2,1)}, u32[]{:S(2)}, u32[]{:S(2)}) %collective-permute-start.47) | collective-permute-done | bytes 786464 | tf_op jit(solution)/shard_map/ppermute | solution.py:24
  664.1 8.2 %shard_map.290 = (bf16[1536,576]{1,0:T(8,128)(2,1)S(1)}, f32[1,1536]{1,0:T(1,128)S(1)}, f32[1,1536]{1,0:T(1,128)S(1)}) custom-call(bf16[2048,1536]{1,0:T(8,128)(2,1)} %copy-done.10, bf16[576,2048]{1,0:T(8,128)(2,1)S(1)} %pad_maximum_fusion.1.grad_ref, bf16[576,1536]{1,0:T(8,128)(2,1)S(1)} %bitcast.347, f32[1,1536]{1,0:T(1,128)S(1)} %copy-done.9, ...), custom_call_target="tpu_custom_call" | custom-call | flops 3623878656 | bytes 12189696 | tf_op jit(solution)/shard_map/pallas_call | solution.py:188
  703.3 8.5 %collective-permute-done.49 = bf16[2,128,1536]{2,1,0:T(8,128)(2,1)} collective-permute-done((bf16[2,128,1536]{2,1,0:T(8,128)(2,1)}, bf16[2,128,1536]{2,1,0:T(8,128)(2,1)}, u32[]{:S(2)}, u32[]{:S(2)}) %collective-permute-start.49) | collective-permute-done | bytes 786464 | tf_op jit(solution)/shard_map/ppermute | solution.py:24
  738.1 8.9 %collective-permute-done.55 = bf16[128,1536]{1,0:T(8,128)(2,1)S(1)} collective-permute-done((bf16[128,1536]{1,0:T(8,128)(2,1)S(1)}, bf16[128,1536]{1,0:T(8,128)(2,1)S(1)}, u32[]{:S(2)}, u32[]{:S(2)}) %collective-permute-start.55) | collective-permute-done | bytes 393248 | tf_op jit(solution)/shard_map/ppermute | solution.py:24
  759.8 13.4 %collective-permute-done.61 = bf16[384,576]{1,0:T(8,128)(2,1)} collective-permute-done((bf16[384,576]{1,0:T(8,128)(2,1)}, bf16[384,576]{1,0:T(8,128)(2,1)}, u32[]{:S(2)}, u32[]{:S(2)}) %collective-permute-start.61) | collective-permute-done | bytes 442400 | tf_op jit(solution)/shard_map/ppermute | solution.py:24
  (677 shorter events, 406.4 us)
Async XLA Ops:
  25.6 78.9 %all-gather.6.cloned.1.call-start = ((), (), s32[]{:S(2)}) async-start(), calls=%async_computation.10 | async-start | bytes 7520256 | tf_op jit(solution)/shard_map/all_gather | solution.py:520
  43.2 24.3 %collective-permute-start.3 = (bf16[384,576]{1,0:T(8,128)(2,1)S(1)}, bf16[384,576]{1,0:T(8,128)(2,1)S(1)}, u32[]{:S(2)}, u32[]{:S(2)}) collective-permute-start(bf16[384,576]{1,0:T(8,128)(2,1)S(1)} %bitcast.395), channel_id=1, source_target_pairs={{0,8},{8,0},{1,9},{9,1},{2,10},{10,2},{3,11},{11,3},{4,12},{12,4},... | collective-permute-start | bytes 1327112 | tf_op jit(solution)/shard_map/ppermute | solution.py:24
  76.5 60.2 %collective-permute-start.12 = (bf16[128,1536]{1,0:T(8,128)(2,1)}, bf16[128,1536]{1,0:T(8,128)(2,1)}, u32[]{:S(2)}, u32[]{:S(2)}) collective-permute-start(bf16[128,1536]{1,0:T(8,128)(2,1)} %get-tuple-element.424), channel_id=1, source_target_pairs={{0,8},{8,0},{1,9},{9,1},{2,10},{10,2},{3,11},{11,3},{4,12},{12,4},... | collective-permute-start | bytes 1179656 | tf_op jit(solution)/shard_map/ppermute | solution.py:24
  104.5 30.8 %collective-permute-start.13 = (bf16[48,1536]{1,0:T(8,128)(2,1)S(1)}, bf16[48,1536]{1,0:T(8,128)(2,1)}, u32[]{:S(2)}, u32[]{:S(2)}) collective-permute-start(bf16[48,1536]{1,0:T(8,128)(2,1)S(1)} %copy-done.87), channel_id=1, source_target_pairs={{0,8},{8,0},{1,9},{9,1},{2,10},{10,2},{3,11},{11,3},{4,12},{12,4},... | collective-permute-start | bytes 442376 | tf_op jit(solution)/shard_map/ppermute | solution.py:24
  106.5 29.8 %all-to-all-start.1 = ((bf16[8,128,384]{1,2,0:T(8,128)(2,1)}), bf16[8,128,384]{1,2,0:T(8,128)(2,1)S(1)}, u32[]{:S(2)}, u32[]{:S(2)}) async-start(bf16[8,128,384]{1,2,0:T(8,128)(2,1)} %pad_maximum_fusion.7), calls=%async_computation.1 | async-start | bytes 1572864 | tf_op jit(solution)/shard_map/all_to_all | solution.py:493
  112.4 80.9 %all-gather.8.cloned.1.call-start = ((), (), s32[]{:S(2)}) async-start(), calls=%async_computation.11 | async-start | bytes 2359296 | tf_op jit(solution)/shard_map/all_gather | solution.py:569
  136.8 126.7 %all-gather.10.cloned.1.call-start = ((), (), s32[]{:S(2)}) async-start(), calls=%async_computation.12 | async-start | bytes 5308416 | tf_op jit(solution)/shard_map/all_gather | solution.py:587
  145.8 151.2 %all-gather.12.cloned.1.call-start = ((), (), s32[]{:S(2)}) async-start(), calls=%async_computation.13 | async-start | bytes 7077888 | tf_op jit(solution)/shard_map/all_gather | solution.py:599
  150.3 42.9 %all-to-all-start.2 = ((bf16[8,48,1024]{2,1,0:T(8,128)(2,1)}), bf16[8,48,1024]{2,1,0:T(8,128)(2,1)}, u32[]{:S(2)}, u32[]{:S(2)}) async-start(bf16[8,48,1024]{2,1,0:T(8,128)(2,1)} %pad_maximum_fusion.8), calls=%async_computation.2 | async-start | bytes 1572864 | tf_op jit(solution)/shard_map/all_to_all | solution.py:493
  155.1 37.8 %collective-permute-start.15 = (bf16[1024,384]{1,0:T(8,128)(2,1)S(1)}, bf16[1024,384]{1,0:T(8,128)(2,1)S(1)}, u32[]{:S(2)}, u32[]{:S(2)}) collective-permute-start(bf16[1024,384]{1,0:T(8,128)(2,1)S(1)} %bitcast.391), channel_id=1, source_target_pairs={{0,8},{8,0},{1,9},{9,1},{2,10},{10,2},{3,11},{11,3},{4,12},{12,4},... | collective-permute-start | bytes 2359304 | tf_op jit(solution)/shard_map/ppermute | solution.py:24
  193.2 40.5 %collective-permute-start.16 = (bf16[2,1024,384]{2,1,0:T(8,128)(2,1)S(1)}, bf16[2,1024,384]{2,1,0:T(8,128)(2,1)S(1)}, u32[]{:S(2)}, u32[]{:S(2)}) collective-permute-start(bf16[2,1024,384]{2,1,0:T(8,128)(2,1)S(1)} %maximum_select_fusion.2), channel_id=1, source_target_pairs={{0,16},{16,0},{1,17},{17,1},{2,18},{18,2},{3,19},{19,3},{4,20},{20... | collective-permute-start | bytes 4718600 | tf_op jit(solution)/shard_map/ppermute | solution.py:24
  194.8 36.2 %collective-permute-start.17 = (bf16[384,1024]{1,0:T(8,128)(2,1)}, bf16[384,1024]{1,0:T(8,128)(2,1)S(1)}, u32[]{:S(2)}, u32[]{:S(2)}) collective-permute-start(bf16[384,1024]{1,0:T(8,128)(2,1)} %bitcast.45), channel_id=1, source_target_pairs={{0,8},{8,0},{1,9},{9,1},{2,10},{10,2},{3,11},{11,3},{4,12},{12,4},... | collective-permute-start | bytes 2359304 | tf_op jit(solution)/shard_map/ppermute | solution.py:24
  263.5 25.0 %all-to-all-start.3 = ((bf16[8,192,256]{2,1,0:T(8,128)(2,1)}), bf16[8,192,256]{2,1,0:T(8,128)(2,1)S(1)}, u32[]{:S(2)}, u32[]{:S(2)}) async-start(bf16[8,192,256]{2,1,0:T(8,128)(2,1)} %bitcast.339), calls=%async_computation.3 | async-start | bytes 1572864 | tf_op jit(solution)/shard_map/all_to_all | solution.py:632
  267.2 70.7 %all-gather.14.cloned.1.call-start = ((), (), s32[]{:S(2)}) async-start(), calls=%async_computation.14 | async-start | bytes 7077888 | tf_op jit(solution)/shard_map/all_gather | solution.py:651
  297.0 36.2 %collective-permute-start.23 = (bf16[2,384,1024]{2,1,0:T(8,128)(2,1)}, bf16[2,384,1024]{2,1,0:T(8,128)(2,1)}, u32[]{:S(2)}, u32[]{:S(2)}) collective-permute-start(bf16[2,384,1024]{2,1,0:T(8,128)(2,1)} %maximum_select_fusion.3), channel_id=1, source_target_pairs={{0,16},{16,0},{1,17},{17,1},{2,18},{18,2},{3,19},{19,3},{4,20},{20... | collective-permute-start | bytes 4718600 | tf_op jit(solution)/shard_map/ppermute | solution.py:24
  412.6 28.7 %collective-permute-start.29 = (bf16[1024,1536]{1,0:T(8,128)(2,1)}, bf16[1024,1536]{1,0:T(8,128)(2,1)}, u32[]{:S(2)}, u32[]{:S(2)}) collective-permute-start(bf16[1024,1536]{1,0:T(8,128)(2,1)} %convolution_convert_fusion.7), channel_id=1, source_target_pairs={{0,1},{1,0},{2,3},{3,2},{4,5},{5,4},{6,7},{7,6},{8,9},{9,8},{10,11... | collective-permute-start | bytes 9437192 | tf_op jit(solution)/shard_map/ppermute | solution.py:24
  425.7 31.5 %all-to-all-start.4 = ((bf16[8,192,256]{2,1,0:T(8,128)(2,1)}), bf16[8,192,256]{2,1,0:T(8,128)(2,1)}, u32[]{:S(2)}, u32[]{:S(2)}) async-start(bf16[8,192,256]{2,1,0:T(8,128)(2,1)} %bitcast.379), calls=%async_computation.4 | async-start | bytes 1572864 | tf_op jit(solution)/shard_map/all_to_all | solution.py:728
  430.0 111.4 %reduce-scatter.3.cloned.1.call-start = ((), (), s32[]{:S(2)}) async-start(), calls=%async_computation.15 | async-start | bytes 3932160 | tf_op jit(solution)/shard_map/reduce_scatter | solution.py:702
  460.4 27.0 %collective-permute-start.33 = (bf16[2,128,1536]{2,1,0:T(8,128)(2,1)}, bf16[2,128,1536]{2,1,0:T(8,128)(2,1)}, u32[]{:S(2)}, u32[]{:S(2)}) collective-permute-start(bf16[2,128,1536]{2,1,0:T(8,128)(2,1)} %dynamic-slice_bitcast_fusion.5), channel_id=1, source_target_pairs={{0,2},{2,0},{1,3},{3,1},{4,6},{6,4},{5,7},{7,5},{8,10},{10,8},{9,1... | collective-permute-start | bytes 2359304 | tf_op jit(solution)/shard_map/ppermute | solution.py:24
  461.8 35.3 %collective-permute-start.32 = (bf16[2,128,1536]{2,1,0:T(8,128)(2,1)}, bf16[2,128,1536]{2,1,0:T(8,128)(2,1)}, u32[]{:S(2)}, u32[]{:S(2)}) collective-permute-start(bf16[2,128,1536]{2,1,0:T(8,128)(2,1)} %dynamic-slice_bitcast_fusion.6), channel_id=1, source_target_pairs={{0,4},{4,0},{1,5},{5,1},{2,6},{6,2},{3,7},{7,3},{8,12},{12,8},{9,1... | collective-permute-start | bytes 2359304 | tf_op jit(solution)/shard_map/ppermute | solution.py:24
  498.6 28.8 %collective-permute-start.36 = (bf16[128,1536]{1,0:T(8,128)(2,1)S(1)}, bf16[128,1536]{1,0:T(8,128)(2,1)S(1)}, u32[]{:S(2)}, u32[]{:S(2)}) collective-permute-start(bf16[128,1536]{1,0:T(8,128)(2,1)S(1)} %fusion.41), channel_id=1, source_target_pairs={{0,2},{2,0},{1,3},{3,1},{4,6},{6,4},{5,7},{7,5},{8,10},{10,8},{9,1... | collective-permute-start | bytes 1179656 | tf_op jit(solution)/shard_map/ppermute | solution.py:24
  500.2 27.3 %collective-permute-start.37 = (bf16[128,1536]{1,0:T(8,128)(2,1)S(1)}, bf16[128,1536]{1,0:T(8,128)(2,1)}, u32[]{:S(2)}, u32[]{:S(2)}) collective-permute-start(bf16[128,1536]{1,0:T(8,128)(2,1)S(1)} %fusion.42), channel_id=1, source_target_pairs={{0,4},{4,0},{1,5},{5,1},{2,6},{6,2},{3,7},{7,3},{8,12},{12,8},{9,1... | collective-permute-start | bytes 1179656 | tf_op jit(solution)/shard_map/ppermute | solution.py:24
  503.1 36.2 %collective-permute-start.38 = (bf16[128,1536]{1,0:T(8,128)(2,1)}, bf16[128,1536]{1,0:T(8,128)(2,1)}, u32[]{:S(2)}, u32[]{:S(2)}) collective-permute-start(bf16[128,1536]{1,0:T(8,128)(2,1)} %dynamic-slice_bitcast_fusion.14), channel_id=1, source_target_pairs={{0,8},{8,0},{1,9},{9,1},{2,10},{10,2},{3,11},{11,3},{4,12},{12,4},... | collective-permute-start | bytes 1179656 | tf_op jit(solution)/shard_map/ppermute | solution.py:24
  547.3 35.9 %collective-permute-start.40 = (bf16[2,1024,384]{2,1,0:T(8,128)(2,1)}, bf16[2,1024,384]{2,1,0:T(8,128)(2,1)}, u32[]{:S(2)}, u32[]{:S(2)}) collective-permute-start(bf16[2,1024,384]{2,1,0:T(8,128)(2,1)} %dynamic-slice_bitcast_fusion), channel_id=1, source_target_pairs={{0,16},{16,0},{1,17},{17,1},{2,18},{18,2},{3,19},{19,3},{4,20},{20... | collective-permute-start | bytes 4718600 | tf_op jit(solution)/shard_map/ppermute | solution.py:24
  590.3 130.8 %reduce-scatter.5.cloned.1.call-start = ((), (), s32[]{:S(2)}) async-start(), calls=%async_computation.16 | async-start | bytes 5308416 | tf_op jit(solution)/shard_map/reduce_scatter | solution.py:761
  623.1 36.3 %collective-permute-start.47 = (bf16[1024,384]{1,0:T(8,128)(2,1)}, bf16[1024,384]{1,0:T(8,128)(2,1)}, u32[]{:S(2)}, u32[]{:S(2)}) collective-permute-start(bf16[1024,384]{1,0:T(8,128)(2,1)} %dynamic-slice_bitcast_fusion.4), channel_id=1, source_target_pairs={{0,8},{8,0},{1,9},{9,1},{2,10},{10,2},{3,11},{11,3},{4,12},{12,4},... | collective-permute-start | bytes 2359304 | tf_op jit(solution)/shard_map/ppermute | solution.py:24
  632.6 54.5 %collective-permute-start.46 = (bf16[1024,1536]{1,0:T(8,128)(2,1)}, bf16[1024,1536]{1,0:T(8,128)(2,1)}, u32[]{:S(2)}, u32[]{:S(2)}) collective-permute-start(bf16[1024,1536]{1,0:T(8,128)(2,1)} %convolution_convert_fusion.4), channel_id=1, source_target_pairs={{0,1},{1,0},{2,3},{3,2},{4,5},{5,4},{6,7},{7,6},{8,9},{9,8},{10,11... | collective-permute-start | bytes 9437192 | tf_op jit(solution)/shard_map/ppermute | solution.py:24
  699.0 84.4 %all-to-all-start.7 = ((bf16[8,128,384]{1,2,0:T(8,128)(2,1)}), bf16[8,128,384]{1,2,0:T(8,128)(2,1)}, u32[]{:S(2)}, u32[]{:S(2)}) async-start(bf16[8,128,384]{1,2,0:T(8,128)(2,1)} %copy.236), calls=%async_computation.9 | async-start | bytes 1572864 | tf_op jit(solution)/shard_map/all_to_all | solution.py:689
  732.8 40.4 %collective-permute-start.61 = (bf16[384,576]{1,0:T(8,128)(2,1)}, bf16[384,576]{1,0:T(8,128)(2,1)}, u32[]{:S(2)}, u32[]{:S(2)}) collective-permute-start(bf16[384,576]{1,0:T(8,128)(2,1)} %dynamic-slice_bitcast_fusion.11), channel_id=1, source_target_pairs={{0,8},{8,0},{1,9},{9,1},{2,10},{10,2},{3,11},{11,3},{4,12},{12,4},... | collective-permute-start | bytes 1327112 | tf_op jit(solution)/shard_map/ppermute | solution.py:24
  751.6 46.9 %collective-permute-start.68 = (bf16[48,1536]{1,0:T(8,128)(2,1)}, bf16[48,1536]{1,0:T(8,128)(2,1)}, u32[]{:S(2)}, u32[]{:S(2)}) collective-permute-start(bf16[48,1536]{1,0:T(8,128)(2,1)} %fusion.51), channel_id=1, source_target_pairs={{0,8},{8,0},{1,9},{9,1},{2,10},{10,2},{3,11},{11,3},{4,12},{12,4},... | collective-permute-start | bytes 442376 | tf_op jit(solution)/shard_map/ppermute | solution.py:24
  753.0 43.0 %collective-permute-start.60 = (bf16[16,4096]{1,0:T(8,128)(2,1)}, bf16[16,4096]{1,0:T(8,128)(2,1)}, u32[]{:S(2)}, u32[]{:S(2)}) collective-permute-start(bf16[16,4096]{1,0:T(8,128)(2,1)} %fusion.62), channel_id=1, source_target_pairs={{0,8},{8,0},{1,9},{9,1},{2,10},{10,2},{3,11},{11,3},{4,12},{12,4},... | collective-permute-start | bytes 393224 | tf_op jit(solution)/shard_map/ppermute | solution.py:24
  755.7 44.5 %collective-permute-start.58 = (bf16[128,1536]{1,0:T(8,128)(2,1)}, bf16[128,1536]{1,0:T(8,128)(2,1)}, u32[]{:S(2)}, u32[]{:S(2)}) collective-permute-start(bf16[128,1536]{1,0:T(8,128)(2,1)} %slice.339), channel_id=1, source_target_pairs={{0,8},{8,0},{1,9},{9,1},{2,10},{10,2},{3,11},{11,3},{4,12},{12,4},... | collective-permute-start | bytes 1179656 | tf_op jit(solution)/shard_map/ppermute | solution.py:24
  (179 other events, 1384.5 us)
Sparse Core Ops, SparseCore 0:
  43.3 61.0 all-gather.5
  136.9 20.7 all-gather.7
  159.9 59.0 all-gather.9
  221.1 46.3 all-gather.11
  297.1 37.7 all-gather.13
  457.4 83.1 reduce-scatter.2
  618.5 54.0 reduce-scatter.4
